TPU v7x, 32 devices: a whole 2x2x4 slice. The times are simulated.
32 devices in a mesh: group: 8 (over y, x, core), tp: 4 (over z).
Axes of the slice: x: 2, y: 2, z: 4, core: 2. Of those that a mesh axis runs over, the one named last changes fastest.
Arguments:
- queries: bfloat16 [128, 8192], P('group', 'tp'), may hold values from -100 to 100
- cache_keys: bfloat16 [128, 512, 1024], P('group', None, 'tp'), may hold values from -6 to 6
- cache_values: bfloat16 [128, 512, 1024], P('group', None, 'tp'), may hold values from -6 to 6
- pool_keys: bfloat16 [16, 4096, 1024], P('group', None, 'tp'), may hold values from -6 to 6
- pool_values: bfloat16 [16, 4096, 1024], P('group', None, 'tp'), may hold values from -6 to 6
- row_lengths: int32 [128], P('group'), may hold values from 2 to 49664, as said below
- slot_owner: int32 [16], P('group'), may hold values from -1 to 127, as said below
- slot_fill: int32 [16], P('group'), may hold values from 0 to 4096, as said below
- free_counts: int32 [8], P('group'), may hold values from 0 to 2047
- out_weight: bfloat16 [8192, 8192], P('tp'), may hold values from -0.0625 to 0.0625
Outputs:
- mixed_out: bfloat16 [128, 8192], P('group', 'tp')
- total_free: int32 [1], replicated
Inputs may be any that keep to these rules, and one draw needn't show every extreme that they name: `row_lengths`: A row of length over 512 has the rest of its positions in the slots it owns, so its length is 512 plus the sum of their slot_fill; other rows own no slot. `slot_owner`: each slot is free or holds one block of one row; slots may sit in any group, the row's own too. `slot_fill`: A free slot has fill 0, an owned one at least 2.
All inputs are finite; a program needn't handle non-finite values.
Results may differ from a plain program's by a relative error of at most 0.0066.
Values may be sent and summed in bfloat16 or wider, within the bound.
No kernel may reach another device: no remote copies, remote signals or barrier semaphores. Data moves between devices by JAX's collectives and lax.ppermute only.
A program may use at most 128 MiB of HBM per device.

v0:
```python
import math

import jax
import jax.numpy as jnp
from jax import lax
from jax.experimental import pallas as pl
from jax.experimental.pallas import tpu as pltpu
from jax.sharding import PartitionSpec as P


HEAD_DIM = 128
LANES = 128
far_below = -1e30


VMEM = pl.BlockSpec(memory_space=pltpu.VMEM)
SMEM = pl.BlockSpec(memory_space=pltpu.SMEM)
HBM = pl.BlockSpec(memory_space=pltpu.MemorySpace.HBM)
f32 = jnp.float32
bf16 = jnp.bfloat16


def call(kernel, outs, ins, scratch=(), out_specs=None, flops=0, moved=0, vmem=8 << 20):
    return pl.pallas_call(
        kernel,
        out_shape=outs,
        in_specs=ins,
        out_specs=out_specs if out_specs is not None else jax.tree.map(lambda _: VMEM, outs),
        scratch_shapes=scratch,
        cost_estimate=pl.CostEstimate(flops=flops, bytes_accessed=moved, transcendentals=0),
        compiler_params=pltpu.CompilerParams(vmem_limit_bytes=vmem),
    )


def spread_heads(tile, kv_heads):
    if kv_heads == 1:
        return tile
    heads = tile.shape[0]
    owner = lax.broadcasted_iota(jnp.int32, tile.shape, 0) // (heads // kv_heads)
    return jnp.concatenate(
        [jnp.where(owner == k, tile, jnp.zeros_like(tile)) for k in range(kv_heads)], axis=1
    )


def own_columns(wide, kv_heads):
    if kv_heads == 1:
        return wide
    heads = wide.shape[0]
    owner = lax.broadcasted_iota(jnp.int32, (heads, HEAD_DIM), 0) // (heads // kv_heads)
    picked = wide[:, :HEAD_DIM]
    for k in range(1, kv_heads):
        picked = jnp.where(owner == k, wide[:, k * HEAD_DIM : (k + 1) * HEAD_DIM], picked)
    return picked


def scores_of(query, keys):
    return lax.dot_general(
        query, keys, (((1,), (1,)), ((), ())), preferred_element_type=f32
    ) * (1.0 / math.sqrt(HEAD_DIM))


def copy_in(source, target, sem):
    copy = pltpu.make_async_copy(source, target, sem)
    copy.start()
    return copy


def local_kernel(
    lengths_in, q_in, keys_in, values_in, pool_in,
    mixed_ref, high_ref, total_ref, q_ref, pool_ref,
    lengths, keys, values, q_heads, scores, weights, sems,
    *, rows, heads, kv_heads, parts,
):
    positions = keys.shape[1]
    step = rows // parts
    lengths_copy = copy_in(lengths_in, lengths, sems.at[0])
    q_copy = copy_in(q_in, q_ref, sems.at[1])
    key_copies, value_copies = [], []
    for held, source, target, base in (
        (key_copies, keys_in, keys, 2),
        (value_copies, values_in, values, 2 + parts),
    ):
        for p in range(parts):
            at = pl.ds(p * step, step)
            held.append(copy_in(source.at[at], target.at[at], sems.at[base + p]))
    pool_copy = copy_in(pool_in, pool_ref, sems.at[2 + 2 * parts])
    q_copy.wait()
    wide = q_ref[...].astype(f32)
    for h in range(heads):
        q_heads[pl.ds(h, rows, stride=heads), :] = wide[:, h * HEAD_DIM : (h + 1) * HEAD_DIM]
    lengths_copy.wait()
    place = lax.broadcasted_iota(jnp.int32, (heads, positions), 1)
    for p in range(parts):
        key_copies[p].wait()
        for r in range(p * step, (p + 1) * step):
            at = pl.ds(r * heads, heads)
            query = spread_heads(q_heads[at, :].astype(bf16), kv_heads)
            scores[at, :] = jnp.where(place < lengths[r], scores_of(query, keys[r]), far_below)
    for r in range(rows):
        at = pl.ds(r * heads, heads)
        masked = scores[at, :]
        high = jnp.max(masked, axis=-1, keepdims=True)
        weight = jnp.where(place < lengths[r], jnp.exp(masked - high), 0.0)
        total = jnp.sum(weight, axis=-1, keepdims=True)
        weights[r] = weight.astype(bf16)
        high_ref[at, :] = jnp.broadcast_to(high, (heads, LANES))
        total_ref[at, :] = jnp.broadcast_to(total, (heads, LANES))
    for p in range(parts):
        value_copies[p].wait()
        for r in range(p * step, (p + 1) * step):
            mixed = jnp.dot(weights[r], values[r], preferred_element_type=f32)
            mixed_ref[pl.ds(r * heads, heads), :] = own_columns(mixed, kv_heads)
    pool_copy.wait()


def fetch_kernel(source, _, target, sem):
    copy_in(source, target, sem).wait()


def columns_of(weight, tp_mask, columns):
    start = jnp.bitwise_xor(lax.axis_index("tp"), tp_mask) * columns
    return weight.at[:, pl.ds(pl.multiple_of(start, columns), columns)]


def fetch_columns_kernel(source, _, target, sem, *, tp_mask, columns):
    copy_in(columns_of(source, tp_mask, columns), target, sem).wait()


def slot_kernel(*refs, groups, rows, heads, kv_heads, slots, chunk, tp_mask, columns):
    owners_in, fills_in, free = refs[:3]
    shards = refs[3 : 3 + groups]
    keys, values, weight_in = refs[3 + groups : 6 + groups]
    packed, weight, owners, fills, q_heads, scores, sems = refs[6 + groups :]
    copies = [
        copy_in(owners_in, owners, sems.at[0]),
        copy_in(fills_in, fills, sems.at[1]),
    ]
    weight_copy = copy_in(columns_of(weight_in, tp_mask, columns), weight, sems.at[2])
    for copy in copies:
        copy.wait()
    positions = keys.shape[1]
    me = lax.axis_index("group")
    row_at = lax.broadcasted_iota(jnp.int32, (rows, heads * HEAD_DIM), 0)
    for s in range(slots):
        owner = jnp.maximum(owners[s], 0)
        home = lax.div(owner, rows)
        row = lax.rem(owner, rows)
        for k in range(groups):

            @pl.when(jnp.bitwise_xor(home, me) == k)
            def _(k=k, s=s, row=row):
                block = jnp.where(row_at == row, shards[k][...].astype(f32), 0.0)
                single = jnp.sum(block, axis=0, keepdims=True)
                for h in range(heads):
                    q_heads[s * heads + h : s * heads + h + 1, :] = single[
                        :, h * HEAD_DIM : (h + 1) * HEAD_DIM
                    ]

    place = lax.broadcasted_iota(jnp.int32, (heads, positions), 1)
    lane = lax.broadcasted_iota(jnp.int32, (heads, LANES), 1)
    stats = jnp.where(lane == 3 * slots, free[0].astype(f32), 0.0)
    for s in range(slots):
        at = pl.ds(s * heads, heads)
        query = spread_heads(q_heads[at, :].astype(bf16), kv_heads)
        for c in range(0, positions, chunk):
            scores[at, c : c + chunk] = scores_of(query, keys[s, c : c + chunk, :])
    for s in range(slots):
        at = pl.ds(s * heads, heads)
        visible = place < fills[s]
        masked = jnp.where(visible, scores[at, :], far_below)
        high = jnp.max(masked, axis=-1, keepdims=True)
        weights = jnp.where(visible, jnp.exp(masked - high), 0.0)
        total = jnp.sum(weights, axis=-1, keepdims=True)
        mixed = jnp.dot(weights.astype(bf16), values[s], preferred_element_type=f32)
        packed[at, :] = own_columns(mixed, kv_heads)
        stats = jnp.where(lane == s, high, stats)
        stats = jnp.where(lane == slots + s, total, stats)
        stats = jnp.where(lane == 2 * slots + s, owners[s].astype(f32), stats)
    packed[slots * heads :, :] = stats
    weight_copy.wait()


def project(x, weight, out, chunk):
    for c in range(0, out.shape[1], chunk):
        out[:, c : c + chunk] = jnp.dot(
            x, weight[:, c : c + chunk], preferred_element_type=f32
        ).astype(out.dtype)


def combine_kernel(*refs, groups, rows, heads, slots, ahead, columns, chunk):
    mixed_ref, high_ref, total_ref = refs[:3]
    parts = refs[3 : 3 + groups]
    weight, weight_in, x_ref, out, free_total = refs[3 + groups : 8 + groups]
    rest = refs[8 + groups :]
    copy = None
    if ahead is not None:
        copy = copy_in(columns_of(weight_in, ahead, columns), rest[0], rest[-1])
        rest = rest[1:-1]
    mixed, high, total = rest
    first = lax.axis_index("group") * rows
    free = jnp.zeros((heads, LANES), f32)
    found = []
    for k in range(groups):
        stats = parts[k][slots * heads :, :]
        free = free + stats
        for s in range(slots):
            row = stats[0, 2 * slots + s].astype(jnp.int32) - first
            found.append((k, s, row))
    free_total[0] = free[0, 3 * slots].astype(jnp.int32)
    high[...] = high_ref[...]
    slot_stats = []
    for k, s, row in found:
        mine = (row >= 0) & (row < rows)
        at = pl.ds(pl.multiple_of(jnp.clip(row, 0, rows - 1) * heads, heads), heads)
        stats = parts[k][slots * heads :, :]
        slot_high = jnp.broadcast_to(stats[:, s : s + 1], (heads, LANES))
        slot_total = jnp.broadcast_to(stats[:, slots + s : slots + s + 1], (heads, LANES))
        slot_stats.append((mine, at, slot_high, slot_total))
        high[at, :] = jnp.maximum(high[at, :], jnp.where(mine, slot_high, far_below))
    keep = jnp.exp(high_ref[...] - high[...])
    mixed[...] = keep * mixed_ref[...]
    total[...] = keep * total_ref[...]
    for (k, s, _), (mine, at, slot_high, slot_total) in zip(found, slot_stats):
        add = jnp.where(mine, jnp.exp(jnp.minimum(slot_high - high[at, :], 0.0)), 0.0)
        mixed[at, :] = mixed[at, :] + add * parts[k][s * heads : (s + 1) * heads, :]
        total[at, :] = total[at, :] + add * slot_total
    mixed[...] = mixed[...] / total[...]
    for h in range(heads):
        x_ref[:, h * HEAD_DIM : (h + 1) * HEAD_DIM] = mixed[
            pl.ds(h, rows, stride=heads), :
        ].astype(bf16)
    project(x_ref[...], weight, out, chunk)
    if copy is not None:
        copy.wait()


def project_kernel(x_ref, weight, weight_in, out, *rest, ahead, columns, chunk):
    copy = None
    if ahead is not None:
        copy = copy_in(columns_of(weight_in, ahead, columns), *rest)
    project(x_ref[...], weight, out, chunk)
    if copy is not None:
        copy.wait()


def sum_kernel(*refs):
    total = refs[0][...]
    for part in refs[1:-1]:
        total = total + part[...].astype(f32)
    refs[-1][...] = total.astype(bf16)


def swap(value, axis, mask):
    size = lax.axis_size(axis)
    return lax.ppermute(value, axis, [(i, i ^ mask) for i in range(size)])


def gather_group(value):
    groups = lax.axis_size("group")
    found = [None] * groups
    found[0] = value
    found[1] = swap(value, "group", 1)
    for k in range(2, groups, 2):
        found[k] = swap(value, "group", k)
    for k in range(2, groups, 2):
        found[k + 1] = swap(found[k], "group", 1)
    return found


def step(
    queries,
    cache_keys,
    cache_values,
    pool_keys,
    pool_values,
    row_lengths,
    slot_owner,
    slot_fill,
    free_counts,
    out_weight,
):
    groups, tp = lax.axis_size("group"), lax.axis_size("tp")
    rows, width = queries.shape
    heads = width // HEAD_DIM
    kv_heads = cache_keys.shape[2] // HEAD_DIM
    slots, positions = pool_keys.shape[:2]
    columns = out_weight.shape[1] // tp
    chunk = math.gcd(columns, 512)
    sizes = dict(rows=rows, heads=heads)
    flat = jax.ShapeDtypeStruct((rows * heads, LANES), f32)

    parts = math.gcd(rows, 4)
    shards = gather_group(queries)
    (
        queries, cache_keys, cache_values, pool_keys, pool_values,
        row_lengths, slot_owner, slot_fill, out_weight,
    ) = (
        pltpu.with_memory_space_constraint(argument, pltpu.MemorySpace.HBM)
        for argument in (
            queries, cache_keys, cache_values, pool_keys, pool_values,
            row_lengths, slot_owner, slot_fill, out_weight,
        )
    )
    copies = pltpu.SemaphoreType.DMA

    *local, own_queries, held_keys = call(
        lambda *refs: local_kernel(*refs, kv_heads=kv_heads, parts=parts, **sizes),
        [flat] * 3
        + [
            jax.ShapeDtypeStruct(queries.shape, queries.dtype),
            jax.ShapeDtypeStruct(pool_keys.shape, pool_keys.dtype),
        ],
        [HBM] * 5,
        scratch=[
            pltpu.SMEM(row_lengths.shape, jnp.int32),
            pltpu.VMEM(cache_keys.shape, bf16),
            pltpu.VMEM(cache_values.shape, bf16),
            pltpu.VMEM((rows * heads, HEAD_DIM), f32),
            pltpu.VMEM((rows * heads, cache_keys.shape[1]), f32),
            pltpu.VMEM((rows, heads, cache_keys.shape[1]), bf16),
            copies((3 + 2 * parts,)),
        ],
        moved=2 * (cache_keys.size + cache_values.size + pool_keys.size),
        vmem=12 << 20,
    )(row_lengths, queries, cache_keys, cache_values, pool_keys)
    shards[0] = own_queries

    held_values = call(
        fetch_kernel,
        jax.ShapeDtypeStruct(pool_values.shape, pool_values.dtype),
        [HBM, pl.BlockSpec(memory_space=pl.ANY)],
        scratch=[copies],
        moved=2 * pool_values.size,
        vmem=1 << 20,
    )(pool_values, own_queries)

    order = list(range(tp - 1, 0, -1)) + [0]
    held = jax.ShapeDtypeStruct((width, columns), out_weight.dtype)
    weights = {}
    packed, weights[order[0]] = call(
        lambda *refs: slot_kernel(
            *refs,
            groups=groups,
            kv_heads=kv_heads,
            slots=slots,
            chunk=math.gcd(positions, 512),
            tp_mask=order[0],
            columns=columns,
            **sizes,
        ),
        [jax.ShapeDtypeStruct(((slots + 1) * heads, LANES), f32), held],
        [HBM] * 2 + [SMEM] + [VMEM] * (groups + 2) + [HBM],
        scratch=[
            pltpu.SMEM(slot_owner.shape, jnp.int32),
            pltpu.SMEM(slot_fill.shape, jnp.int32),
            pltpu.VMEM((slots * heads, HEAD_DIM), f32),
            pltpu.VMEM((slots * heads, positions), f32),
            copies((3,)),
        ],
        moved=2 * width * columns,
        vmem=8 << 20,
    )(slot_owner, slot_fill, free_counts, *shards, held_keys, held_values, out_weight)

    far = gather_group(packed)

    if tp > 1:
        weights[order[1]] = call(
            lambda *refs: fetch_columns_kernel(*refs, tp_mask=order[1], columns=columns),
            held,
            [HBM, pl.BlockSpec(memory_space=pl.ANY)],
            scratch=[copies],
            moved=2 * width * columns,
            vmem=1 << 20,
        )(out_weight, packed)

    block = jax.ShapeDtypeStruct((rows, columns), bf16)
    whole = jax.ShapeDtypeStruct((rows, columns), f32)
    moved = 2 * width * columns
    ahead = order[2] if tp > 2 else None
    x, sent, free_total, *more = call(
        lambda *refs: combine_kernel(
            *refs, groups=groups, slots=slots, ahead=ahead, columns=columns, chunk=chunk, **sizes
        ),
        [
            jax.ShapeDtypeStruct((rows, width), bf16),
            block if tp > 1 else whole,
            jax.ShapeDtypeStruct((1,), jnp.int32),
        ]
        + [held] * (ahead is not None),
        [VMEM] * (3 + groups + 1) + [HBM],
        out_specs=[VMEM, VMEM, SMEM] + [VMEM] * (ahead is not None),
        scratch=[pltpu.VMEM((rows * heads, LANES), f32)] * 3 + [copies] * (ahead is not None),
        moved=moved,
    )(*local, *far, weights[order[0]], out_weight)
    out = sent
    received = []
    for i in range(1, tp):
        received.append(swap(sent, "tp", order[i - 1]))
        if more:
            weights[order[i + 1]] = more[0]
        ahead = order[i + 2] if i + 2 < tp else None
        sent, *more = call(
            lambda *refs, ahead=ahead: project_kernel(
                *refs, ahead=ahead, columns=columns, chunk=chunk
            ),
            [block if order[i] else whole] + [held] * (ahead is not None),
            [VMEM] * 2 + [HBM],
            scratch=[copies] * (ahead is not None),
            moved=moved,
            vmem=4 << 20,
        )(x, weights[order[i]], out_weight)
    out = sent
    mixed_out = call(sum_kernel, block, [VMEM] * tp)(out, *received)
    return (mixed_out, free_total)


def solution(mesh):
    in_specs = (
        P("group", "tp"),
        P("group", None, "tp"),
        P("group", None, "tp"),
        P("group", None, "tp"),
        P("group", None, "tp"),
        P("group"),
        P("group"),
        P("group"),
        P("group"),
        P("tp", None),
    )
    out_specs = (P("group", "tp"), P())
    return jax.shard_map(step, mesh=mesh, in_specs=in_specs, out_specs=out_specs, check_vma=False)
```

profile of v0, /device:TPU:0, one launch (start us, length us, event | category | flops | bytes accessed | tf_op | source)
XLA Modules:
  0.0 53.1 jit_solution(6398543002673721077)
XLA Ops:
  0.6 3.0 %collective-permute-start.1 = (bf16[16,2048]{1,0:T(8,128)(2,1)}, bf16[16,2048]{1,0:T(8,128)(2,1)S(1)}, u32[]{:S(2)}, u32[]{:S(2)}) collective-permute-start(bf16[16,2048]{1,0:T(8,128)(2,1)} %refs_1_.2), channel_id=1, source_target_pairs={{0,8},{4,12},{8,0},{12,4},{16,24},{20,28},{24,16},{28,20},{1,9},{5... | collective-permute-start | bytes 196616 | tf_op jit(solution)/shard_map/ppermute | solution.py:255
  3.7 1.5 %collective-permute-start.5 = (bf16[16,2048]{1,0:T(8,128)(2,1)}, bf16[16,2048]{1,0:T(8,128)(2,1)S(1)}, u32[]{:S(2)}, u32[]{:S(2)}) collective-permute-start(bf16[16,2048]{1,0:T(8,128)(2,1)} %refs_1_.2), channel_id=1, source_target_pairs={{0,24},{4,28},{8,16},{12,20},{16,8},{20,12},{24,0},{28,4},{1,25},{... | collective-permute-start | bytes 196616 | tf_op jit(solution)/shard_map/ppermute | solution.py:255
  5.2 1.2 %collective-permute-done.1.refs_5_ = bf16[16,2048]{1,0:T(8,128)(2,1)S(1)} collective-permute-done((bf16[16,2048]{1,0:T(8,128)(2,1)}, bf16[16,2048]{1,0:T(8,128)(2,1)S(1)}, u32[]{:S(2)}, u32[]{:S(2)}) %collective-permute-start.1) | collective-permute-done | bytes 65568 | tf_op jit(solution)/shard_map/ppermute | solution.py:255
  6.4 2.7 %collective-permute-done.5.refs_9_ = bf16[16,2048]{1,0:T(8,128)(2,1)S(1)} collective-permute-done((bf16[16,2048]{1,0:T(8,128)(2,1)}, bf16[16,2048]{1,0:T(8,128)(2,1)S(1)}, u32[]{:S(2)}, u32[]{:S(2)}) %collective-permute-start.5) | collective-permute-done | bytes 65568 | tf_op jit(solution)/shard_map/ppermute | solution.py:255
  9.1 0.8 %collective-permute-done.3.refs_7_ = bf16[16,2048]{1,0:T(8,128)(2,1)S(1)} collective-permute-done((bf16[16,2048]{1,0:T(8,128)(2,1)}, bf16[16,2048]{1,0:T(8,128)(2,1)S(1)}, u32[]{:S(2)}, u32[]{:S(2)}) %collective-permute-start.3) | collective-permute-done | bytes 65568 | tf_op jit(solution)/shard_map/ppermute | solution.py:255
  10.5 4.8 %shard_map.113 = (f32[256,128]{1,0:T(8,128)S(1)}, f32[256,128]{1,0:T(8,128)S(1)}, f32[256,128]{1,0:T(8,128)S(1)}, bf16[16,2048]{1,0:T(8,128)(2,1)S(1)}, bf16[2,4096,256]{2,1,0:T(8,128)(2,1)S(1)}) custom-call(s32[16]{0:T(128)} %refs_0_.3, bf16[16,2048]{1,0:T(8,128)(2,1)} %refs_1_.2, bf16[16,512,256]{2,1,0:T(8,128)(2,1)} %refs_2_.5, ...), custom_call_target="tpu_custom_call" | custom-call | bytes 12582912 | tf_op jit(solution)/shard_map/pallas_call | solution.py:306
  15.4 2.2 %shard_map.114.refs_12_ = bf16[2,4096,256]{2,1,0:T(8,128)(2,1)S(1)} custom-call(bf16[2,4096,256]{2,1,0:T(8,128)(2,1)} %source.1, bf16[16,2048]{1,0:T(8,128)(2,1)S(1)} %get-tuple-element.18._.refs_3_), custom_call_target="tpu_custom_call" | custom-call | bytes 4194304 | tf_op jit(solution)/shard_map/pallas_call | solution.py:328
  17.6 3.4 %shard_map.115 = (f32[48,128]{1,0:T(8,128)S(1)}, bf16[2048,2048]{1,0:T(8,128)(2,1)S(1)}) custom-call(s32[2]{0:T(128)} %refs_0_.4, s32[2]{0:T(128)} %refs_1_.3, s32[1]{0:T(128)S(6)} %copy.12.refs_2_, bf16[16,2048]{1,0:T(8,128)(2,1)S(1)} %get-tuple-element.18._.refs_3_, bf16[16,2048]{1,0:T(8,128)(2,1)S(1)} %collective-permute-done.refs_4_, ...), custom_call_target="tpu_custom_call" | custom-call | bytes 8388608 | tf_op jit(solution)/shard_map/pallas_call | solution.py:340
  21.0 1.5 %collective-permute-start.12 = (f32[48,128]{1,0:T(8,128)S(1)}, f32[48,128]{1,0:T(8,128)S(1)}, u32[]{:S(2)}, u32[]{:S(2)}) collective-permute-start(f32[48,128]{1,0:T(8,128)S(1)} %get-tuple-element.20.refs_3_.refs_1_), channel_id=1, source_target_pairs={{0,24},{4,28},{8,16},{12,20},{16,8},{20,12},{24,0},{28,4},{1,25},{... | collective-permute-start | bytes 73736 | tf_op jit(solution)/shard_map/ppermute | solution.py:255
  22.6 1.2 %collective-permute-start.10 = (f32[48,128]{1,0:T(8,128)S(1)}, f32[48,128]{1,0:T(8,128)S(1)}, u32[]{:S(2)}, u32[]{:S(2)}) collective-permute-start(f32[48,128]{1,0:T(8,128)S(1)} %get-tuple-element.20.refs_3_.refs_1_), channel_id=1, source_target_pairs={{0,16},{4,20},{8,24},{12,28},{16,0},{20,4},{24,8},{28,12},{1,17},{... | collective-permute-start | bytes 73736 | tf_op jit(solution)/shard_map/ppermute | solution.py:255
  23.8 0.8 %collective-permute-start.8 = (f32[48,128]{1,0:T(8,128)S(1)}, f32[48,128]{1,0:T(8,128)S(1)}, u32[]{:S(2)}, u32[]{:S(2)}) collective-permute-start(f32[48,128]{1,0:T(8,128)S(1)} %get-tuple-element.20.refs_3_.refs_1_), channel_id=1, source_target_pairs={{0,8},{4,12},{8,0},{12,4},{16,24},{20,28},{24,16},{28,20},{1,9},{5... | collective-permute-start | bytes 73736 | tf_op jit(solution)/shard_map/ppermute | solution.py:255
  24.6 1.3 %collective-permute-done.12.refs_9_ = f32[48,128]{1,0:T(8,128)S(1)} collective-permute-done((f32[48,128]{1,0:T(8,128)S(1)}, f32[48,128]{1,0:T(8,128)S(1)}, u32[]{:S(2)}, u32[]{:S(2)}) %collective-permute-start.12) | collective-permute-done | bytes 24608 | tf_op jit(solution)/shard_map/ppermute | solution.py:255
  25.9 0.5 collective-permute-done.10.refs_7_
  26.4 1.2 %collective-permute-done.8.refs_5_ = f32[48,128]{1,0:T(8,128)S(1)} collective-permute-done((f32[48,128]{1,0:T(8,128)S(1)}, f32[48,128]{1,0:T(8,128)S(1)}, u32[]{:S(2)}, u32[]{:S(2)}) %collective-permute-start.8) | collective-permute-done | bytes 24608 | tf_op jit(solution)/shard_map/ppermute | solution.py:255
  27.6 3.4 %shard_map.117.refs_1_ = bf16[2048,2048]{1,0:T(8,128)(2,1)S(1)} custom-call(bf16[2048,8192]{1,0:T(8,128)(2,1)} %refs_2_.8, f32[48,128]{1,0:T(8,128)S(1)} %get-tuple-element.20.refs_3_.refs_1_), custom_call_target="tpu_custom_call" | custom-call | bytes 8388608 | tf_op jit(solution)/shard_map/pallas_call | solution.py:367
  31.1 5.3 %shard_map.116 = (bf16[16,2048]{1,0:T(8,128)(2,1)S(1)}, bf16[16,2048]{1,0:T(8,128)(2,1)S(1)}, s32[1]{0:T(128)}, bf16[2048,2048]{1,0:T(8,128)(2,1)S(1)}) custom-call(f32[256,128]{1,0:T(8,128)S(1)} %get-tuple-element.15.refs_0_, f32[256,128]{1,0:T(8,128)S(1)} %get-tuple-element.16.refs_1_, f32[256,128]{1,0:T(8,128)S(1)} %get-tuple-element.17.refs_2_, ...), custom_call_target="tpu_custom_call" | custom-call | bytes 8388608 | tf_op jit(solution)/shard_map/pallas_call | solution.py:380
  36.4 1.2 %shard_map.120 = bf16[16,2048]{1,0:T(8,128)(2,1)S(1)} custom-call(bf16[16,2048]{1,0:T(8,128)(2,1)S(1)} %get-tuple-element.22.refs_0_, bf16[2048,2048]{1,0:T(8,128)(2,1)S(1)} %get-tuple-element.26.refs_1_, bf16[2048,8192]{1,0:T(8,128)(2,1)} %refs_2_.8), custom_call_target="tpu_custom_call" | custom-call | bytes 8388608 | tf_op jit(solution)/shard_map/pallas_call | solution.py:402
  37.5 1.6 %collective-permute-start.16 = (bf16[16,2048]{1,0:T(8,128)(2,1)S(1)}, bf16[16,2048]{1,0:T(8,128)(2,1)S(1)}, u32[]{:S(2)}, u32[]{:S(2)}) collective-permute-start(bf16[16,2048]{1,0:T(8,128)(2,1)S(1)} %shard_map.120), channel_id=1, source_target_pairs={{0,1},{1,0},{2,3},{3,2},{4,5},{5,4},{6,7},{7,6},{8,9},{9,8},{10,11... | collective-permute-start | bytes 196616 | tf_op jit(solution)/shard_map/ppermute | solution.py:255
  39.1 2.5 %collective-permute-start.14 = (bf16[16,2048]{1,0:T(8,128)(2,1)S(1)}, bf16[16,2048]{1,0:T(8,128)(2,1)S(1)}, u32[]{:S(2)}, u32[]{:S(2)}) collective-permute-start(bf16[16,2048]{1,0:T(8,128)(2,1)S(1)} %get-tuple-element.24), channel_id=1, source_target_pairs={{0,3},{1,2},{2,1},{3,0},{4,7},{5,6},{6,5},{7,4},{8,11},{9,10},{10,... | collective-permute-start | bytes 196616 | tf_op jit(solution)/shard_map/ppermute | solution.py:255
  41.6 4.5 %shard_map.118 = (bf16[16,2048]{1,0:T(8,128)(2,1)S(1)}, bf16[2048,2048]{1,0:T(8,128)(2,1)S(1)}) custom-call(bf16[16,2048]{1,0:T(8,128)(2,1)S(1)} %get-tuple-element.22.refs_0_, bf16[2048,2048]{1,0:T(8,128)(2,1)S(1)} %shard_map.117.refs_1_, bf16[2048,8192]{1,0:T(8,128)(2,1)} %refs_2_.8), custom_call_target="tpu_custom_call" | custom-call | bytes 8388608 | tf_op jit(solution)/shard_map/pallas_call | solution.py:402
  46.1 0.2 collective-permute-start.15
  46.3 1.2 %shard_map.119.refs_0_ = f32[16,2048]{1,0:T(8,128)S(1)} custom-call(bf16[16,2048]{1,0:T(8,128)(2,1)S(1)} %get-tuple-element.22.refs_0_, bf16[2048,2048]{1,0:T(8,128)(2,1)S(1)} %get-tuple-element.23.refs_1_, bf16[2048,8192]{1,0:T(8,128)(2,1)} %refs_2_.8), custom_call_target="tpu_custom_call" | custom-call | bytes 8388608 | tf_op jit(solution)/shard_map/pallas_call | solution.py:402
  47.5 4.9 %collective-permute-done.15.refs_2_ = bf16[16,2048]{1,0:T(8,128)(2,1)S(1)} collective-permute-done((bf16[16,2048]{1,0:T(8,128)(2,1)S(1)}, bf16[16,2048]{1,0:T(8,128)(2,1)S(1)}, u32[]{:S(2)}, u32[]{:S(2)}) %collective-permute-start.15) | collective-permute-done | bytes 65568 | tf_op jit(solution)/shard_map/ppermute | solution.py:255
  52.4 0.7 %shard_map.121 = bf16[16,2048]{1,0:T(8,128)(2,1)} custom-call(f32[16,2048]{1,0:T(8,128)S(1)} %shard_map.119.refs_0_, bf16[16,2048]{1,0:T(8,128)(2,1)S(1)} %collective-permute-done.14.refs_1_, bf16[16,2048]{1,0:T(8,128)(2,1)S(1)} %collective-permute-done.15.refs_2_, bf16[16,2048]{1,0:T(8,128)(2,1)S(1)} %collective-permute-done.16.refs_3_), custom_call_target="tpu_custom_call" | custom-call | tf_op jit(solution)/shard_map/pallas_call | solution.py:413
  (19 shorter events, 0.1 us)
Async XLA Ops:
  0.6 5.8 %collective-permute-start.1 = (bf16[16,2048]{1,0:T(8,128)(2,1)}, bf16[16,2048]{1,0:T(8,128)(2,1)S(1)}, u32[]{:S(2)}, u32[]{:S(2)}) collective-permute-start(bf16[16,2048]{1,0:T(8,128)(2,1)} %refs_1_.2), channel_id=1, source_target_pairs={{0,8},{4,12},{8,0},{12,4},{16,24},{20,28},{24,16},{28,20},{1,9},{5... | collective-permute-start | bytes 196616 | tf_op jit(solution)/shard_map/ppermute | solution.py:255
  3.7 5.4 %collective-permute-start.5 = (bf16[16,2048]{1,0:T(8,128)(2,1)}, bf16[16,2048]{1,0:T(8,128)(2,1)S(1)}, u32[]{:S(2)}, u32[]{:S(2)}) collective-permute-start(bf16[16,2048]{1,0:T(8,128)(2,1)} %refs_1_.2), channel_id=1, source_target_pairs={{0,24},{4,28},{8,16},{12,20},{16,8},{20,12},{24,0},{28,4},{1,25},{... | collective-permute-start | bytes 196616 | tf_op jit(solution)/shard_map/ppermute | solution.py:255
  5.2 4.7 %collective-permute-start.3 = (bf16[16,2048]{1,0:T(8,128)(2,1)}, bf16[16,2048]{1,0:T(8,128)(2,1)S(1)}, u32[]{:S(2)}, u32[]{:S(2)}) collective-permute-start(bf16[16,2048]{1,0:T(8,128)(2,1)} %refs_1_.2), channel_id=1, source_target_pairs={{0,16},{4,20},{8,24},{12,28},{16,0},{20,4},{24,8},{28,12},{1,17},{... | collective-permute-start | bytes 196616 | tf_op jit(solution)/shard_map/ppermute | solution.py:255
  5.2 12.4 %collective-permute-start = (bf16[16,2048]{1,0:T(8,128)(2,1)}, bf16[16,2048]{1,0:T(8,128)(2,1)S(1)}, u32[]{:S(2)}, u32[]{:S(2)}) collective-permute-start(bf16[16,2048]{1,0:T(8,128)(2,1)} %refs_1_.2), channel_id=1, source_target_pairs={{0,4},{4,0},{8,12},{12,8},{16,20},{20,16},{24,28},{28,24},{1,5},{5... | collective-permute-start | bytes 196616 | tf_op jit(solution)/shard_map/ppermute | solution.py:255
  6.4 11.2 %collective-permute-start.2 = (bf16[16,2048]{1,0:T(8,128)(2,1)S(1)}, bf16[16,2048]{1,0:T(8,128)(2,1)S(1)}, u32[]{:S(2)}, u32[]{:S(2)}) collective-permute-start(bf16[16,2048]{1,0:T(8,128)(2,1)S(1)} %collective-permute-done.1.refs_5_), channel_id=1, source_target_pairs={{0,4},{4,0},{8,12},{12,8},{16,20},{20,16},{24,28},{28,24},{1,5},{5... | collective-permute-start | bytes 196616 | tf_op jit(solution)/shard_map/ppermute | solution.py:255
  9.1 8.5 %collective-permute-start.6 = (bf16[16,2048]{1,0:T(8,128)(2,1)S(1)}, bf16[16,2048]{1,0:T(8,128)(2,1)S(1)}, u32[]{:S(2)}, u32[]{:S(2)}) collective-permute-start(bf16[16,2048]{1,0:T(8,128)(2,1)S(1)} %collective-permute-done.5.refs_9_), channel_id=1, source_target_pairs={{0,4},{4,0},{8,12},{12,8},{16,20},{20,16},{24,28},{28,24},{1,5},{5... | collective-permute-start | bytes 196616 | tf_op jit(solution)/shard_map/ppermute | solution.py:255
  9.9 7.7 %collective-permute-start.4 = (bf16[16,2048]{1,0:T(8,128)(2,1)S(1)}, bf16[16,2048]{1,0:T(8,128)(2,1)S(1)}, u32[]{:S(2)}, u32[]{:S(2)}) collective-permute-start(bf16[16,2048]{1,0:T(8,128)(2,1)S(1)} %collective-permute-done.3.refs_7_), channel_id=1, source_target_pairs={{0,4},{4,0},{8,12},{12,8},{16,20},{20,16},{24,28},{28,24},{1,5},{5... | collective-permute-start | bytes 196616 | tf_op jit(solution)/shard_map/ppermute | solution.py:255
  21.0 4.9 %collective-permute-start.12 = (f32[48,128]{1,0:T(8,128)S(1)}, f32[48,128]{1,0:T(8,128)S(1)}, u32[]{:S(2)}, u32[]{:S(2)}) collective-permute-start(f32[48,128]{1,0:T(8,128)S(1)} %get-tuple-element.20.refs_3_.refs_1_), channel_id=1, source_target_pairs={{0,24},{4,28},{8,16},{12,20},{16,8},{20,12},{24,0},{28,4},{1,25},{... | collective-permute-start | bytes 73736 | tf_op jit(solution)/shard_map/ppermute | solution.py:255
  22.6 3.8 %collective-permute-start.10 = (f32[48,128]{1,0:T(8,128)S(1)}, f32[48,128]{1,0:T(8,128)S(1)}, u32[]{:S(2)}, u32[]{:S(2)}) collective-permute-start(f32[48,128]{1,0:T(8,128)S(1)} %get-tuple-element.20.refs_3_.refs_1_), channel_id=1, source_target_pairs={{0,16},{4,20},{8,24},{12,28},{16,0},{20,4},{24,8},{28,12},{1,17},{... | collective-permute-start | bytes 73736 | tf_op jit(solution)/shard_map/ppermute | solution.py:255
  23.8 3.8 %collective-permute-start.8 = (f32[48,128]{1,0:T(8,128)S(1)}, f32[48,128]{1,0:T(8,128)S(1)}, u32[]{:S(2)}, u32[]{:S(2)}) collective-permute-start(f32[48,128]{1,0:T(8,128)S(1)} %get-tuple-element.20.refs_3_.refs_1_), channel_id=1, source_target_pairs={{0,8},{4,12},{8,0},{12,4},{16,24},{20,28},{24,16},{28,20},{1,9},{5... | collective-permute-start | bytes 73736 | tf_op jit(solution)/shard_map/ppermute | solution.py:255
  24.6 6.4 %collective-permute-start.7 = (f32[48,128]{1,0:T(8,128)S(1)}, f32[48,128]{1,0:T(8,128)S(1)}, u32[]{:S(2)}, u32[]{:S(2)}) collective-permute-start(f32[48,128]{1,0:T(8,128)S(1)} %get-tuple-element.20.refs_3_.refs_1_), channel_id=1, source_target_pairs={{0,4},{4,0},{8,12},{12,8},{16,20},{20,16},{24,28},{28,24},{1,5},{5... | collective-permute-start | bytes 73736 | tf_op jit(solution)/shard_map/ppermute | solution.py:255
  25.9 5.1 %collective-permute-start.13 = (f32[48,128]{1,0:T(8,128)S(1)}, f32[48,128]{1,0:T(8,128)S(1)}, u32[]{:S(2)}, u32[]{:S(2)}) collective-permute-start(f32[48,128]{1,0:T(8,128)S(1)} %collective-permute-done.12.refs_9_), channel_id=1, source_target_pairs={{0,4},{4,0},{8,12},{12,8},{16,20},{20,16},{24,28},{28,24},{1,5},{5... | collective-permute-start | bytes 73736 | tf_op jit(solution)/shard_map/ppermute | solution.py:255
  26.4 4.7 %collective-permute-start.11 = (f32[48,128]{1,0:T(8,128)S(1)}, f32[48,128]{1,0:T(8,128)S(1)}, u32[]{:S(2)}, u32[]{:S(2)}) collective-permute-start(f32[48,128]{1,0:T(8,128)S(1)} %collective-permute-done.10.refs_7_), channel_id=1, source_target_pairs={{0,4},{4,0},{8,12},{12,8},{16,20},{20,16},{24,28},{28,24},{1,5},{5... | collective-permute-start | bytes 73736 | tf_op jit(solution)/shard_map/ppermute | solution.py:255
  27.6 3.4 %collective-permute-start.9 = (f32[48,128]{1,0:T(8,128)S(1)}, f32[48,128]{1,0:T(8,128)S(1)}, u32[]{:S(2)}, u32[]{:S(2)}) collective-permute-start(f32[48,128]{1,0:T(8,128)S(1)} %collective-permute-done.8.refs_5_), channel_id=1, source_target_pairs={{0,4},{4,0},{8,12},{12,8},{16,20},{20,16},{24,28},{28,24},{1,5},{5... | collective-permute-start | bytes 73736 | tf_op jit(solution)/shard_map/ppermute | solution.py:255
  37.5 9.9 %collective-permute-start.16 = (bf16[16,2048]{1,0:T(8,128)(2,1)S(1)}, bf16[16,2048]{1,0:T(8,128)(2,1)S(1)}, u32[]{:S(2)}, u32[]{:S(2)}) collective-permute-start(bf16[16,2048]{1,0:T(8,128)(2,1)S(1)} %shard_map.120), channel_id=1, source_target_pairs={{0,1},{1,0},{2,3},{3,2},{4,5},{5,4},{6,7},{7,6},{8,9},{9,8},{10,11... | collective-permute-start | bytes 196616 | tf_op jit(solution)/shard_map/ppermute | solution.py:255
  39.1 8.3 %collective-permute-start.14 = (bf16[16,2048]{1,0:T(8,128)(2,1)S(1)}, bf16[16,2048]{1,0:T(8,128)(2,1)S(1)}, u32[]{:S(2)}, u32[]{:S(2)}) collective-permute-start(bf16[16,2048]{1,0:T(8,128)(2,1)S(1)} %get-tuple-element.24), channel_id=1, source_target_pairs={{0,3},{1,2},{2,1},{3,0},{4,7},{5,6},{6,5},{7,4},{8,11},{9,10},{10,... | collective-permute-start | bytes 196616 | tf_op jit(solution)/shard_map/ppermute | solution.py:255
  46.1 6.3 %collective-permute-start.15 = (bf16[16,2048]{1,0:T(8,128)(2,1)S(1)}, bf16[16,2048]{1,0:T(8,128)(2,1)S(1)}, u32[]{:S(2)}, u32[]{:S(2)}) collective-permute-start(bf16[16,2048]{1,0:T(8,128)(2,1)S(1)} %get-tuple-element.25), channel_id=1, source_target_pairs={{0,2},{1,3},{2,0},{3,1},{4,6},{5,7},{6,4},{7,5},{8,10},{9,11},{10,... | collective-permute-start | bytes 196616 | tf_op jit(solution)/shard_map/ppermute | solution.py:255
where the time goes:
time: 53.4 us; the launch traced here: 53.1 us
  Pallas kernels  26.6 us (50%)
  waiting for transfers between devices  12.6 us (24%)
  starting transfers between devices  12.4 us (23%)
  between operations  1.41 us (3%)
    ppermute x17, waiting for transfers between devices, swap(): return lax.ppermute(value, axis, [(i, i ^ mask) for i in range(size)])  12.6 us
    ppermute x17, starting transfers between devices, swap(): return lax.ppermute(value, axis, [(i, i ^ mask) for i in range(size)])  12.4 us
    pallas_call x3, Pallas kernels, step(): call(lambda *refs, ahead=ahead: project_kernel(*refs, ahead=ahead, column...  6.84 us
    pallas_call x1, Pallas kernels, step(): call(lambda *refs: combine_kernel(*refs, groups=groups, slots=slots, ahea...  5.27 us
    pallas_call x1, Pallas kernels, step(): call(lambda *refs: local_kernel(*refs, kv_heads=kv_heads, parts=parts, **...  4.81 us
    pallas_call x1, Pallas kernels, step(): call(lambda *refs: slot_kernel(*refs, groups=groups, kv_heads=kv_heads, s...  3.43 us
    pallas_call x1, Pallas kernels, step(): call(lambda *refs: fetch_columns_kernel(*refs, tp_mask=order[1], columns=...  3.39 us
    pallas_call x1, Pallas kernels, step(): call(fetch_kernel, jax.ShapeDtypeStruct(pool_values.shape, pool_values.dt...  2.2 us
  transfers between devices with their start and end apart: 17, of which 7 were waited for; matrix products, arithmetic and copies ran while one was open for 0% of the time, Pallas kernels for 30%

commit v1 on v0

--- a/solution.py
+++ b/solution.py
@@ -67,7 +67,7 @@
 
 def local_kernel(
     lengths_in, q_in, keys_in, values_in, pool_in,
-    mixed_ref, high_ref, total_ref, q_ref, pool_ref,
+    packed, q_ref, pool_ref,
     lengths, keys, values, q_heads, scores, weights, sems,
     *, rows, heads, kv_heads, parts,
 ):
@@ -90,6 +90,7 @@
         q_heads[pl.ds(h, rows, stride=heads), :] = wide[:, h * HEAD_DIM : (h + 1) * HEAD_DIM]
     lengths_copy.wait()
     place = lax.broadcasted_iota(jnp.int32, (heads, positions), 1)
+    lane = lax.broadcasted_iota(jnp.int32, (heads, LANES), 1)
     for p in range(parts):
         key_copies[p].wait()
         for r in range(p * step, (p + 1) * step):
@@ -103,13 +104,12 @@
         weight = jnp.where(place < lengths[r], jnp.exp(masked - high), 0.0)
         total = jnp.sum(weight, axis=-1, keepdims=True)
         weights[r] = weight.astype(bf16)
-        high_ref[at, :] = jnp.broadcast_to(high, (heads, LANES))
-        total_ref[at, :] = jnp.broadcast_to(total, (heads, LANES))
+        packed[pl.ds((rows + r) * heads, heads), :] = jnp.where(lane == 0, high, total)
     for p in range(parts):
         value_copies[p].wait()
         for r in range(p * step, (p + 1) * step):
             mixed = jnp.dot(weights[r], values[r], preferred_element_type=f32)
-            mixed_ref[pl.ds(r * heads, heads), :] = own_columns(mixed, kv_heads)
+            packed[pl.ds(r * heads, heads), :] = own_columns(mixed, kv_heads)
     pool_copy.wait()
 
 
@@ -117,16 +117,22 @@
     copy_in(source, target, sem).wait()
 
 
-def columns_of(weight, tp_mask, columns):
-    start = jnp.bitwise_xor(lax.axis_index("tp"), tp_mask) * columns
+def step_mask(group, step, tp):
+    return (tp // 2) * (group % 2) + step
+
+
+def columns_of(weight, step, columns):
+    tp = lax.axis_size("tp")
+    mask = step_mask(lax.axis_index("group"), step, tp)
+    start = jnp.bitwise_xor(lax.axis_index("tp"), mask) * columns
     return weight.at[:, pl.ds(pl.multiple_of(start, columns), columns)]
 
 
-def fetch_columns_kernel(source, _, target, sem, *, tp_mask, columns):
-    copy_in(columns_of(source, tp_mask, columns), target, sem).wait()
-
-
-def slot_kernel(*refs, groups, rows, heads, kv_heads, slots, chunk, tp_mask, columns):
+def fetch_columns_kernel(source, _, target, sem, *, step, columns):
+    copy_in(columns_of(source, step, columns), target, sem).wait()
+
+
+def slot_kernel(*refs, groups, rows, heads, kv_heads, slots, chunk, step, columns):
     owners_in, fills_in, free = refs[:3]
     shards = refs[3 : 3 + groups]
     keys, values, weight_in = refs[3 + groups : 6 + groups]
@@ -135,7 +141,7 @@
         copy_in(owners_in, owners, sems.at[0]),
         copy_in(fills_in, fills, sems.at[1]),
     ]
-    weight_copy = copy_in(columns_of(weight_in, tp_mask, columns), weight, sems.at[2])
+    weight_copy = copy_in(columns_of(weight_in, step, columns), weight, sems.at[2])
     for copy in copies:
         copy.wait()
     positions = keys.shape[1]
@@ -180,46 +186,61 @@
     weight_copy.wait()
 
 
-def project(x, weight, out, chunk):
-    for c in range(0, out.shape[1], chunk):
-        out[:, c : c + chunk] = jnp.dot(
-            x, weight[:, c : c + chunk], preferred_element_type=f32
-        ).astype(out.dtype)
-
-
-def combine_kernel(*refs, groups, rows, heads, slots, ahead, columns, chunk):
-    mixed_ref, high_ref, total_ref = refs[:3]
-    parts = refs[3 : 3 + groups]
-    weight, weight_in, x_ref, out, free_total = refs[3 + groups : 8 + groups]
-    rest = refs[8 + groups :]
+def project(x, weight, same, other, chunk, own=None):
+    rows = x.shape[0] // 2
+    for c in range(0, same.shape[1], chunk):
+        product = jnp.dot(x, weight[:, c : c + chunk], preferred_element_type=f32)
+        same[:, c : c + chunk] = product[:rows].astype(same.dtype)
+        other[:, c : c + chunk] = product[rows:].astype(other.dtype)
+        if own is not None:
+            own[:, c : c + chunk] = product[:rows]
+
+
+def combine_kernel(*refs, groups, rows, heads, slots, ahead, last, columns, chunk):
+    local = refs[:2]
+    parts = refs[2 : 2 + groups]
+    weight, weight_in, x_ref, free_total, same, other = refs[2 + groups : 8 + groups]
+    rest = list(refs[8 + groups :])
+    own = rest.pop(0) if last else None
     copy = None
     if ahead is not None:
-        copy = copy_in(columns_of(weight_in, ahead, columns), rest[0], rest[-1])
-        rest = rest[1:-1]
+        copy = copy_in(columns_of(weight_in, ahead, columns), rest.pop(0), rest.pop())
     mixed, high, total = rest
-    first = lax.axis_index("group") * rows
+    flat = rows * heads
+    me = lax.axis_index("group")
+    first, second = me * rows, jnp.bitwise_xor(me, 1) * rows
     free = jnp.zeros((heads, LANES), f32)
     found = []
     for k in range(groups):
         stats = parts[k][slots * heads :, :]
         free = free + stats
         for s in range(slots):
-            row = stats[0, 2 * slots + s].astype(jnp.int32) - first
-            found.append((k, s, row))
+            owner = stats[0, 2 * slots + s].astype(jnp.int32)
+            found.append((k, s, owner))
     free_total[0] = free[0, 3 * slots].astype(jnp.int32)
-    high[...] = high_ref[...]
+    for i in range(2):
+        stats = local[i][flat:, :]
+        high[i * flat : (i + 1) * flat, :] = jnp.broadcast_to(stats[:, 0:1], (flat, LANES))
     slot_stats = []
-    for k, s, row in found:
-        mine = (row >= 0) & (row < rows)
-        at = pl.ds(pl.multiple_of(jnp.clip(row, 0, rows - 1) * heads, heads), heads)
+    for k, s, owner in found:
+        in_first = (owner >= first) & (owner < first + rows)
+        in_second = (owner >= second) & (owner < second + rows)
+        row = jnp.where(
+            in_first, owner - first, jnp.where(in_second, owner - second + rows, 0)
+        )
+        mine = in_first | in_second
+        at = pl.ds(pl.multiple_of(row * heads, heads), heads)
         stats = parts[k][slots * heads :, :]
         slot_high = jnp.broadcast_to(stats[:, s : s + 1], (heads, LANES))
         slot_total = jnp.broadcast_to(stats[:, slots + s : slots + s + 1], (heads, LANES))
         slot_stats.append((mine, at, slot_high, slot_total))
         high[at, :] = jnp.maximum(high[at, :], jnp.where(mine, slot_high, far_below))
-    keep = jnp.exp(high_ref[...] - high[...])
-    mixed[...] = keep * mixed_ref[...]
-    total[...] = keep * total_ref[...]
+    for i in range(2):
+        at = slice(i * flat, (i + 1) * flat)
+        stats = local[i][flat:, :]
+        keep = jnp.exp(jnp.broadcast_to(stats[:, 0:1], (flat, LANES)) - high[at, :])
+        mixed[at, :] = keep * local[i][:flat, :]
+        total[at, :] = keep * jnp.broadcast_to(stats[:, 1:2], (flat, LANES))
     for (k, s, _), (mine, at, slot_high, slot_total) in zip(found, slot_stats):
         add = jnp.where(mine, jnp.exp(jnp.minimum(slot_high - high[at, :], 0.0)), 0.0)
         mixed[at, :] = mixed[at, :] + add * parts[k][s * heads : (s + 1) * heads, :]
@@ -227,27 +248,40 @@
     mixed[...] = mixed[...] / total[...]
     for h in range(heads):
         x_ref[:, h * HEAD_DIM : (h + 1) * HEAD_DIM] = mixed[
-            pl.ds(h, rows, stride=heads), :
+            pl.ds(h, 2 * rows, stride=heads), :
         ].astype(bf16)
-    project(x_ref[...], weight, out, chunk)
+    project(x_ref[...], weight, same, other, chunk, own)
     if copy is not None:
         copy.wait()
 
 
-def project_kernel(x_ref, weight, weight_in, out, *rest, ahead, columns, chunk):
+def project_kernel(x_ref, weight, weight_in, same, other, *rest, ahead, last, columns, chunk):
+    rest = list(rest)
+    own = rest.pop(0) if last else None
     copy = None
     if ahead is not None:
         copy = copy_in(columns_of(weight_in, ahead, columns), *rest)
-    project(x_ref[...], weight, out, chunk)
+    project(x_ref[...], weight, same, other, chunk, own)
     if copy is not None:
         copy.wait()
 
 
-def sum_kernel(*refs):
-    total = refs[0][...]
-    for part in refs[1:-1]:
+def sum_kernel(own, final, *refs):
+    total = jnp.where(lax.axis_index("group") % 2 == 0, own[...], final[...].astype(f32))
+    for part in refs[:-1]:
         total = total + part[...].astype(f32)
     refs[-1][...] = total.astype(bf16)
+
+
+def send_block(value, step, cross):
+    groups, tp = lax.axis_size("group"), lax.axis_size("tp")
+    pairs = [
+        (g * tp + z, (g ^ cross) * tp + (z ^ step_mask(g, step, tp)))
+        for g in range(groups)
+        for z in range(tp)
+        if cross or step_mask(g, step, tp)
+    ]
+    return lax.ppermute(value, ("group", "tp"), pairs)
 
 
 def swap(value, axis, mask):
@@ -287,7 +321,6 @@
     columns = out_weight.shape[1] // tp
     chunk = math.gcd(columns, 512)
     sizes = dict(rows=rows, heads=heads)
-    flat = jax.ShapeDtypeStruct((rows * heads, LANES), f32)
 
     parts = math.gcd(rows, 4)
     shards = gather_group(queries)
@@ -303,10 +336,10 @@
     )
     copies = pltpu.SemaphoreType.DMA
 
-    *local, own_queries, held_keys = call(
+    local, own_queries, held_keys = call(
         lambda *refs: local_kernel(*refs, kv_heads=kv_heads, parts=parts, **sizes),
-        [flat] * 3
-        + [
+        [
+            jax.ShapeDtypeStruct((2 * rows * heads, LANES), f32),
             jax.ShapeDtypeStruct(queries.shape, queries.dtype),
             jax.ShapeDtypeStruct(pool_keys.shape, pool_keys.dtype),
         ],
@@ -324,6 +357,7 @@
         vmem=12 << 20,
     )(row_lengths, queries, cache_keys, cache_values, pool_keys)
     shards[0] = own_queries
+    pair_local = swap(local, "group", 1)
 
     held_values = call(
         fetch_kernel,
@@ -334,7 +368,7 @@
         vmem=1 << 20,
     )(pool_values, own_queries)
 
-    order = list(range(tp - 1, 0, -1)) + [0]
+    order = list(range(tp // 2 - 1, -1, -1))
     held = jax.ShapeDtypeStruct((width, columns), out_weight.dtype)
     weights = {}
     packed, weights[order[0]] = call(
@@ -344,7 +378,7 @@
             kv_heads=kv_heads,
             slots=slots,
             chunk=math.gcd(positions, 512),
-            tp_mask=order[0],
+            step=order[0],
             columns=columns,
             **sizes,
         ),
@@ -363,9 +397,9 @@
 
     far = gather_group(packed)
 
-    if tp > 1:
+    if len(order) > 1:
         weights[order[1]] = call(
-            lambda *refs: fetch_columns_kernel(*refs, tp_mask=order[1], columns=columns),
+            lambda *refs: fetch_columns_kernel(*refs, step=order[1], columns=columns),
             held,
             [HBM, pl.BlockSpec(memory_space=pl.ANY)],
             scratch=[copies],
@@ -376,41 +410,47 @@
     block = jax.ShapeDtypeStruct((rows, columns), bf16)
     whole = jax.ShapeDtypeStruct((rows, columns), f32)
     moved = 2 * width * columns
-    ahead = order[2] if tp > 2 else None
-    x, sent, free_total, *more = call(
-        lambda *refs: combine_kernel(
-            *refs, groups=groups, slots=slots, ahead=ahead, columns=columns, chunk=chunk, **sizes
-        ),
-        [
-            jax.ShapeDtypeStruct((rows, width), bf16),
-            block if tp > 1 else whole,
-            jax.ShapeDtypeStruct((1,), jnp.int32),
-        ]
-        + [held] * (ahead is not None),
-        [VMEM] * (3 + groups + 1) + [HBM],
-        out_specs=[VMEM, VMEM, SMEM] + [VMEM] * (ahead is not None),
-        scratch=[pltpu.VMEM((rows * heads, LANES), f32)] * 3 + [copies] * (ahead is not None),
-        moved=moved,
-    )(*local, *far, weights[order[0]], out_weight)
-    out = sent
     received = []
-    for i in range(1, tp):
-        received.append(swap(sent, "tp", order[i - 1]))
-        if more:
-            weights[order[i + 1]] = more[0]
-        ahead = order[i + 2] if i + 2 < tp else None
-        sent, *more = call(
-            lambda *refs, ahead=ahead: project_kernel(
-                *refs, ahead=ahead, columns=columns, chunk=chunk
-            ),
-            [block if order[i] else whole] + [held] * (ahead is not None),
-            [VMEM] * 2 + [HBM],
-            scratch=[copies] * (ahead is not None),
-            moved=moved,
-            vmem=4 << 20,
-        )(x, weights[order[i]], out_weight)
-    out = sent
-    mixed_out = call(sum_kernel, block, [VMEM] * tp)(out, *received)
+    for i, step in enumerate(order):
+        last = step == 0
+        ahead = order[i + 2] if i + 2 < len(order) else None
+        outs = [block] * 2 + [whole] * last + [held] * (ahead is not None)
+        settings = dict(ahead=ahead, last=last, columns=columns, chunk=chunk)
+        if i == 0:
+            x, free_total, same, other, *more = call(
+                lambda *refs: combine_kernel(
+                    *refs, groups=groups, slots=slots, **settings, **sizes
+                ),
+                [
+                    jax.ShapeDtypeStruct((2 * rows, width), bf16),
+                    jax.ShapeDtypeStruct((1,), jnp.int32),
+                ]
+                + outs,
+                [VMEM] * (2 + groups + 1) + [HBM],
+                out_specs=[VMEM, SMEM] + [VMEM] * len(outs),
+                scratch=[pltpu.VMEM((2 * rows * heads, LANES), f32)] * 3
+                + [copies] * (ahead is not None),
+                moved=moved,
+            )(local, pair_local, *far, weights[step], out_weight)
+        else:
+            same, other, *more = call(
+                lambda *refs, settings=settings: project_kernel(*refs, **settings),
+                outs,
+                [VMEM] * 2 + [HBM],
+                scratch=[copies] * (ahead is not None),
+                moved=moved,
+                vmem=4 << 20,
+            )(x, weights[step], out_weight)
+        if last:
+            own = more.pop(0)
+        if ahead is not None:
+            weights[ahead] = more.pop(0)
+        received.append(send_block(same, step, 0))
+        received.append(send_block(other, step, 1))
+    final = received.pop(-2)
+    mixed_out = call(sum_kernel, block, [VMEM] * (2 + len(received)))(
+        own, final, *received
+    )
     return (mixed_out, free_total)
 
 

time: 53.4 us -> 47.8 us (0.90)
  Pallas kernels: 26.6 us -> 18.5 us
  starting transfers between devices: 12.4 us -> 14.3 us
  waiting for transfers between devices: 12.6 us -> 13.3 us
    pallas_call x6 -> x4, Pallas kernels: 16.2 us -> 8.05 us  [the longest x1 3.39 us: step(): call(lambda *refs: fetch_columns_kernel(*refs, step=order[1], columns=col...]
    ppermute x0 -> x4, starting transfers between devices: none -> 5.85 us  [send_block(): return lax.ppermute(value, ('group', 'tp'), pairs)]
    ppermute x0 -> x4, waiting for transfers between devices: none -> 5.59 us  [send_block(): return lax.ppermute(value, ('group', 'tp'), pairs)]
    ppermute x17 -> x15, waiting for transfers between devices: 12.6 us -> 7.76 us  [swap(): return lax.ppermute(value, axis, [(i, i ^ mask) for i in range(size)])]
    ppermute x17 -> x15, starting transfers between devices: 12.4 us -> 8.41 us  [swap(): return lax.ppermute(value, axis, [(i, i ^ mask) for i in range(size)])]
  transfers between devices with their start and end apart: 17 -> 19, of which waited for: 7 -> 9; matrix products, arithmetic and copies ran while one was open for 0% -> 0% of each run, Pallas kernels for 30% -> 19%
where the time goes in v1:
time: 47.8 us; the launch traced here: 47.5 us
  Pallas kernels  18.5 us (39%)
  starting transfers between devices  14.3 us (30%)
  waiting for transfers between devices  13.3 us (28%)
  between operations  1.43 us (3%)
    ppermute x15, starting transfers between devices, swap(): return lax.ppermute(value, axis, [(i, i ^ mask) for i in range(size)])  8.41 us
    ppermute x15, waiting for transfers between devices, swap(): return lax.ppermute(value, axis, [(i, i ^ mask) for i in range(size)])  7.76 us
    ppermute x4, starting transfers between devices, send_block(): return lax.ppermute(value, ('group', 'tp'), pairs)  5.85 us
    ppermute x4, waiting for transfers between devices, send_block(): return lax.ppermute(value, ('group', 'tp'), pairs)  5.59 us
    pallas_call x1, Pallas kernels, step(): call(lambda *refs: local_kernel(*refs, kv_heads=kv_heads, parts=parts, **...  4.83 us
    pallas_call x1, Pallas kernels, step(): call(lambda *refs: slot_kernel(*refs, groups=groups, kv_heads=kv_heads, s...  3.43 us
    pallas_call x1, Pallas kernels, step(): call(lambda *refs: fetch_columns_kernel(*refs, step=order[1], columns=col...  3.39 us
    pallas_call x1, Pallas kernels, step(): call(lambda *refs: combine_kernel(*refs, groups=groups, slots=slots, **se...  2.44 us
  transfers between devices with their start and end apart: 19, of which 9 were waited for; matrix products, arithmetic and copies ran while one was open for 0% of the time, Pallas kernels for 19%

profile of v1, /device:TPU:0, one launch (start us, length us, event | category | flops | bytes accessed | tf_op | source)
XLA Modules:
  0.0 47.5 jit_solution(11010206871715505817)
XLA Ops:
  0.6 4.8 %shard_map.113 = (f32[512,128]{1,0:T(8,128)S(1)}, bf16[16,2048]{1,0:T(8,128)(2,1)S(1)}, bf16[2,4096,256]{2,1,0:T(8,128)(2,1)S(1)}) custom-call(s32[16]{0:T(128)} %refs_0_.3, bf16[16,2048]{1,0:T(8,128)(2,1)} %refs_1_.2, bf16[16,512,256]{2,1,0:T(8,128)(2,1)} %refs_2_.3, bf16[16,512,256]{2,1,0:T(8,128)(2,1)} %refs_3_.1, bf16[2,4096,256]{2,1,0:T(8,128)(2,1)} %refs_4_.1), custom_call_target="tpu_custom_call" | custom-call | bytes 12582912 | tf_op jit(solution)/shard_map/pallas_call | solution.py:339
  5.5 0.6 %collective-permute-start = (f32[512,128]{1,0:T(8,128)S(1)}, f32[512,128]{1,0:T(8,128)S(1)}, u32[]{:S(2)}, u32[]{:S(2)}) collective-permute-start(f32[512,128]{1,0:T(8,128)S(1)} %get-tuple-element.14.refs_0_), channel_id=1, source_target_pairs={{0,4},{4,0},{8,12},{12,8},{16,20},{20,16},{24,28},{28,24},{1,5},{5... | collective-permute-start | bytes 786440 | tf_op jit(solution)/shard_map/ppermute | solution.py:289
  6.0 2.6 %collective-permute-start.2 = (bf16[16,2048]{1,0:T(8,128)(2,1)S(1)}, bf16[16,2048]{1,0:T(8,128)(2,1)S(1)}, u32[]{:S(2)}, u32[]{:S(2)}) collective-permute-start(bf16[16,2048]{1,0:T(8,128)(2,1)S(1)} %copy-done), channel_id=1, source_target_pairs={{0,8},{4,12},{8,0},{12,4},{16,24},{20,28},{24,16},{28,20},{1,9},{5... | collective-permute-start | bytes 196616 | tf_op jit(solution)/shard_map/ppermute | solution.py:289
  8.6 1.5 %collective-permute-start.4 = (bf16[16,2048]{1,0:T(8,128)(2,1)S(1)}, bf16[16,2048]{1,0:T(8,128)(2,1)S(1)}, u32[]{:S(2)}, u32[]{:S(2)}) collective-permute-start(bf16[16,2048]{1,0:T(8,128)(2,1)S(1)} %copy-done), channel_id=1, source_target_pairs={{0,16},{4,20},{8,24},{12,28},{16,0},{20,4},{24,8},{28,12},{1,17},{... | collective-permute-start | bytes 196616 | tf_op jit(solution)/shard_map/ppermute | solution.py:289
  10.1 1.1 %collective-permute-done.2.refs_5_ = bf16[16,2048]{1,0:T(8,128)(2,1)S(1)} collective-permute-done((bf16[16,2048]{1,0:T(8,128)(2,1)S(1)}, bf16[16,2048]{1,0:T(8,128)(2,1)S(1)}, u32[]{:S(2)}, u32[]{:S(2)}) %collective-permute-start.2) | collective-permute-done | bytes 65568 | tf_op jit(solution)/shard_map/ppermute | solution.py:289
  11.3 1.6 %collective-permute-done.4.refs_7_ = bf16[16,2048]{1,0:T(8,128)(2,1)S(1)} collective-permute-done((bf16[16,2048]{1,0:T(8,128)(2,1)S(1)}, bf16[16,2048]{1,0:T(8,128)(2,1)S(1)}, u32[]{:S(2)}, u32[]{:S(2)}) %collective-permute-start.4) | collective-permute-done | bytes 65568 | tf_op jit(solution)/shard_map/ppermute | solution.py:289
  12.9 2.4 %collective-permute-done.6.refs_9_ = bf16[16,2048]{1,0:T(8,128)(2,1)S(1)} collective-permute-done((bf16[16,2048]{1,0:T(8,128)(2,1)S(1)}, bf16[16,2048]{1,0:T(8,128)(2,1)S(1)}, u32[]{:S(2)}, u32[]{:S(2)}) %collective-permute-start.6) | collective-permute-done | bytes 65568 | tf_op jit(solution)/shard_map/ppermute | solution.py:289
  15.9 2.2 %shard_map.114.refs_12_ = bf16[2,4096,256]{2,1,0:T(8,128)(2,1)S(1)} custom-call(bf16[2,4096,256]{2,1,0:T(8,128)(2,1)} %source.1, bf16[16,2048]{1,0:T(8,128)(2,1)S(1)} %get-tuple-element.15._.refs_3_), custom_call_target="tpu_custom_call" | custom-call | bytes 4194304 | tf_op jit(solution)/shard_map/pallas_call | solution.py:362
  18.2 3.4 %shard_map.115 = (f32[48,128]{1,0:T(8,128)S(1)}, bf16[2048,2048]{1,0:T(8,128)(2,1)S(1)}) custom-call(s32[2]{0:T(128)} %refs_0_.4, s32[2]{0:T(128)} %refs_1_.3, s32[1]{0:T(128)S(6)} %copy.12.refs_2_, bf16[16,2048]{1,0:T(8,128)(2,1)S(1)} %get-tuple-element.15._.refs_3_, bf16[16,2048]{1,0:T(8,128)(2,1)S(1)} %collective-permute-done.1.refs_4_, ...), custom_call_target="tpu_custom_call" | custom-call | bytes 8388608 | tf_op jit(solution)/shard_map/pallas_call | solution.py:374
  21.6 0.6 %collective-permute-start.9 = (f32[48,128]{1,0:T(8,128)S(1)}, f32[48,128]{1,0:T(8,128)S(1)}, u32[]{:S(2)}, u32[]{:S(2)}) collective-permute-start(f32[48,128]{1,0:T(8,128)S(1)} %get-tuple-element.17.refs_2_.refs_1_), channel_id=1, source_target_pairs={{0,8},{4,12},{8,0},{12,4},{16,24},{20,28},{24,16},{28,20},{1,9},{5... | collective-permute-start | bytes 73736 | tf_op jit(solution)/shard_map/ppermute | solution.py:289
  22.2 1.0 %collective-permute-start.11 = (f32[48,128]{1,0:T(8,128)S(1)}, f32[48,128]{1,0:T(8,128)S(1)}, u32[]{:S(2)}, u32[]{:S(2)}) collective-permute-start(f32[48,128]{1,0:T(8,128)S(1)} %get-tuple-element.17.refs_2_.refs_1_), channel_id=1, source_target_pairs={{0,16},{4,20},{8,24},{12,28},{16,0},{20,4},{24,8},{28,12},{1,17},{... | collective-permute-start | bytes 73736 | tf_op jit(solution)/shard_map/ppermute | solution.py:289
  23.2 1.9 %collective-permute-start.13 = (f32[48,128]{1,0:T(8,128)S(1)}, f32[48,128]{1,0:T(8,128)S(1)}, u32[]{:S(2)}, u32[]{:S(2)}) collective-permute-start(f32[48,128]{1,0:T(8,128)S(1)} %get-tuple-element.17.refs_2_.refs_1_), channel_id=1, source_target_pairs={{0,24},{4,28},{8,16},{12,20},{16,8},{20,12},{24,0},{28,4},{1,25},{... | collective-permute-start | bytes 73736 | tf_op jit(solution)/shard_map/ppermute | solution.py:289
  25.7 0.4 collective-permute-done.11.refs_6_
  26.1 1.9 %collective-permute-done.13.refs_8_ = f32[48,128]{1,0:T(8,128)S(1)} collective-permute-done((f32[48,128]{1,0:T(8,128)S(1)}, f32[48,128]{1,0:T(8,128)S(1)}, u32[]{:S(2)}, u32[]{:S(2)}) %collective-permute-start.13) | collective-permute-done | bytes 24608 | tf_op jit(solution)/shard_map/ppermute | solution.py:289
  28.0 3.4 %shard_map.117.refs_1_ = bf16[2048,2048]{1,0:T(8,128)(2,1)S(1)} custom-call(bf16[2048,8192]{1,0:T(8,128)(2,1)} %refs_2_.4, f32[48,128]{1,0:T(8,128)S(1)} %get-tuple-element.17.refs_2_.refs_1_), custom_call_target="tpu_custom_call" | custom-call | bytes 8388608 | tf_op jit(solution)/shard_map/pallas_call | solution.py:401
  31.4 2.4 %shard_map.116 = (bf16[32,2048]{1,0:T(8,128)(2,1)S(1)}, s32[1]{0:T(128)}, bf16[16,2048]{1,0:T(8,128)(2,1)S(1)}, bf16[16,2048]{1,0:T(8,128)(2,1)S(1)}) custom-call(f32[512,128]{1,0:T(8,128)S(1)} %get-tuple-element.14.refs_0_, f32[512,128]{1,0:T(8,128)S(1)} %collective-permute-done.refs_1_, f32[48,128]{1,0:T(8,128)S(1)} %get-tuple-element.17.refs_2_.refs_1_, ...), custom_call_target="tpu_custom_call" | custom-call | bytes 8388608 | tf_op jit(solution)/shard_map/pallas_call | solution.py:420
  33.9 1.5 %shard_map.118 = (bf16[16,2048]{1,0:T(8,128)(2,1)S(1)}, bf16[16,2048]{1,0:T(8,128)(2,1)S(1)}, f32[16,2048]{1,0:T(8,128)S(1)}) custom-call(bf16[32,2048]{1,0:T(8,128)(2,1)S(1)} %get-tuple-element.19.refs_0_, bf16[2048,2048]{1,0:T(8,128)(2,1)S(1)} %shard_map.117.refs_1_, bf16[2048,8192]{1,0:T(8,128)(2,1)} %refs_2_.4), custom_call_target="tpu_custom_call" | custom-call | bytes 8388608 | tf_op jit(solution)/shard_map/pallas_call | solution.py:436
  35.4 0.7 %collective-permute-start.15 = (bf16[16,2048]{1,0:T(8,128)(2,1)S(1)}, bf16[16,2048]{1,0:T(8,128)(2,1)S(1)}, u32[]{:S(2)}, u32[]{:S(2)}) collective-permute-start(bf16[16,2048]{1,0:T(8,128)(2,1)S(1)} %get-tuple-element.21), channel_id=1, source_target_pairs={{4,6},{5,7},{6,4},{7,5},{12,14},{13,15},{14,12},{15,13},{20,22},{2... | collective-permute-start | bytes 196616 | tf_op jit(solution)/shard_map/ppermute | solution.py:284
  36.1 3.6 %collective-permute-start.18 = (bf16[16,2048]{1,0:T(8,128)(2,1)S(1)}, bf16[16,2048]{1,0:T(8,128)(2,1)S(1)}, u32[]{:S(2)}, u32[]{:S(2)}) collective-permute-start(bf16[16,2048]{1,0:T(8,128)(2,1)S(1)} %get-tuple-element.24), channel_id=1, source_target_pairs={{0,4},{1,5},{2,6},{3,7},{4,2},{5,3},{6,0},{7,1},{8,12},{9,13},{10,... | collective-permute-start | bytes 196616 | tf_op jit(solution)/shard_map/ppermute | solution.py:284
  39.7 1.6 %collective-permute-start.16 = (bf16[16,2048]{1,0:T(8,128)(2,1)S(1)}, bf16[16,2048]{1,0:T(8,128)(2,1)S(1)}, u32[]{:S(2)}, u32[]{:S(2)}) collective-permute-start(bf16[16,2048]{1,0:T(8,128)(2,1)S(1)} %get-tuple-element.22), channel_id=1, source_target_pairs={{0,1},{1,0},{2,3},{3,2},{4,7},{5,6},{6,5},{7,4},{8,9},{9,8},{10,11... | collective-permute-start | bytes 196616 | tf_op jit(solution)/shard_map/ppermute | solution.py:284
  41.3 2.9 %collective-permute-done.18.refs_2_ = bf16[16,2048]{1,0:T(8,128)(2,1)S(1)} collective-permute-done((bf16[16,2048]{1,0:T(8,128)(2,1)S(1)}, bf16[16,2048]{1,0:T(8,128)(2,1)S(1)}, u32[]{:S(2)}, u32[]{:S(2)}) %collective-permute-start.18) | collective-permute-done | bytes 65568 | tf_op jit(solution)/shard_map/ppermute | solution.py:284
  44.2 1.2 %collective-permute-done.16.refs_0_ = bf16[16,2048]{1,0:T(8,128)(2,1)S(1)} collective-permute-done((bf16[16,2048]{1,0:T(8,128)(2,1)S(1)}, bf16[16,2048]{1,0:T(8,128)(2,1)S(1)}, u32[]{:S(2)}, u32[]{:S(2)}) %collective-permute-start.16) | collective-permute-done | bytes 65568 | tf_op jit(solution)/shard_map/ppermute | solution.py:284
  45.5 1.4 %collective-permute-done.17.refs_1_ = bf16[16,2048]{1,0:T(8,128)(2,1)S(1)} collective-permute-done((bf16[16,2048]{1,0:T(8,128)(2,1)S(1)}, bf16[16,2048]{1,0:T(8,128)(2,1)S(1)}, u32[]{:S(2)}, u32[]{:S(2)}) %collective-permute-start.17) | collective-permute-done | bytes 65568 | tf_op jit(solution)/shard_map/ppermute | solution.py:284
  46.9 0.7 %shard_map.119 = bf16[16,2048]{1,0:T(8,128)(2,1)} custom-call(f32[16,2048]{1,0:T(8,128)S(1)} %get-tuple-element.20.own, bf16[16,2048]{1,0:T(8,128)(2,1)S(1)} %collective-permute-done.15.final, bf16[16,2048]{1,0:T(8,128)(2,1)S(1)} %collective-permute-done.16.refs_0_, bf16[16,2048]{1,0:T(8,128)(2,1)S(1)} %collective-permute-done.17.refs_1_, ...), custom_call_target="tpu_custom_call" | custom-call | tf_op jit(solution)/shard_map/pallas_call | solution.py:451
  (23 shorter events, 0.6 us)
Async XLA Ops:
  0.6 5.4 %copy-start = (bf16[16,2048]{1,0:T(8,128)(2,1)S(1)}, bf16[16,2048]{1,0:T(8,128)(2,1)}, u32[]{:S(2)}) copy-start(bf16[16,2048]{1,0:T(8,128)(2,1)} %refs_1_.2) | copy-start | bytes 196612
  5.5 25.9 %collective-permute-start = (f32[512,128]{1,0:T(8,128)S(1)}, f32[512,128]{1,0:T(8,128)S(1)}, u32[]{:S(2)}, u32[]{:S(2)}) collective-permute-start(f32[512,128]{1,0:T(8,128)S(1)} %get-tuple-element.14.refs_0_), channel_id=1, source_target_pairs={{0,4},{4,0},{8,12},{12,8},{16,20},{20,16},{24,28},{28,24},{1,5},{5... | collective-permute-start | bytes 786440 | tf_op jit(solution)/shard_map/ppermute | solution.py:289
  6.0 5.2 %collective-permute-start.2 = (bf16[16,2048]{1,0:T(8,128)(2,1)S(1)}, bf16[16,2048]{1,0:T(8,128)(2,1)S(1)}, u32[]{:S(2)}, u32[]{:S(2)}) collective-permute-start(bf16[16,2048]{1,0:T(8,128)(2,1)S(1)} %copy-done), channel_id=1, source_target_pairs={{0,8},{4,12},{8,0},{12,4},{16,24},{20,28},{24,16},{28,20},{1,9},{5... | collective-permute-start | bytes 196616 | tf_op jit(solution)/shard_map/ppermute | solution.py:289
  8.6 4.3 %collective-permute-start.4 = (bf16[16,2048]{1,0:T(8,128)(2,1)S(1)}, bf16[16,2048]{1,0:T(8,128)(2,1)S(1)}, u32[]{:S(2)}, u32[]{:S(2)}) collective-permute-start(bf16[16,2048]{1,0:T(8,128)(2,1)S(1)} %copy-done), channel_id=1, source_target_pairs={{0,16},{4,20},{8,24},{12,28},{16,0},{20,4},{24,8},{28,12},{1,17},{... | collective-permute-start | bytes 196616 | tf_op jit(solution)/shard_map/ppermute | solution.py:289
  10.1 5.2 %collective-permute-start.6 = (bf16[16,2048]{1,0:T(8,128)(2,1)S(1)}, bf16[16,2048]{1,0:T(8,128)(2,1)S(1)}, u32[]{:S(2)}, u32[]{:S(2)}) collective-permute-start(bf16[16,2048]{1,0:T(8,128)(2,1)S(1)} %copy-done), channel_id=1, source_target_pairs={{0,24},{4,28},{8,16},{12,20},{16,8},{20,12},{24,0},{28,4},{1,25},{... | collective-permute-start | bytes 196616 | tf_op jit(solution)/shard_map/ppermute | solution.py:289
  10.1 8.0 %collective-permute-start.1 = (bf16[16,2048]{1,0:T(8,128)(2,1)S(1)}, bf16[16,2048]{1,0:T(8,128)(2,1)S(1)}, u32[]{:S(2)}, u32[]{:S(2)}) collective-permute-start(bf16[16,2048]{1,0:T(8,128)(2,1)S(1)} %copy-done), channel_id=1, source_target_pairs={{0,4},{4,0},{8,12},{12,8},{16,20},{20,16},{24,28},{28,24},{1,5},{5... | collective-permute-start | bytes 196616 | tf_op jit(solution)/shard_map/ppermute | solution.py:289
  11.3 6.9 %collective-permute-start.3 = (bf16[16,2048]{1,0:T(8,128)(2,1)S(1)}, bf16[16,2048]{1,0:T(8,128)(2,1)S(1)}, u32[]{:S(2)}, u32[]{:S(2)}) collective-permute-start(bf16[16,2048]{1,0:T(8,128)(2,1)S(1)} %collective-permute-done.2.refs_5_), channel_id=1, source_target_pairs={{0,4},{4,0},{8,12},{12,8},{16,20},{20,16},{24,28},{28,24},{1,5},{5... | collective-permute-start | bytes 196616 | tf_op jit(solution)/shard_map/ppermute | solution.py:289
  12.9 5.3 %collective-permute-start.5 = (bf16[16,2048]{1,0:T(8,128)(2,1)S(1)}, bf16[16,2048]{1,0:T(8,128)(2,1)S(1)}, u32[]{:S(2)}, u32[]{:S(2)}) collective-permute-start(bf16[16,2048]{1,0:T(8,128)(2,1)S(1)} %collective-permute-done.4.refs_7_), channel_id=1, source_target_pairs={{0,4},{4,0},{8,12},{12,8},{16,20},{20,16},{24,28},{28,24},{1,5},{5... | collective-permute-start | bytes 196616 | tf_op jit(solution)/shard_map/ppermute | solution.py:289
  15.3 2.9 %collective-permute-start.7 = (bf16[16,2048]{1,0:T(8,128)(2,1)S(1)}, bf16[16,2048]{1,0:T(8,128)(2,1)S(1)}, u32[]{:S(2)}, u32[]{:S(2)}) collective-permute-start(bf16[16,2048]{1,0:T(8,128)(2,1)S(1)} %collective-permute-done.6.refs_9_), channel_id=1, source_target_pairs={{0,4},{4,0},{8,12},{12,8},{16,20},{20,16},{24,28},{28,24},{1,5},{5... | collective-permute-start | bytes 196616 | tf_op jit(solution)/shard_map/ppermute | solution.py:289
  21.6 3.9 %collective-permute-start.9 = (f32[48,128]{1,0:T(8,128)S(1)}, f32[48,128]{1,0:T(8,128)S(1)}, u32[]{:S(2)}, u32[]{:S(2)}) collective-permute-start(f32[48,128]{1,0:T(8,128)S(1)} %get-tuple-element.17.refs_2_.refs_1_), channel_id=1, source_target_pairs={{0,8},{4,12},{8,0},{12,4},{16,24},{20,28},{24,16},{28,20},{1,9},{5... | collective-permute-start | bytes 73736 | tf_op jit(solution)/shard_map/ppermute | solution.py:289
  22.2 3.8 %collective-permute-start.11 = (f32[48,128]{1,0:T(8,128)S(1)}, f32[48,128]{1,0:T(8,128)S(1)}, u32[]{:S(2)}, u32[]{:S(2)}) collective-permute-start(f32[48,128]{1,0:T(8,128)S(1)} %get-tuple-element.17.refs_2_.refs_1_), channel_id=1, source_target_pairs={{0,16},{4,20},{8,24},{12,28},{16,0},{20,4},{24,8},{28,12},{1,17},{... | collective-permute-start | bytes 73736 | tf_op jit(solution)/shard_map/ppermute | solution.py:289
  23.2 4.7 %collective-permute-start.13 = (f32[48,128]{1,0:T(8,128)S(1)}, f32[48,128]{1,0:T(8,128)S(1)}, u32[]{:S(2)}, u32[]{:S(2)}) collective-permute-start(f32[48,128]{1,0:T(8,128)S(1)} %get-tuple-element.17.refs_2_.refs_1_), channel_id=1, source_target_pairs={{0,24},{4,28},{8,16},{12,20},{16,8},{20,12},{24,0},{28,4},{1,25},{... | collective-permute-start | bytes 73736 | tf_op jit(solution)/shard_map/ppermute | solution.py:289
  25.2 6.2 %collective-permute-start.8 = (f32[48,128]{1,0:T(8,128)S(1)}, f32[48,128]{1,0:T(8,128)S(1)}, u32[]{:S(2)}, u32[]{:S(2)}) collective-permute-start(f32[48,128]{1,0:T(8,128)S(1)} %get-tuple-element.17.refs_2_.refs_1_), channel_id=1, source_target_pairs={{0,4},{4,0},{8,12},{12,8},{16,20},{20,16},{24,28},{28,24},{1,5},{5... | collective-permute-start | bytes 73736 | tf_op jit(solution)/shard_map/ppermute | solution.py:289
  25.5 5.9 %collective-permute-start.10 = (f32[48,128]{1,0:T(8,128)S(1)}, f32[48,128]{1,0:T(8,128)S(1)}, u32[]{:S(2)}, u32[]{:S(2)}) collective-permute-start(f32[48,128]{1,0:T(8,128)S(1)} %collective-permute-done.9.refs_4_), channel_id=1, source_target_pairs={{0,4},{4,0},{8,12},{12,8},{16,20},{20,16},{24,28},{28,24},{1,5},{5... | collective-permute-start | bytes 73736 | tf_op jit(solution)/shard_map/ppermute | solution.py:289
  26.1 5.3 %collective-permute-start.12 = (f32[48,128]{1,0:T(8,128)S(1)}, f32[48,128]{1,0:T(8,128)S(1)}, u32[]{:S(2)}, u32[]{:S(2)}) collective-permute-start(f32[48,128]{1,0:T(8,128)S(1)} %collective-permute-done.11.refs_6_), channel_id=1, source_target_pairs={{0,4},{4,0},{8,12},{12,8},{16,20},{20,16},{24,28},{28,24},{1,5},{5... | collective-permute-start | bytes 73736 | tf_op jit(solution)/shard_map/ppermute | solution.py:289
  28.0 3.4 %collective-permute-start.14 = (f32[48,128]{1,0:T(8,128)S(1)}, f32[48,128]{1,0:T(8,128)S(1)}, u32[]{:S(2)}, u32[]{:S(2)}) collective-permute-start(f32[48,128]{1,0:T(8,128)S(1)} %collective-permute-done.13.refs_8_), channel_id=1, source_target_pairs={{0,4},{4,0},{8,12},{12,8},{16,20},{20,16},{24,28},{28,24},{1,5},{5... | collective-permute-start | bytes 73736 | tf_op jit(solution)/shard_map/ppermute | solution.py:289
  35.4 5.9 %collective-permute-start.15 = (bf16[16,2048]{1,0:T(8,128)(2,1)S(1)}, bf16[16,2048]{1,0:T(8,128)(2,1)S(1)}, u32[]{:S(2)}, u32[]{:S(2)}) collective-permute-start(bf16[16,2048]{1,0:T(8,128)(2,1)S(1)} %get-tuple-element.21), channel_id=1, source_target_pairs={{4,6},{5,7},{6,4},{7,5},{12,14},{13,15},{14,12},{15,13},{20,22},{2... | collective-permute-start | bytes 196616 | tf_op jit(solution)/shard_map/ppermute | solution.py:284
  36.1 8.1 %collective-permute-start.18 = (bf16[16,2048]{1,0:T(8,128)(2,1)S(1)}, bf16[16,2048]{1,0:T(8,128)(2,1)S(1)}, u32[]{:S(2)}, u32[]{:S(2)}) collective-permute-start(bf16[16,2048]{1,0:T(8,128)(2,1)S(1)} %get-tuple-element.24), channel_id=1, source_target_pairs={{0,4},{1,5},{2,6},{3,7},{4,2},{5,3},{6,0},{7,1},{8,12},{9,13},{10,... | collective-permute-start | bytes 196616 | tf_op jit(solution)/shard_map/ppermute | solution.py:284
  39.7 5.8 %collective-permute-start.16 = (bf16[16,2048]{1,0:T(8,128)(2,1)S(1)}, bf16[16,2048]{1,0:T(8,128)(2,1)S(1)}, u32[]{:S(2)}, u32[]{:S(2)}) collective-permute-start(bf16[16,2048]{1,0:T(8,128)(2,1)S(1)} %get-tuple-element.22), channel_id=1, source_target_pairs={{0,1},{1,0},{2,3},{3,2},{4,7},{5,6},{6,5},{7,4},{8,9},{9,8},{10,11... | collective-permute-start | bytes 196616 | tf_op jit(solution)/shard_map/ppermute | solution.py:284
  41.3 5.6 %collective-permute-start.17 = (bf16[16,2048]{1,0:T(8,128)(2,1)S(1)}, bf16[16,2048]{1,0:T(8,128)(2,1)S(1)}, u32[]{:S(2)}, u32[]{:S(2)}) collective-permute-start(bf16[16,2048]{1,0:T(8,128)(2,1)S(1)} %get-tuple-element.23), channel_id=1, source_target_pairs={{0,5},{1,4},{2,7},{3,6},{4,3},{5,2},{6,1},{7,0},{8,13},{9,12},{10,... | collective-permute-start | bytes 196616 | tf_op jit(solution)/shard_map/ppermute | solution.py:284

commit v2 on v1

--- a/solution.py
+++ b/solution.py
@@ -65,25 +65,20 @@
     return copy
 
 
+def open_kernel(_, token):
+    token[...] = jnp.zeros_like(token)
+
+
 def local_kernel(
-    lengths_in, q_in, keys_in, values_in, pool_in,
-    packed, q_ref, pool_ref,
-    lengths, keys, values, q_heads, scores, weights, sems,
-    *, rows, heads, kv_heads, parts,
+    lengths_in, q_in, keys, values, weight_in, _,
+    packed, q_ref, weight,
+    lengths, q_heads, scores, weights, sems,
+    *, rows, heads, kv_heads, step, columns,
 ):
     positions = keys.shape[1]
-    step = rows // parts
     lengths_copy = copy_in(lengths_in, lengths, sems.at[0])
     q_copy = copy_in(q_in, q_ref, sems.at[1])
-    key_copies, value_copies = [], []
-    for held, source, target, base in (
-        (key_copies, keys_in, keys, 2),
-        (value_copies, values_in, values, 2 + parts),
-    ):
-        for p in range(parts):
-            at = pl.ds(p * step, step)
-            held.append(copy_in(source.at[at], target.at[at], sems.at[base + p]))
-    pool_copy = copy_in(pool_in, pool_ref, sems.at[2 + 2 * parts])
+    weight_copy = copy_in(columns_of(weight_in, step, columns), weight, sems.at[2])
     q_copy.wait()
     wide = q_ref[...].astype(f32)
     for h in range(heads):
@@ -91,57 +86,48 @@
     lengths_copy.wait()
     place = lax.broadcasted_iota(jnp.int32, (heads, positions), 1)
     lane = lax.broadcasted_iota(jnp.int32, (heads, LANES), 1)
-    for p in range(parts):
-        key_copies[p].wait()
-        for r in range(p * step, (p + 1) * step):
-            at = pl.ds(r * heads, heads)
-            query = spread_heads(q_heads[at, :].astype(bf16), kv_heads)
-            scores[at, :] = jnp.where(place < lengths[r], scores_of(query, keys[r]), far_below)
+    for r in range(rows):
+        at = pl.ds(r * heads, heads)
+        query = spread_heads(q_heads[at, :].astype(bf16), kv_heads)
+        scores[at, :] = jnp.where(place < lengths[r], scores_of(query, keys[r]), far_below)
     for r in range(rows):
         at = pl.ds(r * heads, heads)
         masked = scores[at, :]
         high = jnp.max(masked, axis=-1, keepdims=True)
-        weight = jnp.where(place < lengths[r], jnp.exp(masked - high), 0.0)
-        total = jnp.sum(weight, axis=-1, keepdims=True)
-        weights[r] = weight.astype(bf16)
+        weight_of = jnp.where(place < lengths[r], jnp.exp(masked - high), 0.0)
+        total = jnp.sum(weight_of, axis=-1, keepdims=True)
+        weights[r] = weight_of.astype(bf16)
         packed[pl.ds((rows + r) * heads, heads), :] = jnp.where(lane == 0, high, total)
-    for p in range(parts):
-        value_copies[p].wait()
-        for r in range(p * step, (p + 1) * step):
-            mixed = jnp.dot(weights[r], values[r], preferred_element_type=f32)
-            packed[pl.ds(r * heads, heads), :] = own_columns(mixed, kv_heads)
-    pool_copy.wait()
-
-
-def fetch_kernel(source, _, target, sem):
-    copy_in(source, target, sem).wait()
-
-
-def step_mask(group, step, tp):
-    return (tp // 2) * (group % 2) + step
+    for r in range(rows):
+        mixed = jnp.dot(weights[r], values[r], preferred_element_type=f32)
+        packed[pl.ds(r * heads, heads), :] = own_columns(mixed, kv_heads)
+    weight_copy.wait()
+
+
+def step_mask(group, step):
+    return 2 * step + group % 2
 
 
 def columns_of(weight, step, columns):
-    tp = lax.axis_size("tp")
-    mask = step_mask(lax.axis_index("group"), step, tp)
+    mask = step_mask(lax.axis_index("group"), step)
     start = jnp.bitwise_xor(lax.axis_index("tp"), mask) * columns
     return weight.at[:, pl.ds(pl.multiple_of(start, columns), columns)]
 
 
-def fetch_columns_kernel(source, _, target, sem, *, step, columns):
-    copy_in(columns_of(source, step, columns), target, sem).wait()
-
-
-def slot_kernel(*refs, groups, rows, heads, kv_heads, slots, chunk, step, columns):
+def slot_kernel(*refs, groups, rows, heads, kv_heads, slots, chunk, ahead, columns):
     owners_in, fills_in, free = refs[:3]
     shards = refs[3 : 3 + groups]
     keys, values, weight_in = refs[3 + groups : 6 + groups]
-    packed, weight, owners, fills, q_heads, scores, sems = refs[6 + groups :]
+    packed, *rest = refs[6 + groups :]
+    weight_copy = None
+    if ahead is not None:
+        weight_copy = copy_in(columns_of(weight_in, ahead, columns), rest[0], rest[-1].at[2])
+        rest = rest[1:]
+    owners, fills, q_heads, scores, sems = rest
     copies = [
         copy_in(owners_in, owners, sems.at[0]),
         copy_in(fills_in, fills, sems.at[1]),
     ]
-    weight_copy = copy_in(columns_of(weight_in, step, columns), weight, sems.at[2])
     for copy in copies:
         copy.wait()
     positions = keys.shape[1]
@@ -183,7 +169,8 @@
         stats = jnp.where(lane == slots + s, total, stats)
         stats = jnp.where(lane == 2 * slots + s, owners[s].astype(f32), stats)
     packed[slots * heads :, :] = stats
-    weight_copy.wait()
+    if weight_copy is not None:
+        weight_copy.wait()
 
 
 def project(x, weight, same, other, chunk, own=None):
@@ -276,10 +263,10 @@
 def send_block(value, step, cross):
     groups, tp = lax.axis_size("group"), lax.axis_size("tp")
     pairs = [
-        (g * tp + z, (g ^ cross) * tp + (z ^ step_mask(g, step, tp)))
+        (g * tp + z, (g ^ cross) * tp + (z ^ step_mask(g, step)))
         for g in range(groups)
         for z in range(tp)
-        if cross or step_mask(g, step, tp)
+        if cross or step_mask(g, step)
     ]
     return lax.ppermute(value, ("group", "tp"), pairs)
 
@@ -322,67 +309,57 @@
     chunk = math.gcd(columns, 512)
     sizes = dict(rows=rows, heads=heads)
 
-    parts = math.gcd(rows, 4)
     shards = gather_group(queries)
-    (
-        queries, cache_keys, cache_values, pool_keys, pool_values,
-        row_lengths, slot_owner, slot_fill, out_weight,
-    ) = (
+    queries, row_lengths, slot_owner, slot_fill, out_weight = (
         pltpu.with_memory_space_constraint(argument, pltpu.MemorySpace.HBM)
-        for argument in (
-            queries, cache_keys, cache_values, pool_keys, pool_values,
-            row_lengths, slot_owner, slot_fill, out_weight,
-        )
+        for argument in (queries, row_lengths, slot_owner, slot_fill, out_weight)
     )
     copies = pltpu.SemaphoreType.DMA
 
-    local, own_queries, held_keys = call(
-        lambda *refs: local_kernel(*refs, kv_heads=kv_heads, parts=parts, **sizes),
+    order = list(range(tp // 2 - 1, -1, -1))
+    held = jax.ShapeDtypeStruct((width, columns), out_weight.dtype)
+    moved = 2 * width * columns
+    weights = {}
+
+    token = call(open_kernel, jax.ShapeDtypeStruct((8, LANES), f32), [HBM], vmem=1 << 20)(
+        out_weight
+    )
+    local, own_queries, weights[order[0]] = call(
+        lambda *refs: local_kernel(
+            *refs, kv_heads=kv_heads, step=order[0], columns=columns, **sizes
+        ),
         [
             jax.ShapeDtypeStruct((2 * rows * heads, LANES), f32),
             jax.ShapeDtypeStruct(queries.shape, queries.dtype),
-            jax.ShapeDtypeStruct(pool_keys.shape, pool_keys.dtype),
+            held,
         ],
-        [HBM] * 5,
+        [HBM, HBM, VMEM, VMEM, HBM, VMEM],
         scratch=[
             pltpu.SMEM(row_lengths.shape, jnp.int32),
-            pltpu.VMEM(cache_keys.shape, bf16),
-            pltpu.VMEM(cache_values.shape, bf16),
             pltpu.VMEM((rows * heads, HEAD_DIM), f32),
             pltpu.VMEM((rows * heads, cache_keys.shape[1]), f32),
             pltpu.VMEM((rows, heads, cache_keys.shape[1]), bf16),
-            copies((3 + 2 * parts,)),
+            copies((3,)),
         ],
-        moved=2 * (cache_keys.size + cache_values.size + pool_keys.size),
-        vmem=12 << 20,
-    )(row_lengths, queries, cache_keys, cache_values, pool_keys)
+        moved=moved,
+        vmem=4 << 20,
+    )(row_lengths, queries, cache_keys, cache_values, out_weight, token)
     shards[0] = own_queries
     pair_local = swap(local, "group", 1)
 
-    held_values = call(
-        fetch_kernel,
-        jax.ShapeDtypeStruct(pool_values.shape, pool_values.dtype),
-        [HBM, pl.BlockSpec(memory_space=pl.ANY)],
-        scratch=[copies],
-        moved=2 * pool_values.size,
-        vmem=1 << 20,
-    )(pool_values, own_queries)
-
-    order = list(range(tp // 2 - 1, -1, -1))
-    held = jax.ShapeDtypeStruct((width, columns), out_weight.dtype)
-    weights = {}
-    packed, weights[order[0]] = call(
+    ahead = order[1] if len(order) > 1 else None
+    packed, *more = call(
         lambda *refs: slot_kernel(
             *refs,
             groups=groups,
             kv_heads=kv_heads,
             slots=slots,
             chunk=math.gcd(positions, 512),
-            step=order[0],
+            ahead=ahead,
             columns=columns,
             **sizes,
         ),
-        [jax.ShapeDtypeStruct(((slots + 1) * heads, LANES), f32), held],
+        [jax.ShapeDtypeStruct(((slots + 1) * heads, LANES), f32)] + [held] * (ahead is not None),
         [HBM] * 2 + [SMEM] + [VMEM] * (groups + 2) + [HBM],
         scratch=[
             pltpu.SMEM(slot_owner.shape, jnp.int32),
@@ -391,25 +368,16 @@
             pltpu.VMEM((slots * heads, positions), f32),
             copies((3,)),
         ],
-        moved=2 * width * columns,
-        vmem=8 << 20,
-    )(slot_owner, slot_fill, free_counts, *shards, held_keys, held_values, out_weight)
+        moved=moved,
+        vmem=4 << 20,
+    )(slot_owner, slot_fill, free_counts, *shards, pool_keys, pool_values, out_weight)
+    if more:
+        weights[ahead] = more[0]
 
     far = gather_group(packed)
-
-    if len(order) > 1:
-        weights[order[1]] = call(
-            lambda *refs: fetch_columns_kernel(*refs, step=order[1], columns=columns),
-            held,
-            [HBM, pl.BlockSpec(memory_space=pl.ANY)],
-            scratch=[copies],
-            moved=2 * width * columns,
-            vmem=1 << 20,
-        )(out_weight, packed)
 
     block = jax.ShapeDtypeStruct((rows, columns), bf16)
     whole = jax.ShapeDtypeStruct((rows, columns), f32)
-    moved = 2 * width * columns
     received = []
     for i, step in enumerate(order):
         last = step == 0

time: 47.8 us -> 46.2 us (0.967)
  Pallas kernels: 18.5 us -> 11.7 us
  local copies, waits for them, and re-layouts: 0.01 us -> 3.45 us
  waiting for transfers between devices: 13.3 us -> 15 us
    pallas_call x3 -> x2, Pallas kernels: 10.4 us -> 3.6 us  [the longest x1 3.59 us: step(): call(lambda *refs: local_kernel(*refs, kv_heads=kv_heads, step=order[0],...]
    unnamed x2 -> x10, local copies, waits for them, and re-layouts: 0.01 us -> 3.45 us
    ppermute x15, waiting for transfers between devices: 7.76 us -> 9.15 us  [swap(): return lax.ppermute(value, axis, [(i, i ^ mask) for i in range(size)])]
  transfers between devices with their start and end apart: 19 -> 19, of which waited for: 9 -> 10; matrix products, arithmetic and copies ran while one was open for 0% -> 0% of each run, Pallas kernels for 19% -> 7%
where the time goes in v2:
time: 46.2 us; the launch traced here: 45.7 us
  waiting for transfers between devices  15 us (32%)
  starting transfers between devices  14.3 us (31%)
  Pallas kernels  11.7 us (25%)
  local copies, waits for them, and re-layouts  3.45 us (7%)
  between operations  1.39 us (3%)
    ppermute x15, waiting for transfers between devices, swap(): return lax.ppermute(value, axis, [(i, i ^ mask) for i in range(size)])  9.15 us
    ppermute x15, starting transfers between devices, swap(): return lax.ppermute(value, axis, [(i, i ^ mask) for i in range(size)])  8.41 us
    ppermute x4, starting transfers between devices, send_block(): return lax.ppermute(value, ('group', 'tp'), pairs)  5.85 us
    ppermute x4, waiting for transfers between devices, send_block(): return lax.ppermute(value, ('group', 'tp'), pairs)  5.81 us
    pallas_call x1, Pallas kernels, step(): call(lambda *refs: local_kernel(*refs, kv_heads=kv_heads, step=order[0],...  3.59 us
    unnamed x10, local copies, waits for them, and re-layouts  3.45 us
    pallas_call x1, Pallas kernels, step(): call(lambda *refs: slot_kernel(*refs, groups=groups, kv_heads=kv_heads, s...  3.41 us
    pallas_call x1, Pallas kernels, step(): call(lambda *refs: combine_kernel(*refs, groups=groups, slots=slots, **se...  2.44 us
  transfers between devices with their start and end apart: 19, of which 10 were waited for; matrix products, arithmetic and copies ran while one was open for 0% of the time, Pallas kernels for 7%

profile of v2, /device:TPU:0, one launch (start us, length us, event | category | flops | bytes accessed | tf_op | source)
XLA Modules:
  0.0 45.7 jit_solution(127621085661999834)
XLA Ops:
  0.7 2.2 %copy-done = bf16[16,512,256]{2,1,0:T(8,128)(2,1)S(1)} copy-done((bf16[16,512,256]{2,1,0:T(8,128)(2,1)S(1)}, bf16[16,512,256]{2,1,0:T(8,128)(2,1)}, u32[]{:S(2)}) %copy-start) | copy-done | bytes 4194328
  2.8 1.3 %copy-done.1 = bf16[16,512,256]{2,1,0:T(8,128)(2,1)S(1)} copy-done((bf16[16,512,256]{2,1,0:T(8,128)(2,1)S(1)}, bf16[16,512,256]{2,1,0:T(8,128)(2,1)}, u32[]{:S(2)}) %copy-start.1) | copy-done | bytes 4194328
  4.1 3.6 %shard_map.114 = (f32[512,128]{1,0:T(8,128)S(1)}, bf16[16,2048]{1,0:T(8,128)(2,1)S(1)}, bf16[2048,2048]{1,0:T(8,128)(2,1)S(1)}) custom-call(s32[16]{0:T(128)} %refs_0_.2, bf16[16,2048]{1,0:T(8,128)(2,1)} %refs_1_.2, bf16[16,512,256]{2,1,0:T(8,128)(2,1)S(1)} %copy-done, bf16[16,512,256]{2,1,0:T(8,128)(2,1)S(1)} %copy-done.1, bf16[2048,8192]{1,0:T(8,128)(2,1)} %refs_2_.4, ...), custom_call_target="tpu_custom_call" | custom-call | bytes 8388608 | tf_op jit(solution)/shard_map/pallas_call | solution.py:327
  7.7 0.6 %collective-permute-start = (f32[512,128]{1,0:T(8,128)S(1)}, f32[512,128]{1,0:T(8,128)S(1)}, u32[]{:S(2)}, u32[]{:S(2)}) collective-permute-start(f32[512,128]{1,0:T(8,128)S(1)} %get-tuple-element.14.refs_0_), channel_id=1, source_target_pairs={{0,4},{4,0},{8,12},{12,8},{16,20},{20,16},{24,28},{28,24},{1,5},{5... | collective-permute-start | bytes 786440 | tf_op jit(solution)/shard_map/ppermute | solution.py:276
  8.3 2.6 %collective-permute-start.2 = (bf16[16,2048]{1,0:T(8,128)(2,1)S(1)}, bf16[16,2048]{1,0:T(8,128)(2,1)S(1)}, u32[]{:S(2)}, u32[]{:S(2)}) collective-permute-start(bf16[16,2048]{1,0:T(8,128)(2,1)S(1)} %copy-done.4), channel_id=1, source_target_pairs={{0,8},{4,12},{8,0},{12,4},{16,24},{20,28},{24,16},{28,20},{1,9},{5... | collective-permute-start | bytes 196616 | tf_op jit(solution)/shard_map/ppermute | solution.py:276
  10.8 1.5 %collective-permute-start.4 = (bf16[16,2048]{1,0:T(8,128)(2,1)S(1)}, bf16[16,2048]{1,0:T(8,128)(2,1)S(1)}, u32[]{:S(2)}, u32[]{:S(2)}) collective-permute-start(bf16[16,2048]{1,0:T(8,128)(2,1)S(1)} %copy-done.4), channel_id=1, source_target_pairs={{0,16},{4,20},{8,24},{12,28},{16,0},{20,4},{24,8},{28,12},{1,17},{... | collective-permute-start | bytes 196616 | tf_op jit(solution)/shard_map/ppermute | solution.py:276
  12.4 1.1 %collective-permute-done.2.refs_5_ = bf16[16,2048]{1,0:T(8,128)(2,1)S(1)} collective-permute-done((bf16[16,2048]{1,0:T(8,128)(2,1)S(1)}, bf16[16,2048]{1,0:T(8,128)(2,1)S(1)}, u32[]{:S(2)}, u32[]{:S(2)}) %collective-permute-start.2) | collective-permute-done | bytes 65568 | tf_op jit(solution)/shard_map/ppermute | solution.py:276
  13.5 1.6 %collective-permute-done.4.refs_7_ = bf16[16,2048]{1,0:T(8,128)(2,1)S(1)} collective-permute-done((bf16[16,2048]{1,0:T(8,128)(2,1)S(1)}, bf16[16,2048]{1,0:T(8,128)(2,1)S(1)}, u32[]{:S(2)}, u32[]{:S(2)}) %collective-permute-start.4) | collective-permute-done | bytes 65568 | tf_op jit(solution)/shard_map/ppermute | solution.py:276
  15.1 2.4 %collective-permute-done.6.refs_9_ = bf16[16,2048]{1,0:T(8,128)(2,1)S(1)} collective-permute-done((bf16[16,2048]{1,0:T(8,128)(2,1)S(1)}, bf16[16,2048]{1,0:T(8,128)(2,1)S(1)}, u32[]{:S(2)}, u32[]{:S(2)}) %collective-permute-start.6) | collective-permute-done | bytes 65568 | tf_op jit(solution)/shard_map/ppermute | solution.py:276
  18.2 0.6 %collective-permute-done.7.refs_10_ = bf16[16,2048]{1,0:T(8,128)(2,1)S(1)} collective-permute-done((bf16[16,2048]{1,0:T(8,128)(2,1)S(1)}, bf16[16,2048]{1,0:T(8,128)(2,1)S(1)}, u32[]{:S(2)}, u32[]{:S(2)}) %collective-permute-start.7) | collective-permute-done | bytes 65568 | tf_op jit(solution)/shard_map/ppermute | solution.py:276
  18.8 3.4 %shard_map.115 = (f32[48,128]{1,0:T(8,128)S(1)}, bf16[2048,2048]{1,0:T(8,128)(2,1)S(1)}) custom-call(s32[2]{0:T(128)} %refs_0_.3, s32[2]{0:T(128)} %refs_1_.3, s32[1]{0:T(128)S(6)} %copy.12.refs_2_, bf16[16,2048]{1,0:T(8,128)(2,1)S(1)} %get-tuple-element.15.refs_3_, bf16[16,2048]{1,0:T(8,128)(2,1)S(1)} %collective-permute-done.1.refs_4_, ...), custom_call_target="tpu_custom_call" | custom-call | bytes 8388608 | tf_op jit(solution)/shard_map/pallas_call | solution.py:351
  22.2 0.6 %collective-permute-start.9 = (f32[48,128]{1,0:T(8,128)S(1)}, f32[48,128]{1,0:T(8,128)S(1)}, u32[]{:S(2)}, u32[]{:S(2)}) collective-permute-start(f32[48,128]{1,0:T(8,128)S(1)} %get-tuple-element.16.refs_2_), channel_id=1, source_target_pairs={{0,8},{4,12},{8,0},{12,4},{16,24},{20,28},{24,16},{28,20},{1,9},{5... | collective-permute-start | bytes 73736 | tf_op jit(solution)/shard_map/ppermute | solution.py:276
  22.8 0.7 %collective-permute-start.11 = (f32[48,128]{1,0:T(8,128)S(1)}, f32[48,128]{1,0:T(8,128)S(1)}, u32[]{:S(2)}, u32[]{:S(2)}) collective-permute-start(f32[48,128]{1,0:T(8,128)S(1)} %get-tuple-element.16.refs_2_), channel_id=1, source_target_pairs={{0,16},{4,20},{8,24},{12,28},{16,0},{20,4},{24,8},{28,12},{1,17},{... | collective-permute-start | bytes 73736 | tf_op jit(solution)/shard_map/ppermute | solution.py:276
  23.5 2.3 %collective-permute-start.13 = (f32[48,128]{1,0:T(8,128)S(1)}, f32[48,128]{1,0:T(8,128)S(1)}, u32[]{:S(2)}, u32[]{:S(2)}) collective-permute-start(f32[48,128]{1,0:T(8,128)S(1)} %get-tuple-element.16.refs_2_), channel_id=1, source_target_pairs={{0,24},{4,28},{8,16},{12,20},{16,8},{20,12},{24,0},{28,4},{1,25},{... | collective-permute-start | bytes 73736 | tf_op jit(solution)/shard_map/ppermute | solution.py:276
  26.3 0.4 collective-permute-done.11.refs_6_
  26.6 1.6 %collective-permute-done.13.refs_8_ = f32[48,128]{1,0:T(8,128)S(1)} collective-permute-done((f32[48,128]{1,0:T(8,128)S(1)}, f32[48,128]{1,0:T(8,128)S(1)}, u32[]{:S(2)}, u32[]{:S(2)}) %collective-permute-start.13) | collective-permute-done | bytes 24608 | tf_op jit(solution)/shard_map/ppermute | solution.py:276
  28.2 1.2 %collective-permute-done.14.refs_9_ = f32[48,128]{1,0:T(8,128)S(1)} collective-permute-done((f32[48,128]{1,0:T(8,128)S(1)}, f32[48,128]{1,0:T(8,128)S(1)}, u32[]{:S(2)}, u32[]{:S(2)}) %collective-permute-start.14) | collective-permute-done | bytes 24608 | tf_op jit(solution)/shard_map/ppermute | solution.py:276
  29.4 2.4 %shard_map.116 = (bf16[32,2048]{1,0:T(8,128)(2,1)S(1)}, s32[1]{0:T(128)}, bf16[16,2048]{1,0:T(8,128)(2,1)S(1)}, bf16[16,2048]{1,0:T(8,128)(2,1)S(1)}) custom-call(f32[512,128]{1,0:T(8,128)S(1)} %get-tuple-element.14.refs_0_, f32[512,128]{1,0:T(8,128)S(1)} %collective-permute-done.refs_1_, f32[48,128]{1,0:T(8,128)S(1)} %get-tuple-element.16.refs_2_, ...), custom_call_target="tpu_custom_call" | custom-call | bytes 8388608 | tf_op jit(solution)/shard_map/pallas_call | solution.py:388
  31.8 1.5 %shard_map.117 = (bf16[16,2048]{1,0:T(8,128)(2,1)S(1)}, bf16[16,2048]{1,0:T(8,128)(2,1)S(1)}, f32[16,2048]{1,0:T(8,128)S(1)}) custom-call(bf16[32,2048]{1,0:T(8,128)(2,1)S(1)} %get-tuple-element.18.refs_0_, bf16[2048,2048]{1,0:T(8,128)(2,1)S(1)} %get-tuple-element.19.refs_1_, bf16[2048,8192]{1,0:T(8,128)(2,1)} %refs_2_.4), custom_call_target="tpu_custom_call" | custom-call | bytes 8388608 | tf_op jit(solution)/shard_map/pallas_call | solution.py:404
  33.4 0.7 %collective-permute-start.15 = (bf16[16,2048]{1,0:T(8,128)(2,1)S(1)}, bf16[16,2048]{1,0:T(8,128)(2,1)S(1)}, u32[]{:S(2)}, u32[]{:S(2)}) collective-permute-start(bf16[16,2048]{1,0:T(8,128)(2,1)S(1)} %get-tuple-element.21), channel_id=1, source_target_pairs={{4,5},{5,4},{6,7},{7,6},{12,13},{13,12},{14,15},{15,14},{20,21},{2... | collective-permute-start | bytes 196616 | tf_op jit(solution)/shard_map/ppermute | solution.py:271
  34.0 2.6 %collective-permute-start.18 = (bf16[16,2048]{1,0:T(8,128)(2,1)S(1)}, bf16[16,2048]{1,0:T(8,128)(2,1)S(1)}, u32[]{:S(2)}, u32[]{:S(2)}) collective-permute-start(bf16[16,2048]{1,0:T(8,128)(2,1)S(1)} %get-tuple-element.24), channel_id=1, source_target_pairs={{0,4},{1,5},{2,6},{3,7},{4,1},{5,0},{6,3},{7,2},{8,12},{9,13},{10,... | collective-permute-start | bytes 196616 | tf_op jit(solution)/shard_map/ppermute | solution.py:271
  36.6 2.6 %collective-permute-start.16 = (bf16[16,2048]{1,0:T(8,128)(2,1)S(1)}, bf16[16,2048]{1,0:T(8,128)(2,1)S(1)}, u32[]{:S(2)}, u32[]{:S(2)}) collective-permute-start(bf16[16,2048]{1,0:T(8,128)(2,1)S(1)} %get-tuple-element.22), channel_id=1, source_target_pairs={{0,2},{1,3},{2,0},{3,1},{4,7},{5,6},{6,5},{7,4},{8,10},{9,11},{10,... | collective-permute-start | bytes 196616 | tf_op jit(solution)/shard_map/ppermute | solution.py:271
  39.4 5.6 %collective-permute-done.16.refs_0_ = bf16[16,2048]{1,0:T(8,128)(2,1)S(1)} collective-permute-done((bf16[16,2048]{1,0:T(8,128)(2,1)S(1)}, bf16[16,2048]{1,0:T(8,128)(2,1)S(1)}, u32[]{:S(2)}, u32[]{:S(2)}) %collective-permute-start.16) | collective-permute-done | bytes 65568 | tf_op jit(solution)/shard_map/ppermute | solution.py:271
  45.0 0.7 %shard_map.118 = bf16[16,2048]{1,0:T(8,128)(2,1)} custom-call(f32[16,2048]{1,0:T(8,128)S(1)} %get-tuple-element.20.own, bf16[16,2048]{1,0:T(8,128)(2,1)S(1)} %collective-permute-done.15.final, bf16[16,2048]{1,0:T(8,128)(2,1)S(1)} %collective-permute-done.16.refs_0_, bf16[16,2048]{1,0:T(8,128)(2,1)S(1)} %collective-permute-done.17.refs_1_, ...), custom_call_target="tpu_custom_call" | custom-call | tf_op jit(solution)/shard_map/pallas_call | solution.py:419
  (30 shorter events, 0.8 us)
Async XLA Ops:
  0.6 2.2 %copy-start = (bf16[16,512,256]{2,1,0:T(8,128)(2,1)S(1)}, bf16[16,512,256]{2,1,0:T(8,128)(2,1)}, u32[]{:S(2)}) copy-start(bf16[16,512,256]{2,1,0:T(8,128)(2,1)} %refs_2_.3) | copy-start | bytes 12582916
  0.6 3.5 %copy-start.1 = (bf16[16,512,256]{2,1,0:T(8,128)(2,1)S(1)}, bf16[16,512,256]{2,1,0:T(8,128)(2,1)}, u32[]{:S(2)}) copy-start(bf16[16,512,256]{2,1,0:T(8,128)(2,1)} %refs_3_.1) | copy-start | bytes 12582916
  4.1 4.2 %copy-start.4 = (bf16[16,2048]{1,0:T(8,128)(2,1)S(1)}, bf16[16,2048]{1,0:T(8,128)(2,1)}, u32[]{:S(2)}) copy-start(bf16[16,2048]{1,0:T(8,128)(2,1)} %refs_1_.2) | copy-start | bytes 196612
  4.1 14.7 %copy-start.2 = (bf16[2,4096,256]{2,1,0:T(8,128)(2,1)S(1)}, bf16[2,4096,256]{2,1,0:T(8,128)(2,1)}, u32[]{:S(2)}) copy-start(bf16[2,4096,256]{2,1,0:T(8,128)(2,1)} %refs_11_.2) | copy-start | bytes 12582916
  4.1 14.7 %copy-start.3 = (bf16[2,4096,256]{2,1,0:T(8,128)(2,1)S(1)}, bf16[2,4096,256]{2,1,0:T(8,128)(2,1)}, u32[]{:S(2)}) copy-start(bf16[2,4096,256]{2,1,0:T(8,128)(2,1)} %refs_12_.1) | copy-start | bytes 12582916
  7.7 21.7 %collective-permute-start = (f32[512,128]{1,0:T(8,128)S(1)}, f32[512,128]{1,0:T(8,128)S(1)}, u32[]{:S(2)}, u32[]{:S(2)}) collective-permute-start(f32[512,128]{1,0:T(8,128)S(1)} %get-tuple-element.14.refs_0_), channel_id=1, source_target_pairs={{0,4},{4,0},{8,12},{12,8},{16,20},{20,16},{24,28},{28,24},{1,5},{5... | collective-permute-start | bytes 786440 | tf_op jit(solution)/shard_map/ppermute | solution.py:276
  8.3 5.2 %collective-permute-start.2 = (bf16[16,2048]{1,0:T(8,128)(2,1)S(1)}, bf16[16,2048]{1,0:T(8,128)(2,1)S(1)}, u32[]{:S(2)}, u32[]{:S(2)}) collective-permute-start(bf16[16,2048]{1,0:T(8,128)(2,1)S(1)} %copy-done.4), channel_id=1, source_target_pairs={{0,8},{4,12},{8,0},{12,4},{16,24},{20,28},{24,16},{28,20},{1,9},{5... | collective-permute-start | bytes 196616 | tf_op jit(solution)/shard_map/ppermute | solution.py:276
  10.8 4.3 %collective-permute-start.4 = (bf16[16,2048]{1,0:T(8,128)(2,1)S(1)}, bf16[16,2048]{1,0:T(8,128)(2,1)S(1)}, u32[]{:S(2)}, u32[]{:S(2)}) collective-permute-start(bf16[16,2048]{1,0:T(8,128)(2,1)S(1)} %copy-done.4), channel_id=1, source_target_pairs={{0,16},{4,20},{8,24},{12,28},{16,0},{20,4},{24,8},{28,12},{1,17},{... | collective-permute-start | bytes 196616 | tf_op jit(solution)/shard_map/ppermute | solution.py:276
  12.3 5.2 %collective-permute-start.6 = (bf16[16,2048]{1,0:T(8,128)(2,1)S(1)}, bf16[16,2048]{1,0:T(8,128)(2,1)S(1)}, u32[]{:S(2)}, u32[]{:S(2)}) collective-permute-start(bf16[16,2048]{1,0:T(8,128)(2,1)S(1)} %copy-done.4), channel_id=1, source_target_pairs={{0,24},{4,28},{8,16},{12,20},{16,8},{20,12},{24,0},{28,4},{1,25},{... | collective-permute-start | bytes 196616 | tf_op jit(solution)/shard_map/ppermute | solution.py:276
  12.4 5.8 %collective-permute-start.1 = (bf16[16,2048]{1,0:T(8,128)(2,1)S(1)}, bf16[16,2048]{1,0:T(8,128)(2,1)S(1)}, u32[]{:S(2)}, u32[]{:S(2)}) collective-permute-start(bf16[16,2048]{1,0:T(8,128)(2,1)S(1)} %copy-done.4), channel_id=1, source_target_pairs={{0,4},{4,0},{8,12},{12,8},{16,20},{20,16},{24,28},{28,24},{1,5},{5... | collective-permute-start | bytes 196616 | tf_op jit(solution)/shard_map/ppermute | solution.py:276
  13.5 4.7 %collective-permute-start.3 = (bf16[16,2048]{1,0:T(8,128)(2,1)S(1)}, bf16[16,2048]{1,0:T(8,128)(2,1)S(1)}, u32[]{:S(2)}, u32[]{:S(2)}) collective-permute-start(bf16[16,2048]{1,0:T(8,128)(2,1)S(1)} %collective-permute-done.2.refs_5_), channel_id=1, source_target_pairs={{0,4},{4,0},{8,12},{12,8},{16,20},{20,16},{24,28},{28,24},{1,5},{5... | collective-permute-start | bytes 196616 | tf_op jit(solution)/shard_map/ppermute | solution.py:276
  15.1 3.1 %collective-permute-start.5 = (bf16[16,2048]{1,0:T(8,128)(2,1)S(1)}, bf16[16,2048]{1,0:T(8,128)(2,1)S(1)}, u32[]{:S(2)}, u32[]{:S(2)}) collective-permute-start(bf16[16,2048]{1,0:T(8,128)(2,1)S(1)} %collective-permute-done.4.refs_7_), channel_id=1, source_target_pairs={{0,4},{4,0},{8,12},{12,8},{16,20},{20,16},{24,28},{28,24},{1,5},{5... | collective-permute-start | bytes 196616 | tf_op jit(solution)/shard_map/ppermute | solution.py:276
  17.5 1.3 %collective-permute-start.7 = (bf16[16,2048]{1,0:T(8,128)(2,1)S(1)}, bf16[16,2048]{1,0:T(8,128)(2,1)S(1)}, u32[]{:S(2)}, u32[]{:S(2)}) collective-permute-start(bf16[16,2048]{1,0:T(8,128)(2,1)S(1)} %collective-permute-done.6.refs_9_), channel_id=1, source_target_pairs={{0,4},{4,0},{8,12},{12,8},{16,20},{20,16},{24,28},{28,24},{1,5},{5... | collective-permute-start | bytes 196616 | tf_op jit(solution)/shard_map/ppermute | solution.py:276
  22.2 3.9 %collective-permute-start.9 = (f32[48,128]{1,0:T(8,128)S(1)}, f32[48,128]{1,0:T(8,128)S(1)}, u32[]{:S(2)}, u32[]{:S(2)}) collective-permute-start(f32[48,128]{1,0:T(8,128)S(1)} %get-tuple-element.16.refs_2_), channel_id=1, source_target_pairs={{0,8},{4,12},{8,0},{12,4},{16,24},{20,28},{24,16},{28,20},{1,9},{5... | collective-permute-start | bytes 73736 | tf_op jit(solution)/shard_map/ppermute | solution.py:276
  22.8 3.8 %collective-permute-start.11 = (f32[48,128]{1,0:T(8,128)S(1)}, f32[48,128]{1,0:T(8,128)S(1)}, u32[]{:S(2)}, u32[]{:S(2)}) collective-permute-start(f32[48,128]{1,0:T(8,128)S(1)} %get-tuple-element.16.refs_2_), channel_id=1, source_target_pairs={{0,16},{4,20},{8,24},{12,28},{16,0},{20,4},{24,8},{28,12},{1,17},{... | collective-permute-start | bytes 73736 | tf_op jit(solution)/shard_map/ppermute | solution.py:276
  23.5 4.7 %collective-permute-start.13 = (f32[48,128]{1,0:T(8,128)S(1)}, f32[48,128]{1,0:T(8,128)S(1)}, u32[]{:S(2)}, u32[]{:S(2)}) collective-permute-start(f32[48,128]{1,0:T(8,128)S(1)} %get-tuple-element.16.refs_2_), channel_id=1, source_target_pairs={{0,24},{4,28},{8,16},{12,20},{16,8},{20,12},{24,0},{28,4},{1,25},{... | collective-permute-start | bytes 73736 | tf_op jit(solution)/shard_map/ppermute | solution.py:276
  25.7 2.4 %collective-permute-start.8 = (f32[48,128]{1,0:T(8,128)S(1)}, f32[48,128]{1,0:T(8,128)S(1)}, u32[]{:S(2)}, u32[]{:S(2)}) collective-permute-start(f32[48,128]{1,0:T(8,128)S(1)} %get-tuple-element.16.refs_2_), channel_id=1, source_target_pairs={{0,4},{4,0},{8,12},{12,8},{16,20},{20,16},{24,28},{28,24},{1,5},{5... | collective-permute-start | bytes 73736 | tf_op jit(solution)/shard_map/ppermute | solution.py:276
  26.1 2.1 %collective-permute-start.10 = (f32[48,128]{1,0:T(8,128)S(1)}, f32[48,128]{1,0:T(8,128)S(1)}, u32[]{:S(2)}, u32[]{:S(2)}) collective-permute-start(f32[48,128]{1,0:T(8,128)S(1)} %collective-permute-done.9.refs_4_), channel_id=1, source_target_pairs={{0,4},{4,0},{8,12},{12,8},{16,20},{20,16},{24,28},{28,24},{1,5},{5... | collective-permute-start | bytes 73736 | tf_op jit(solution)/shard_map/ppermute | solution.py:276
  26.6 1.6 %collective-permute-start.12 = (f32[48,128]{1,0:T(8,128)S(1)}, f32[48,128]{1,0:T(8,128)S(1)}, u32[]{:S(2)}, u32[]{:S(2)}) collective-permute-start(f32[48,128]{1,0:T(8,128)S(1)} %collective-permute-done.11.refs_6_), channel_id=1, source_target_pairs={{0,4},{4,0},{8,12},{12,8},{16,20},{20,16},{24,28},{28,24},{1,5},{5... | collective-permute-start | bytes 73736 | tf_op jit(solution)/shard_map/ppermute | solution.py:276
  28.2 1.2 %collective-permute-start.14 = (f32[48,128]{1,0:T(8,128)S(1)}, f32[48,128]{1,0:T(8,128)S(1)}, u32[]{:S(2)}, u32[]{:S(2)}) collective-permute-start(f32[48,128]{1,0:T(8,128)S(1)} %collective-permute-done.13.refs_8_), channel_id=1, source_target_pairs={{0,4},{4,0},{8,12},{12,8},{16,20},{20,16},{24,28},{28,24},{1,5},{5... | collective-permute-start | bytes 73736 | tf_op jit(solution)/shard_map/ppermute | solution.py:276
  33.4 5.9 %collective-permute-start.15 = (bf16[16,2048]{1,0:T(8,128)(2,1)S(1)}, bf16[16,2048]{1,0:T(8,128)(2,1)S(1)}, u32[]{:S(2)}, u32[]{:S(2)}) collective-permute-start(bf16[16,2048]{1,0:T(8,128)(2,1)S(1)} %get-tuple-element.21), channel_id=1, source_target_pairs={{4,5},{5,4},{6,7},{7,6},{12,13},{13,12},{14,15},{15,14},{20,21},{2... | collective-permute-start | bytes 196616 | tf_op jit(solution)/shard_map/ppermute | solution.py:271
  34.0 5.4 %collective-permute-start.18 = (bf16[16,2048]{1,0:T(8,128)(2,1)S(1)}, bf16[16,2048]{1,0:T(8,128)(2,1)S(1)}, u32[]{:S(2)}, u32[]{:S(2)}) collective-permute-start(bf16[16,2048]{1,0:T(8,128)(2,1)S(1)} %get-tuple-element.24), channel_id=1, source_target_pairs={{0,4},{1,5},{2,6},{3,7},{4,1},{5,0},{6,3},{7,2},{8,12},{9,13},{10,... | collective-permute-start | bytes 196616 | tf_op jit(solution)/shard_map/ppermute | solution.py:271
  36.6 8.4 %collective-permute-start.16 = (bf16[16,2048]{1,0:T(8,128)(2,1)S(1)}, bf16[16,2048]{1,0:T(8,128)(2,1)S(1)}, u32[]{:S(2)}, u32[]{:S(2)}) collective-permute-start(bf16[16,2048]{1,0:T(8,128)(2,1)S(1)} %get-tuple-element.22), channel_id=1, source_target_pairs={{0,2},{1,3},{2,0},{3,1},{4,7},{5,6},{6,5},{7,4},{8,10},{9,11},{10,... | collective-permute-start | bytes 196616 | tf_op jit(solution)/shard_map/ppermute | solution.py:271
  39.2 5.8 %collective-permute-start.17 = (bf16[16,2048]{1,0:T(8,128)(2,1)S(1)}, bf16[16,2048]{1,0:T(8,128)(2,1)S(1)}, u32[]{:S(2)}, u32[]{:S(2)}) collective-permute-start(bf16[16,2048]{1,0:T(8,128)(2,1)S(1)} %get-tuple-element.23), channel_id=1, source_target_pairs={{0,6},{1,7},{2,4},{3,5},{4,3},{5,2},{6,1},{7,0},{8,14},{9,15},{10,... | collective-permute-start | bytes 196616 | tf_op jit(solution)/shard_map/ppermute | solution.py:271

commit v3 on v2

--- a/solution.py
+++ b/solution.py
@@ -70,15 +70,14 @@
 
 
 def local_kernel(
-    lengths_in, q_in, keys, values, weight_in, _,
-    packed, q_ref, weight,
+    lengths_in, q_in, keys, values, _, __,
+    packed, q_ref,
     lengths, q_heads, scores, weights, sems,
-    *, rows, heads, kv_heads, step, columns,
+    *, rows, heads, kv_heads,
 ):
     positions = keys.shape[1]
     lengths_copy = copy_in(lengths_in, lengths, sems.at[0])
     q_copy = copy_in(q_in, q_ref, sems.at[1])
-    weight_copy = copy_in(columns_of(weight_in, step, columns), weight, sems.at[2])
     q_copy.wait()
     wide = q_ref[...].astype(f32)
     for h in range(heads):
@@ -101,29 +100,40 @@
     for r in range(rows):
         mixed = jnp.dot(weights[r], values[r], preferred_element_type=f32)
         packed[pl.ds(r * heads, heads), :] = own_columns(mixed, kv_heads)
-    weight_copy.wait()
 
 
 def step_mask(group, step):
     return 2 * step + group % 2
 
 
-def columns_of(weight, step, columns):
-    mask = step_mask(lax.axis_index("group"), step)
-    start = jnp.bitwise_xor(lax.axis_index("tp"), mask) * columns
-    return weight.at[:, pl.ds(pl.multiple_of(start, columns), columns)]
-
-
-def slot_kernel(*refs, groups, rows, heads, kv_heads, slots, chunk, ahead, columns):
+def piece_of(weight, piece, columns):
+    step, half = piece
+    place = jnp.bitwise_xor(lax.axis_index("tp"), step_mask(lax.axis_index("group"), step))
+    depth = weight.shape[0] // 2
+    return weight.at[
+        pl.ds(half * depth, depth), pl.ds(pl.multiple_of(place * columns, columns), columns)
+    ]
+
+
+def fetch(weight, pieces, targets, sems, columns):
+    return [
+        copy_in(piece_of(weight, piece, columns), target, sems.at[i])
+        for i, (piece, target) in enumerate(zip(pieces, targets))
+    ]
+
+
+def fetch_kernel(weight, _, *rest, pieces, columns):
+    for copy in fetch(weight, pieces, rest[:-1], rest[-1], columns):
+        copy.wait()
+
+
+def slot_kernel(*refs, groups, rows, heads, kv_heads, slots, chunk, pieces, columns):
     owners_in, fills_in, free = refs[:3]
     shards = refs[3 : 3 + groups]
     keys, values, weight_in = refs[3 + groups : 6 + groups]
     packed, *rest = refs[6 + groups :]
-    weight_copy = None
-    if ahead is not None:
-        weight_copy = copy_in(columns_of(weight_in, ahead, columns), rest[0], rest[-1].at[2])
-        rest = rest[1:]
-    owners, fills, q_heads, scores, sems = rest
+    owners, fills, q_heads, scores, sems, fetch_sems = rest[len(pieces) :]
+    weight_copies = fetch(weight_in, pieces, rest, fetch_sems, columns)
     copies = [
         copy_in(owners_in, owners, sems.at[0]),
         copy_in(fills_in, fills, sems.at[1]),
@@ -169,47 +179,47 @@
         stats = jnp.where(lane == slots + s, total, stats)
         stats = jnp.where(lane == 2 * slots + s, owners[s].astype(f32), stats)
     packed[slots * heads :, :] = stats
-    if weight_copy is not None:
-        weight_copy.wait()
-
-
-def project(x, weight, same, other, chunk, own=None):
-    rows = x.shape[0] // 2
+    for copy in weight_copies:
+        copy.wait()
+
+
+def project(x, halves, same, other, chunk, own=None):
+    rows, depth = x.shape[0] // 2, x.shape[1] // 2
     for c in range(0, same.shape[1], chunk):
-        product = jnp.dot(x, weight[:, c : c + chunk], preferred_element_type=f32)
-        same[:, c : c + chunk] = product[:rows].astype(same.dtype)
-        other[:, c : c + chunk] = product[rows:].astype(other.dtype)
+        at = slice(c, c + chunk)
+        product = jnp.dot(
+            x[:, :depth], halves[0][:, at], preferred_element_type=f32
+        ) + jnp.dot(x[:, depth:], halves[1][:, at], preferred_element_type=f32)
+        same[:, at] = product[:rows].astype(same.dtype)
+        other[:, at] = product[rows:].astype(other.dtype)
         if own is not None:
-            own[:, c : c + chunk] = product[:rows]
-
-
-def combine_kernel(*refs, groups, rows, heads, slots, ahead, last, columns, chunk):
-    local = refs[:2]
-    parts = refs[2 : 2 + groups]
-    weight, weight_in, x_ref, free_total, same, other = refs[2 + groups : 8 + groups]
-    rest = list(refs[8 + groups :])
+            own[:, at] = product[:rows]
+
+
+def combine_kernel(*refs, rows, heads, slots, pieces, last, columns, chunk):
+    local, gathered, halves = refs[:2], refs[2:4], refs[4:6]
+    weight_in, x_ref, free_total, same, other, *rest = refs[6:]
     own = rest.pop(0) if last else None
-    copy = None
-    if ahead is not None:
-        copy = copy_in(columns_of(weight_in, ahead, columns), rest.pop(0), rest.pop())
-    mixed, high, total = rest
-    flat = rows * heads
+    mixed, high, total, sems = rest[len(pieces) :]
+    copies = fetch(weight_in, pieces, rest, sems, columns)
+    flat, each = rows * heads, (slots + 1) * heads
     me = lax.axis_index("group")
     first, second = me * rows, jnp.bitwise_xor(me, 1) * rows
     free = jnp.zeros((heads, LANES), f32)
     found = []
-    for k in range(groups):
-        stats = parts[k][slots * heads :, :]
-        free = free + stats
-        for s in range(slots):
-            owner = stats[0, 2 * slots + s].astype(jnp.int32)
-            found.append((k, s, owner))
+    for part in gathered:
+        for k in range(0, part.shape[0], each):
+            stats = part[k + slots * heads : k + each, :]
+            free = free + stats
+            for s in range(slots):
+                owner = stats[0, 2 * slots + s].astype(jnp.int32)
+                found.append((part, k, s, stats, owner))
     free_total[0] = free[0, 3 * slots].astype(jnp.int32)
     for i in range(2):
         stats = local[i][flat:, :]
         high[i * flat : (i + 1) * flat, :] = jnp.broadcast_to(stats[:, 0:1], (flat, LANES))
     slot_stats = []
-    for k, s, owner in found:
+    for part, k, s, stats, owner in found:
         in_first = (owner >= first) & (owner < first + rows)
         in_second = (owner >= second) & (owner < second + rows)
         row = jnp.where(
@@ -217,10 +227,9 @@
         )
         mine = in_first | in_second
         at = pl.ds(pl.multiple_of(row * heads, heads), heads)
-        stats = parts[k][slots * heads :, :]
         slot_high = jnp.broadcast_to(stats[:, s : s + 1], (heads, LANES))
         slot_total = jnp.broadcast_to(stats[:, slots + s : slots + s + 1], (heads, LANES))
-        slot_stats.append((mine, at, slot_high, slot_total))
+        slot_stats.append((part, k + s * heads, mine, at, slot_high, slot_total))
         high[at, :] = jnp.maximum(high[at, :], jnp.where(mine, slot_high, far_below))
     for i in range(2):
         at = slice(i * flat, (i + 1) * flat)
@@ -228,28 +237,27 @@
         keep = jnp.exp(jnp.broadcast_to(stats[:, 0:1], (flat, LANES)) - high[at, :])
         mixed[at, :] = keep * local[i][:flat, :]
         total[at, :] = keep * jnp.broadcast_to(stats[:, 1:2], (flat, LANES))
-    for (k, s, _), (mine, at, slot_high, slot_total) in zip(found, slot_stats):
+    for part, k, mine, at, slot_high, slot_total in slot_stats:
         add = jnp.where(mine, jnp.exp(jnp.minimum(slot_high - high[at, :], 0.0)), 0.0)
-        mixed[at, :] = mixed[at, :] + add * parts[k][s * heads : (s + 1) * heads, :]
+        mixed[at, :] = mixed[at, :] + add * part[k : k + heads, :]
         total[at, :] = total[at, :] + add * slot_total
     mixed[...] = mixed[...] / total[...]
     for h in range(heads):
         x_ref[:, h * HEAD_DIM : (h + 1) * HEAD_DIM] = mixed[
             pl.ds(h, 2 * rows, stride=heads), :
         ].astype(bf16)
-    project(x_ref[...], weight, same, other, chunk, own)
-    if copy is not None:
+    project(x_ref[...], halves, same, other, chunk, own)
+    for copy in copies:
         copy.wait()
 
 
-def project_kernel(x_ref, weight, weight_in, same, other, *rest, ahead, last, columns, chunk):
-    rest = list(rest)
+def project_kernel(x_ref, *refs, pieces, last, columns, chunk):
+    halves = refs[:2]
+    weight_in, same, other, *rest = refs[2:]
     own = rest.pop(0) if last else None
-    copy = None
-    if ahead is not None:
-        copy = copy_in(columns_of(weight_in, ahead, columns), *rest)
-    project(x_ref[...], weight, same, other, chunk, own)
-    if copy is not None:
+    copies = fetch(weight_in, pieces, rest, rest[-1], columns)
+    project(x_ref[...], halves, same, other, chunk, own)
+    for copy in copies:
         copy.wait()
 
 
@@ -274,6 +282,10 @@
 def swap(value, axis, mask):
     size = lax.axis_size(axis)
     return lax.ppermute(value, axis, [(i, i ^ mask) for i in range(size)])
+
+
+def pair_masks(groups):
+    return [1 << i for i in range(1, (groups - 1).bit_length())]
 
 
 def gather_group(value):
@@ -317,21 +329,24 @@
     copies = pltpu.SemaphoreType.DMA
 
     order = list(range(tp // 2 - 1, -1, -1))
-    held = jax.ShapeDtypeStruct((width, columns), out_weight.dtype)
-    moved = 2 * width * columns
+    pieces = [(step, half) for step in order for half in range(2)]
+    held = jax.ShapeDtypeStruct((width // 2, columns), out_weight.dtype)
+    piece_bytes = width * columns
     weights = {}
+
+    def take(count):
+        taken = pieces[:count]
+        del pieces[:count]
+        return taken
 
     token = call(open_kernel, jax.ShapeDtypeStruct((8, LANES), f32), [HBM], vmem=1 << 20)(
         out_weight
     )
-    local, own_queries, weights[order[0]] = call(
-        lambda *refs: local_kernel(
-            *refs, kv_heads=kv_heads, step=order[0], columns=columns, **sizes
-        ),
+    local, own_queries = call(
+        lambda *refs: local_kernel(*refs, kv_heads=kv_heads, **sizes),
         [
             jax.ShapeDtypeStruct((2 * rows * heads, LANES), f32),
             jax.ShapeDtypeStruct(queries.shape, queries.dtype),
-            held,
         ],
         [HBM, HBM, VMEM, VMEM, HBM, VMEM],
         scratch=[
@@ -339,80 +354,94 @@
             pltpu.VMEM((rows * heads, HEAD_DIM), f32),
             pltpu.VMEM((rows * heads, cache_keys.shape[1]), f32),
             pltpu.VMEM((rows, heads, cache_keys.shape[1]), bf16),
-            copies((3,)),
+            copies((2,)),
         ],
-        moved=moved,
+        moved=2 * (cache_keys.size + cache_values.size),
         vmem=4 << 20,
     )(row_lengths, queries, cache_keys, cache_values, out_weight, token)
     shards[0] = own_queries
     pair_local = swap(local, "group", 1)
 
-    ahead = order[1] if len(order) > 1 else None
+    taken = take(1)
     packed, *more = call(
-        lambda *refs: slot_kernel(
+        lambda *refs, taken=taken: slot_kernel(
             *refs,
             groups=groups,
             kv_heads=kv_heads,
             slots=slots,
             chunk=math.gcd(positions, 512),
-            ahead=ahead,
+            pieces=taken,
             columns=columns,
             **sizes,
         ),
-        [jax.ShapeDtypeStruct(((slots + 1) * heads, LANES), f32)] + [held] * (ahead is not None),
+        [jax.ShapeDtypeStruct(((slots + 1) * heads, LANES), f32)] + [held] * len(taken),
         [HBM] * 2 + [SMEM] + [VMEM] * (groups + 2) + [HBM],
         scratch=[
             pltpu.SMEM(slot_owner.shape, jnp.int32),
             pltpu.SMEM(slot_fill.shape, jnp.int32),
             pltpu.VMEM((slots * heads, HEAD_DIM), f32),
             pltpu.VMEM((slots * heads, positions), f32),
-            copies((3,)),
+            copies((2,)),
+            copies((1,)),
         ],
-        moved=moved,
+        moved=2 * (pool_keys.size + pool_values.size),
         vmem=4 << 20,
     )(slot_owner, slot_fill, free_counts, *shards, pool_keys, pool_values, out_weight)
-    if more:
-        weights[ahead] = more[0]
-
-    far = gather_group(packed)
+    weights.update(zip(taken, more))
+
+    gathered = packed
+    for mask in pair_masks(groups):
+        other = swap(gathered, "group", mask)
+        taken = take(1)
+        if taken:
+            more = call(
+                lambda *refs, taken=taken: fetch_kernel(*refs, pieces=taken, columns=columns),
+                [held] * len(taken),
+                [HBM, pl.BlockSpec(memory_space=pl.ANY)],
+                scratch=[copies((1,))],
+                moved=piece_bytes,
+                vmem=1 << 20,
+            )(out_weight, packed)
+            weights.update(zip(taken, more))
+        gathered = jnp.concatenate([gathered, other], axis=0)
+    pair_gathered = swap(gathered, "group", 1)
 
     block = jax.ShapeDtypeStruct((rows, columns), bf16)
     whole = jax.ShapeDtypeStruct((rows, columns), f32)
     received = []
     for i, step in enumerate(order):
         last = step == 0
-        ahead = order[i + 2] if i + 2 < len(order) else None
-        outs = [block] * 2 + [whole] * last + [held] * (ahead is not None)
-        settings = dict(ahead=ahead, last=last, columns=columns, chunk=chunk)
+        taken = take(max(0, len(pieces) - 2 * (len(order) - 2 - i)))
+        outs = [block] * 2 + [whole] * last + [held] * len(taken)
+        settings = dict(pieces=taken, last=last, columns=columns, chunk=chunk)
+        halves = [weights[step, half] for half in range(2)]
+        moved = piece_bytes * max(2, len(taken))
         if i == 0:
             x, free_total, same, other, *more = call(
-                lambda *refs: combine_kernel(
-                    *refs, groups=groups, slots=slots, **settings, **sizes
-                ),
+                lambda *refs: combine_kernel(*refs, slots=slots, **settings, **sizes),
                 [
                     jax.ShapeDtypeStruct((2 * rows, width), bf16),
                     jax.ShapeDtypeStruct((1,), jnp.int32),
                 ]
                 + outs,
-                [VMEM] * (2 + groups + 1) + [HBM],
+                [VMEM] * 6 + [HBM],
                 out_specs=[VMEM, SMEM] + [VMEM] * len(outs),
                 scratch=[pltpu.VMEM((2 * rows * heads, LANES), f32)] * 3
-                + [copies] * (ahead is not None),
+                + [copies((max(1, len(taken)),))],
                 moved=moved,
-            )(local, pair_local, *far, weights[step], out_weight)
+            )(local, pair_local, gathered, pair_gathered, *halves, out_weight)
         else:
             same, other, *more = call(
                 lambda *refs, settings=settings: project_kernel(*refs, **settings),
                 outs,
-                [VMEM] * 2 + [HBM],
-                scratch=[copies] * (ahead is not None),
+                [VMEM] * 3 + [HBM],
+                scratch=[copies((max(1, len(taken)),))],
                 moved=moved,
                 vmem=4 << 20,
-            )(x, weights[step], out_weight)
+            )(x, *halves, out_weight)
         if last:
             own = more.pop(0)
-        if ahead is not None:
-            weights[ahead] = more.pop(0)
+        weights.update(zip(taken, more))
         received.append(send_block(same, step, 0))
         received.append(send_block(other, step, 1))
     final = received.pop(-2)

time: 46.2 us -> 49.5 us (1.071)
  Pallas kernels: 11.7 us -> 16.9 us
  local copies, waits for them, and re-layouts: 3.45 us -> 0.03 us
  waiting for transfers between devices: 15 us -> 17.9 us
  starting transfers between devices: 14.3 us -> 12.6 us
    pallas_call x3 -> x5, Pallas kernels: 9.44 us -> 14.7 us  [the longest x1 4.61 us: step(): call(lambda *refs: combine_kernel(*refs, slots=slots, **settings, **sizes...]
    unnamed x10, local copies, waits for them, and re-layouts: 3.45 us -> 0.03 us
    ppermute x15 -> x11, waiting for transfers between devices: 9.15 us -> 12.2 us  [swap(): return lax.ppermute(value, axis, [(i, i ^ mask) for i in range(size)])]
    ppermute x15 -> x11, starting transfers between devices: 8.41 us -> 6.24 us  [swap(): return lax.ppermute(value, axis, [(i, i ^ mask) for i in range(size)])]
  transfers between devices with their start and end apart: 19 -> 15, of which waited for: 10 -> 6; matrix products, arithmetic and copies ran while one was open for 0% -> 0% of each run, Pallas kernels for 7% -> 21%
where the time goes in v3:
time: 49.5 us; the launch traced here: 48.9 us
  waiting for transfers between devices  17.9 us (36%)
  Pallas kernels  16.9 us (34%)
  starting transfers between devices  12.6 us (25%)
  between operations  1.46 us (3%)
    ppermute x11, waiting for transfers between devices, swap(): return lax.ppermute(value, axis, [(i, i ^ mask) for i in range(size)])  12.2 us
    ppermute x4, starting transfers between devices, send_block(): return lax.ppermute(value, ('group', 'tp'), pairs)  6.34 us
    ppermute x11, starting transfers between devices, swap(): return lax.ppermute(value, axis, [(i, i ^ mask) for i in range(size)])  6.24 us
    ppermute x4, waiting for transfers between devices, send_block(): return lax.ppermute(value, ('group', 'tp'), pairs)  5.68 us
    pallas_call x1, Pallas kernels, step(): call(lambda *refs: combine_kernel(*refs, slots=slots, **settings, **sizes...  4.61 us
    pallas_call x2, Pallas kernels, step(): call(lambda *refs, taken=taken: fetch_kernel(*refs, pieces=taken, columns...  4.43 us
    pallas_call x1, Pallas kernels, step(): call(lambda *refs: local_kernel(*refs, kv_heads=kv_heads, **sizes), [jax....  2.84 us
    pallas_call x1, Pallas kernels, step(): call(lambda *refs, taken=taken: slot_kernel(*refs, groups=groups, kv_head...  2.81 us
  transfers between devices with their start and end apart: 15, of which 6 were waited for; matrix products, arithmetic and copies ran while one was open for 0% of the time, Pallas kernels for 21%

profile of v3, /device:TPU:0, one launch (start us, length us, event | category | flops | bytes accessed | tf_op | source)
XLA Modules:
  0.0 48.9 jit_solution(9776729564735193809)
XLA Ops:
  0.6 3.0 %collective-permute-start.2 = (bf16[16,2048]{1,0:T(8,128)(2,1)}, bf16[16,2048]{1,0:T(8,128)(2,1)S(1)}, u32[]{:S(2)}, u32[]{:S(2)}) collective-permute-start(bf16[16,2048]{1,0:T(8,128)(2,1)} %refs_1_.2), channel_id=1, source_target_pairs={{0,8},{4,12},{8,0},{12,4},{16,24},{20,28},{24,16},{28,20},{1,9},{5... | collective-permute-start | bytes 196616 | tf_op jit(solution)/shard_map/ppermute | solution.py:284
  3.7 1.5 %collective-permute-start.4 = (bf16[16,2048]{1,0:T(8,128)(2,1)}, bf16[16,2048]{1,0:T(8,128)(2,1)S(1)}, u32[]{:S(2)}, u32[]{:S(2)}) collective-permute-start(bf16[16,2048]{1,0:T(8,128)(2,1)} %refs_1_.2), channel_id=1, source_target_pairs={{0,16},{4,20},{8,24},{12,28},{16,0},{20,4},{24,8},{28,12},{1,17},{... | collective-permute-start | bytes 196616 | tf_op jit(solution)/shard_map/ppermute | solution.py:284
  5.2 0.0 collective-permute-start.6
  5.2 1.1 %collective-permute-done.2.refs_5_ = bf16[16,2048]{1,0:T(8,128)(2,1)S(1)} collective-permute-done((bf16[16,2048]{1,0:T(8,128)(2,1)}, bf16[16,2048]{1,0:T(8,128)(2,1)S(1)}, u32[]{:S(2)}, u32[]{:S(2)}) %collective-permute-start.2) | collective-permute-done | bytes 65568 | tf_op jit(solution)/shard_map/ppermute | solution.py:284
  6.3 1.8 %collective-permute-done.4.refs_7_ = bf16[16,2048]{1,0:T(8,128)(2,1)S(1)} collective-permute-done((bf16[16,2048]{1,0:T(8,128)(2,1)}, bf16[16,2048]{1,0:T(8,128)(2,1)S(1)}, u32[]{:S(2)}, u32[]{:S(2)}) %collective-permute-start.4) | collective-permute-done | bytes 65568 | tf_op jit(solution)/shard_map/ppermute | solution.py:284
  8.2 2.4 %collective-permute-done.6.refs_9_ = bf16[16,2048]{1,0:T(8,128)(2,1)S(1)} collective-permute-done((bf16[16,2048]{1,0:T(8,128)(2,1)}, bf16[16,2048]{1,0:T(8,128)(2,1)S(1)}, u32[]{:S(2)}, u32[]{:S(2)}) %collective-permute-start.6) | collective-permute-done | bytes 65568 | tf_op jit(solution)/shard_map/ppermute | solution.py:284
  10.6 0.0 copy-start.2
  10.6 2.8 %shard_map.114 = (f32[512,128]{1,0:T(8,128)S(1)}, bf16[16,2048]{1,0:T(8,128)(2,1)S(1)}) custom-call(s32[16]{0:T(128)} %refs_0_.4, bf16[16,2048]{1,0:T(8,128)(2,1)} %refs_1_.2, bf16[16,512,256]{2,1,0:T(8,128)(2,1)S(1)} %copy-done, bf16[16,512,256]{2,1,0:T(8,128)(2,1)S(1)} %copy-done.1, bf16[2048,8192]{1,0:T(8,128)(2,1)} %refs_3_.3, ...), custom_call_target="tpu_custom_call" | custom-call | bytes 8388608 | tf_op jit(solution)/shard_map/pallas_call | solution.py:345
  13.5 0.6 %collective-permute-start = (f32[512,128]{1,0:T(8,128)S(1)}, f32[512,128]{1,0:T(8,128)S(1)}, u32[]{:S(2)}, u32[]{:S(2)}) collective-permute-start(f32[512,128]{1,0:T(8,128)S(1)} %get-tuple-element.14.refs_0_), channel_id=1, source_target_pairs={{0,4},{4,0},{8,12},{12,8},{16,20},{20,16},{24,28},{28,24},{1,5},{5... | collective-permute-start | bytes 786440 | tf_op jit(solution)/shard_map/ppermute | solution.py:284
  14.7 2.8 %shard_map.115 = (f32[48,128]{1,0:T(8,128)S(1)}, bf16[1024,2048]{1,0:T(8,128)(2,1)S(1)}) custom-call(s32[2]{0:T(128)} %refs_0_.5, s32[2]{0:T(128)} %refs_1_.3, s32[1]{0:T(128)S(6)} %copy.14.refs_2_, bf16[16,2048]{1,0:T(8,128)(2,1)S(1)} %get-tuple-element.15.refs_3_, bf16[16,2048]{1,0:T(8,128)(2,1)S(1)} %collective-permute-done.1.refs_4_, ...), custom_call_target="tpu_custom_call" | custom-call | bytes 8388608 | tf_op jit(solution)/shard_map/pallas_call | solution.py:366
  17.6 0.6 %collective-permute-start.8 = (f32[48,128]{1,0:T(8,128)S(1)}, f32[48,128]{1,0:T(8,128)S(1)}, u32[]{:S(2)}, u32[]{:S(2)}) collective-permute-start(f32[48,128]{1,0:T(8,128)S(1)} %get-tuple-element.16.refs_1_), channel_id=1, source_target_pairs={{0,8},{4,12},{8,0},{12,4},{16,24},{20,28},{24,16},{28,20},{1,9},{5... | collective-permute-start | bytes 73736 | tf_op jit(solution)/shard_map/ppermute | solution.py:284
  18.2 3.3 %collective-permute-done.8 = f32[48,128]{1,0:T(8,128)S(1)} collective-permute-done((f32[48,128]{1,0:T(8,128)S(1)}, f32[48,128]{1,0:T(8,128)S(1)}, u32[]{:S(2)}, u32[]{:S(2)}) %collective-permute-start.8) | collective-permute-done | bytes 24608 | tf_op jit(solution)/shard_map/ppermute | solution.py:284
  21.5 0.5 %collective-permute-start.9 = (f32[96,128]{1,0:T(8,128)S(1)}, f32[96,128]{1,0:T(8,128)S(1)}, u32[]{:S(2)}, u32[]{:S(2)}) collective-permute-start(f32[96,128]{1,0:T(8,128)S(1)} %pad_maximum_fusion), channel_id=1, source_target_pairs={{0,16},{4,20},{8,24},{12,28},{16,0},{20,4},{24,8},{28,12},{1,17},{... | collective-permute-start | bytes 147464 | tf_op jit(solution)/shard_map/ppermute | solution.py:284
  22.0 3.6 %collective-permute-done.9 = f32[96,128]{1,0:T(8,128)S(1)} collective-permute-done((f32[96,128]{1,0:T(8,128)S(1)}, f32[96,128]{1,0:T(8,128)S(1)}, u32[]{:S(2)}, u32[]{:S(2)}) %collective-permute-start.9) | collective-permute-done | bytes 49184 | tf_op jit(solution)/shard_map/ppermute | solution.py:284
  25.6 2.2 %shard_map.116.refs_5_ = bf16[1024,2048]{1,0:T(8,128)(2,1)S(1)} custom-call(bf16[2048,8192]{1,0:T(8,128)(2,1)} %refs_3_.3, f32[48,128]{1,0:T(8,128)S(1)} %get-tuple-element.16.refs_1_), custom_call_target="tpu_custom_call" | custom-call | bytes 4194304 | tf_op jit(solution)/shard_map/pallas_call | solution.py:397
  27.8 2.2 %shard_map.118.refs_1_ = bf16[1024,2048]{1,0:T(8,128)(2,1)S(1)} custom-call(bf16[2048,8192]{1,0:T(8,128)(2,1)} %refs_3_.3, f32[48,128]{1,0:T(8,128)S(1)} %get-tuple-element.16.refs_1_), custom_call_target="tpu_custom_call" | custom-call | bytes 4194304 | tf_op jit(solution)/shard_map/pallas_call | solution.py:397
  30.0 4.6 %shard_map.117 = (bf16[32,2048]{1,0:T(8,128)(2,1)S(1)}, s32[1]{0:T(128)}, bf16[16,2048]{1,0:T(8,128)(2,1)S(1)}, bf16[16,2048]{1,0:T(8,128)(2,1)S(1)}, bf16[1024,2048]{1,0:T(8,128)(2,1)S(1)}) custom-call(f32[512,128]{1,0:T(8,128)S(1)} %get-tuple-element.14.refs_0_, f32[512,128]{1,0:T(8,128)S(1)} %collective-permute-done.refs_1_, ...), custom_call_target="tpu_custom_call" | custom-call | bytes 8388608 | tf_op jit(solution)/shard_map/pallas_call | solution.py:420
  34.6 1.6 %shard_map.119 = (bf16[16,2048]{1,0:T(8,128)(2,1)S(1)}, bf16[16,2048]{1,0:T(8,128)(2,1)S(1)}, f32[16,2048]{1,0:T(8,128)S(1)}) custom-call(bf16[32,2048]{1,0:T(8,128)(2,1)S(1)} %get-tuple-element.18.refs_0_, bf16[1024,2048]{1,0:T(8,128)(2,1)S(1)} %shard_map.118.refs_1_, bf16[1024,2048]{1,0:T(8,128)(2,1)S(1)} %get-tuple-element.19.refs_2_, ...), custom_call_target="tpu_custom_call" | custom-call | bytes 8388608 | tf_op jit(solution)/shard_map/pallas_call | solution.py:434
  36.2 0.7 %collective-permute-start.11 = (bf16[16,2048]{1,0:T(8,128)(2,1)S(1)}, bf16[16,2048]{1,0:T(8,128)(2,1)S(1)}, u32[]{:S(2)}, u32[]{:S(2)}) collective-permute-start(bf16[16,2048]{1,0:T(8,128)(2,1)S(1)} %get-tuple-element.21), channel_id=1, source_target_pairs={{4,5},{5,4},{6,7},{7,6},{12,13},{13,12},{14,15},{15,14},{20,21},{2... | collective-permute-start | bytes 196616 | tf_op jit(solution)/shard_map/ppermute | solution.py:279
  36.9 3.1 %collective-permute-start.14 = (bf16[16,2048]{1,0:T(8,128)(2,1)S(1)}, bf16[16,2048]{1,0:T(8,128)(2,1)S(1)}, u32[]{:S(2)}, u32[]{:S(2)}) collective-permute-start(bf16[16,2048]{1,0:T(8,128)(2,1)S(1)} %get-tuple-element.24), channel_id=1, source_target_pairs={{0,4},{1,5},{2,6},{3,7},{4,1},{5,0},{6,3},{7,2},{8,12},{9,13},{10,... | collective-permute-start | bytes 196616 | tf_op jit(solution)/shard_map/ppermute | solution.py:279
  40.0 2.6 %collective-permute-start.12 = (bf16[16,2048]{1,0:T(8,128)(2,1)S(1)}, bf16[16,2048]{1,0:T(8,128)(2,1)S(1)}, u32[]{:S(2)}, u32[]{:S(2)}) collective-permute-start(bf16[16,2048]{1,0:T(8,128)(2,1)S(1)} %get-tuple-element.22), channel_id=1, source_target_pairs={{0,2},{1,3},{2,0},{3,1},{4,7},{5,6},{6,5},{7,4},{8,10},{9,11},{10,... | collective-permute-start | bytes 196616 | tf_op jit(solution)/shard_map/ppermute | solution.py:279
  42.6 0.0 collective-permute-done.14.refs_2_
  42.6 5.6 %collective-permute-done.12.refs_0_ = bf16[16,2048]{1,0:T(8,128)(2,1)S(1)} collective-permute-done((bf16[16,2048]{1,0:T(8,128)(2,1)S(1)}, bf16[16,2048]{1,0:T(8,128)(2,1)S(1)}, u32[]{:S(2)}, u32[]{:S(2)}) %collective-permute-start.12) | collective-permute-done | bytes 65568 | tf_op jit(solution)/shard_map/ppermute | solution.py:279
  48.2 0.7 %shard_map.120 = bf16[16,2048]{1,0:T(8,128)(2,1)} custom-call(f32[16,2048]{1,0:T(8,128)S(1)} %get-tuple-element.20.own, bf16[16,2048]{1,0:T(8,128)(2,1)S(1)} %collective-permute-done.11.final, bf16[16,2048]{1,0:T(8,128)(2,1)S(1)} %collective-permute-done.12.refs_0_, bf16[16,2048]{1,0:T(8,128)(2,1)S(1)} %collective-permute-done.13.refs_1_, ...), custom_call_target="tpu_custom_call" | custom-call | tf_op jit(solution)/shard_map/pallas_call | solution.py:448
  (26 shorter events, 0.1 us)
Async XLA Ops:
  0.6 10.0 %copy-start = (bf16[16,512,256]{2,1,0:T(8,128)(2,1)S(1)}, bf16[16,512,256]{2,1,0:T(8,128)(2,1)}, u32[]{:S(2)}) copy-start(bf16[16,512,256]{2,1,0:T(8,128)(2,1)} %refs_2_.2) | copy-start | bytes 12582916
  0.6 10.0 %copy-start.1 = (bf16[16,512,256]{2,1,0:T(8,128)(2,1)S(1)}, bf16[16,512,256]{2,1,0:T(8,128)(2,1)}, u32[]{:S(2)}) copy-start(bf16[16,512,256]{2,1,0:T(8,128)(2,1)} %refs_3_.2) | copy-start | bytes 12582916
  0.6 5.7 %collective-permute-start.2 = (bf16[16,2048]{1,0:T(8,128)(2,1)}, bf16[16,2048]{1,0:T(8,128)(2,1)S(1)}, u32[]{:S(2)}, u32[]{:S(2)}) collective-permute-start(bf16[16,2048]{1,0:T(8,128)(2,1)} %refs_1_.2), channel_id=1, source_target_pairs={{0,8},{4,12},{8,0},{12,4},{16,24},{20,28},{24,16},{28,20},{1,9},{5... | collective-permute-start | bytes 196616 | tf_op jit(solution)/shard_map/ppermute | solution.py:284
  3.7 4.5 %collective-permute-start.4 = (bf16[16,2048]{1,0:T(8,128)(2,1)}, bf16[16,2048]{1,0:T(8,128)(2,1)S(1)}, u32[]{:S(2)}, u32[]{:S(2)}) collective-permute-start(bf16[16,2048]{1,0:T(8,128)(2,1)} %refs_1_.2), channel_id=1, source_target_pairs={{0,16},{4,20},{8,24},{12,28},{16,0},{20,4},{24,8},{28,12},{1,17},{... | collective-permute-start | bytes 196616 | tf_op jit(solution)/shard_map/ppermute | solution.py:284
  5.2 5.4 %collective-permute-start.6 = (bf16[16,2048]{1,0:T(8,128)(2,1)}, bf16[16,2048]{1,0:T(8,128)(2,1)S(1)}, u32[]{:S(2)}, u32[]{:S(2)}) collective-permute-start(bf16[16,2048]{1,0:T(8,128)(2,1)} %refs_1_.2), channel_id=1, source_target_pairs={{0,24},{4,28},{8,16},{12,20},{16,8},{20,12},{24,0},{28,4},{1,25},{... | collective-permute-start | bytes 196616 | tf_op jit(solution)/shard_map/ppermute | solution.py:284
  5.2 9.5 %collective-permute-start.1 = (bf16[16,2048]{1,0:T(8,128)(2,1)}, bf16[16,2048]{1,0:T(8,128)(2,1)S(1)}, u32[]{:S(2)}, u32[]{:S(2)}) collective-permute-start(bf16[16,2048]{1,0:T(8,128)(2,1)} %refs_1_.2), channel_id=1, source_target_pairs={{0,4},{4,0},{8,12},{12,8},{16,20},{20,16},{24,28},{28,24},{1,5},{5... | collective-permute-start | bytes 196616 | tf_op jit(solution)/shard_map/ppermute | solution.py:284
  6.3 8.4 %collective-permute-start.3 = (bf16[16,2048]{1,0:T(8,128)(2,1)S(1)}, bf16[16,2048]{1,0:T(8,128)(2,1)S(1)}, u32[]{:S(2)}, u32[]{:S(2)}) collective-permute-start(bf16[16,2048]{1,0:T(8,128)(2,1)S(1)} %collective-permute-done.2.refs_5_), channel_id=1, source_target_pairs={{0,4},{4,0},{8,12},{12,8},{16,20},{20,16},{24,28},{28,24},{1,5},{5... | collective-permute-start | bytes 196616 | tf_op jit(solution)/shard_map/ppermute | solution.py:284
  8.2 6.5 %collective-permute-start.5 = (bf16[16,2048]{1,0:T(8,128)(2,1)S(1)}, bf16[16,2048]{1,0:T(8,128)(2,1)S(1)}, u32[]{:S(2)}, u32[]{:S(2)}) collective-permute-start(bf16[16,2048]{1,0:T(8,128)(2,1)S(1)} %collective-permute-done.4.refs_7_), channel_id=1, source_target_pairs={{0,4},{4,0},{8,12},{12,8},{16,20},{20,16},{24,28},{28,24},{1,5},{5... | collective-permute-start | bytes 196616 | tf_op jit(solution)/shard_map/ppermute | solution.py:284
  10.6 4.1 %collective-permute-start.7 = (bf16[16,2048]{1,0:T(8,128)(2,1)S(1)}, bf16[16,2048]{1,0:T(8,128)(2,1)S(1)}, u32[]{:S(2)}, u32[]{:S(2)}) collective-permute-start(bf16[16,2048]{1,0:T(8,128)(2,1)S(1)} %collective-permute-done.6.refs_9_), channel_id=1, source_target_pairs={{0,4},{4,0},{8,12},{12,8},{16,20},{20,16},{24,28},{28,24},{1,5},{5... | collective-permute-start | bytes 196616 | tf_op jit(solution)/shard_map/ppermute | solution.py:284
  10.6 4.1 %copy-start.2 = (bf16[2,4096,256]{2,1,0:T(8,128)(2,1)S(1)}, bf16[2,4096,256]{2,1,0:T(8,128)(2,1)}, u32[]{:S(2)}) copy-start(bf16[2,4096,256]{2,1,0:T(8,128)(2,1)} %refs_11_.1) | copy-start | bytes 12582916
  10.6 4.1 %copy-start.3 = (bf16[2,4096,256]{2,1,0:T(8,128)(2,1)S(1)}, bf16[2,4096,256]{2,1,0:T(8,128)(2,1)}, u32[]{:S(2)}) copy-start(bf16[2,4096,256]{2,1,0:T(8,128)(2,1)} %refs_12_.1) | copy-start | bytes 12582916
  13.5 16.5 %collective-permute-start = (f32[512,128]{1,0:T(8,128)S(1)}, f32[512,128]{1,0:T(8,128)S(1)}, u32[]{:S(2)}, u32[]{:S(2)}) collective-permute-start(f32[512,128]{1,0:T(8,128)S(1)} %get-tuple-element.14.refs_0_), channel_id=1, source_target_pairs={{0,4},{4,0},{8,12},{12,8},{16,20},{20,16},{24,28},{28,24},{1,5},{5... | collective-permute-start | bytes 786440 | tf_op jit(solution)/shard_map/ppermute | solution.py:284
  17.6 3.9 %collective-permute-start.8 = (f32[48,128]{1,0:T(8,128)S(1)}, f32[48,128]{1,0:T(8,128)S(1)}, u32[]{:S(2)}, u32[]{:S(2)}) collective-permute-start(f32[48,128]{1,0:T(8,128)S(1)} %get-tuple-element.16.refs_1_), channel_id=1, source_target_pairs={{0,8},{4,12},{8,0},{12,4},{16,24},{20,28},{24,16},{28,20},{1,9},{5... | collective-permute-start | bytes 73736 | tf_op jit(solution)/shard_map/ppermute | solution.py:284
  21.5 4.1 %collective-permute-start.9 = (f32[96,128]{1,0:T(8,128)S(1)}, f32[96,128]{1,0:T(8,128)S(1)}, u32[]{:S(2)}, u32[]{:S(2)}) collective-permute-start(f32[96,128]{1,0:T(8,128)S(1)} %pad_maximum_fusion), channel_id=1, source_target_pairs={{0,16},{4,20},{8,24},{12,28},{16,0},{20,4},{24,8},{28,12},{1,17},{... | collective-permute-start | bytes 147464 | tf_op jit(solution)/shard_map/ppermute | solution.py:284
  25.6 4.5 %collective-permute-start.10 = (f32[192,128]{1,0:T(8,128)S(1)}, f32[192,128]{1,0:T(8,128)S(1)}, u32[]{:S(2)}, u32[]{:S(2)}) collective-permute-start(f32[192,128]{1,0:T(8,128)S(1)} %constant_dynamic-update-slice_fusion.refs_2_), channel_id=1, source_target_pairs={{0,4},{4,0},{8,12},{12,8},{16,20},{20,16},{24,28},{28,24},{1,5},{5... | collective-permute-start | bytes 294920 | tf_op jit(solution)/shard_map/ppermute | solution.py:284
  36.2 6.3 %collective-permute-start.11 = (bf16[16,2048]{1,0:T(8,128)(2,1)S(1)}, bf16[16,2048]{1,0:T(8,128)(2,1)S(1)}, u32[]{:S(2)}, u32[]{:S(2)}) collective-permute-start(bf16[16,2048]{1,0:T(8,128)(2,1)S(1)} %get-tuple-element.21), channel_id=1, source_target_pairs={{4,5},{5,4},{6,7},{7,6},{12,13},{13,12},{14,15},{15,14},{20,21},{2... | collective-permute-start | bytes 196616 | tf_op jit(solution)/shard_map/ppermute | solution.py:279
  36.9 5.7 %collective-permute-start.14 = (bf16[16,2048]{1,0:T(8,128)(2,1)S(1)}, bf16[16,2048]{1,0:T(8,128)(2,1)S(1)}, u32[]{:S(2)}, u32[]{:S(2)}) collective-permute-start(bf16[16,2048]{1,0:T(8,128)(2,1)S(1)} %get-tuple-element.24), channel_id=1, source_target_pairs={{0,4},{1,5},{2,6},{3,7},{4,1},{5,0},{6,3},{7,2},{8,12},{9,13},{10,... | collective-permute-start | bytes 196616 | tf_op jit(solution)/shard_map/ppermute | solution.py:279
  40.0 8.3 %collective-permute-start.12 = (bf16[16,2048]{1,0:T(8,128)(2,1)S(1)}, bf16[16,2048]{1,0:T(8,128)(2,1)S(1)}, u32[]{:S(2)}, u32[]{:S(2)}) collective-permute-start(bf16[16,2048]{1,0:T(8,128)(2,1)S(1)} %get-tuple-element.22), channel_id=1, source_target_pairs={{0,2},{1,3},{2,0},{3,1},{4,7},{5,6},{6,5},{7,4},{8,10},{9,11},{10,... | collective-permute-start | bytes 196616 | tf_op jit(solution)/shard_map/ppermute | solution.py:279
  42.6 5.7 %collective-permute-start.13 = (bf16[16,2048]{1,0:T(8,128)(2,1)S(1)}, bf16[16,2048]{1,0:T(8,128)(2,1)S(1)}, u32[]{:S(2)}, u32[]{:S(2)}) collective-permute-start(bf16[16,2048]{1,0:T(8,128)(2,1)S(1)} %get-tuple-element.23), channel_id=1, source_target_pairs={{0,6},{1,7},{2,4},{3,5},{4,3},{5,2},{6,1},{7,0},{8,14},{9,15},{10,... | collective-permute-start | bytes 196616 | tf_op jit(solution)/shard_map/ppermute | solution.py:279

commit v4 on v3

--- a/solution.py
+++ b/solution.py
@@ -70,14 +70,14 @@
 
 
 def local_kernel(
-    lengths_in, q_in, keys, values, _, __,
-    packed, q_ref,
-    lengths, q_heads, scores, weights, sems,
-    *, rows, heads, kv_heads,
+    lengths_in, q_in, keys, values, weight_in, _, packed, q_ref, *rest,
+    rows, heads, kv_heads, pieces, columns,
 ):
+    lengths, q_heads, scores, weights, sems, fetch_sems = rest[len(pieces) :]
     positions = keys.shape[1]
     lengths_copy = copy_in(lengths_in, lengths, sems.at[0])
     q_copy = copy_in(q_in, q_ref, sems.at[1])
+    weight_copies = fetch(weight_in, pieces, rest, fetch_sems, columns)
     q_copy.wait()
     wide = q_ref[...].astype(f32)
     for h in range(heads):
@@ -100,6 +100,8 @@
     for r in range(rows):
         mixed = jnp.dot(weights[r], values[r], preferred_element_type=f32)
         packed[pl.ds(r * heads, heads), :] = own_columns(mixed, kv_heads)
+    for copy in weight_copies:
+        copy.wait()
 
 
 def step_mask(group, step):
@@ -116,10 +118,17 @@
 
 
 def fetch(weight, pieces, targets, sems, columns):
-    return [
-        copy_in(piece_of(weight, piece, columns), target, sems.at[i])
+    copies = [
+        pltpu.make_async_copy(piece_of(weight, piece, columns), target, sems.at[i])
         for i, (piece, target) in enumerate(zip(pieces, targets))
     ]
+
+    @pl.when(lax.axis_index("group") >= 0)
+    def _():
+        for copy in copies:
+            copy.start()
+
+    return copies
 
 
 def fetch_kernel(weight, _, *rest, pieces, columns):
@@ -196,9 +205,9 @@
             own[:, at] = product[:rows]
 
 
-def combine_kernel(*refs, rows, heads, slots, pieces, last, columns, chunk):
-    local, gathered, halves = refs[:2], refs[2:4], refs[4:6]
-    weight_in, x_ref, free_total, same, other, *rest = refs[6:]
+def combine_kernel(*refs, groups, rows, heads, slots, pieces, last, columns, chunk):
+    local, gathered, halves = refs[:2], refs[2 : 2 + groups], refs[2 + groups : 4 + groups]
+    weight_in, x_ref, free_total, same, other, *rest = refs[4 + groups :]
     own = rest.pop(0) if last else None
     mixed, high, total, sems = rest[len(pieces) :]
     copies = fetch(weight_in, pieces, rest, sems, columns)
@@ -261,20 +270,31 @@
         copy.wait()
 
 
-def sum_kernel(own, final, *refs):
-    total = jnp.where(lax.axis_index("group") % 2 == 0, own[...], final[...].astype(f32))
+def pick_kernel(even, odd, out):
+    first = lax.axis_index("group") % 2 == 0
+
+    @pl.when(first)
+    def _():
+        out[...] = even[...]
+
+    @pl.when(jnp.logical_not(first))
+    def _():
+        out[...] = odd[...]
+
+
+def sum_kernel(own, crossed, *refs):
+    total = jnp.where(lax.axis_index("group") % 2 == 0, own[...], crossed[...].astype(f32))
     for part in refs[:-1]:
         total = total + part[...].astype(f32)
     refs[-1][...] = total.astype(bf16)
 
 
-def send_block(value, step, cross):
+def send_block(value, step, crossed):
     groups, tp = lax.axis_size("group"), lax.axis_size("tp")
     pairs = [
-        (g * tp + z, (g ^ cross) * tp + (z ^ step_mask(g, step)))
+        (g * tp + z, g * tp + (z ^ step_mask(g ^ crossed, step)))
         for g in range(groups)
         for z in range(tp)
-        if cross or step_mask(g, step)
     ]
     return lax.ppermute(value, ("group", "tp"), pairs)
 
@@ -282,10 +302,6 @@
 def swap(value, axis, mask):
     size = lax.axis_size(axis)
     return lax.ppermute(value, axis, [(i, i ^ mask) for i in range(size)])
-
-
-def pair_masks(groups):
-    return [1 << i for i in range(1, (groups - 1).bit_length())]
 
 
 def gather_group(value):
@@ -342,12 +358,16 @@
     token = call(open_kernel, jax.ShapeDtypeStruct((8, LANES), f32), [HBM], vmem=1 << 20)(
         out_weight
     )
-    local, own_queries = call(
-        lambda *refs: local_kernel(*refs, kv_heads=kv_heads, **sizes),
+    taken = take(1)
+    local, own_queries, *more = call(
+        lambda *refs, taken=taken: local_kernel(
+            *refs, kv_heads=kv_heads, pieces=taken, columns=columns, **sizes
+        ),
         [
             jax.ShapeDtypeStruct((2 * rows * heads, LANES), f32),
             jax.ShapeDtypeStruct(queries.shape, queries.dtype),
-        ],
+        ]
+        + [held] * len(taken),
         [HBM, HBM, VMEM, VMEM, HBM, VMEM],
         scratch=[
             pltpu.SMEM(row_lengths.shape, jnp.int32),
@@ -355,10 +375,12 @@
             pltpu.VMEM((rows * heads, cache_keys.shape[1]), f32),
             pltpu.VMEM((rows, heads, cache_keys.shape[1]), bf16),
             copies((2,)),
+            copies((1,)),
         ],
         moved=2 * (cache_keys.size + cache_values.size),
         vmem=4 << 20,
     )(row_lengths, queries, cache_keys, cache_values, out_weight, token)
+    weights.update(zip(taken, more))
     shards[0] = own_queries
     pair_local = swap(local, "group", 1)
 
@@ -389,22 +411,17 @@
     )(slot_owner, slot_fill, free_counts, *shards, pool_keys, pool_values, out_weight)
     weights.update(zip(taken, more))
 
-    gathered = packed
-    for mask in pair_masks(groups):
-        other = swap(gathered, "group", mask)
-        taken = take(1)
-        if taken:
-            more = call(
-                lambda *refs, taken=taken: fetch_kernel(*refs, pieces=taken, columns=columns),
-                [held] * len(taken),
-                [HBM, pl.BlockSpec(memory_space=pl.ANY)],
-                scratch=[copies((1,))],
-                moved=piece_bytes,
-                vmem=1 << 20,
-            )(out_weight, packed)
-            weights.update(zip(taken, more))
-        gathered = jnp.concatenate([gathered, other], axis=0)
-    pair_gathered = swap(gathered, "group", 1)
+    far = gather_group(packed)
+    taken = take(1)
+    more = call(
+        lambda *refs, taken=taken: fetch_kernel(*refs, pieces=taken, columns=columns),
+        [held] * len(taken),
+        [HBM, pl.BlockSpec(memory_space=pl.ANY)],
+        scratch=[copies((1,))],
+        moved=piece_bytes,
+        vmem=1 << 20,
+    )(out_weight, packed)
+    weights.update(zip(taken, more))
 
     block = jax.ShapeDtypeStruct((rows, columns), bf16)
     whole = jax.ShapeDtypeStruct((rows, columns), f32)
@@ -418,18 +435,20 @@
         moved = piece_bytes * max(2, len(taken))
         if i == 0:
             x, free_total, same, other, *more = call(
-                lambda *refs: combine_kernel(*refs, slots=slots, **settings, **sizes),
+                lambda *refs: combine_kernel(
+                    *refs, groups=groups, slots=slots, **settings, **sizes
+                ),
                 [
                     jax.ShapeDtypeStruct((2 * rows, width), bf16),
                     jax.ShapeDtypeStruct((1,), jnp.int32),
                 ]
                 + outs,
-                [VMEM] * 6 + [HBM],
+                [VMEM] * (4 + groups) + [HBM],
                 out_specs=[VMEM, SMEM] + [VMEM] * len(outs),
                 scratch=[pltpu.VMEM((2 * rows * heads, LANES), f32)] * 3
                 + [copies((max(1, len(taken)),))],
                 moved=moved,
-            )(local, pair_local, gathered, pair_gathered, *halves, out_weight)
+            )(local, pair_local, *far, *halves, out_weight)
         else:
             same, other, *more = call(
                 lambda *refs, settings=settings: project_kernel(*refs, **settings),
@@ -442,12 +461,14 @@
         if last:
             own = more.pop(0)
         weights.update(zip(taken, more))
-        received.append(send_block(same, step, 0))
-        received.append(send_block(other, step, 1))
-    final = received.pop(-2)
-    mixed_out = call(sum_kernel, block, [VMEM] * (2 + len(received)))(
-        own, final, *received
-    )
+        crossed = swap(other, "group", 1)
+        if last:
+            leaving = call(pick_kernel, block, [VMEM] * 2, vmem=1 << 20)(crossed, same)
+            received.append(swap(leaving, "tp", 1))
+        else:
+            received.append(send_block(same, step, 0))
+            received.append(send_block(crossed, step, 1))
+    mixed_out = call(sum_kernel, block, [VMEM] * (2 + len(received)))(own, crossed, *received)
     return (mixed_out, free_total)
 
 

time: 49.5 us -> 47.2 us (0.954)
  waiting for transfers between devices: 17.9 us -> 14.2 us
  local copies, waits for them, and re-layouts: 0.03 us -> 3.45 us
  Pallas kernels: 16.9 us -> 14.7 us
  starting transfers between devices: 12.6 us -> 13.2 us
    unnamed x10, local copies, waits for them, and re-layouts: 0.03 us -> 3.45 us
    ppermute x11 -> x18, starting transfers between devices: 6.24 us -> 9.2 us  [swap(): return lax.ppermute(value, axis, [(i, i ^ mask) for i in range(size)])]
    ppermute x11 -> x18, waiting for transfers between devices: 12.2 us -> 9.67 us  [swap(): return lax.ppermute(value, axis, [(i, i ^ mask) for i in range(size)])]
    ppermute x4 -> x2, starting transfers between devices: 6.34 us -> 4 us  [send_block(): return lax.ppermute(value, ('group', 'tp'), pairs)]
    pallas_call x2 -> x1, Pallas kernels: 4.43 us -> 2.2 us  [step(): call(lambda *refs, taken=taken: fetch_kernel(*refs, pieces=taken, columns...]
    ppermute x4 -> x2, waiting for transfers between devices: 5.68 us -> 4.53 us  [send_block(): return lax.ppermute(value, ('group', 'tp'), pairs)]
    pallas_call x3 -> x4, Pallas kernels: 8.13 us -> 8.14 us  [the longest x1 4.61 us: step(): call(lambda *refs: combine_kernel(*refs, groups=groups, slots=slots, **se...]
  transfers between devices with their start and end apart: 15 -> 20, of which waited for: 6 -> 10; matrix products, arithmetic and copies ran while one was open for 0% -> 0% of each run, Pallas kernels for 21% -> 14%
where the time goes in v4:
time: 47.2 us; the launch traced here: 47 us
  Pallas kernels  14.7 us (31%)
  waiting for transfers between devices  14.2 us (30%)
  starting transfers between devices  13.2 us (28%)
  local copies, waits for them, and re-layouts  3.45 us (7%)
  between operations  1.44 us (3%)
    ppermute x18, waiting for transfers between devices, swap(): return lax.ppermute(value, axis, [(i, i ^ mask) for i in range(size)])  9.67 us
    ppermute x18, starting transfers between devices, swap(): return lax.ppermute(value, axis, [(i, i ^ mask) for i in range(size)])  9.2 us
    pallas_call x1, Pallas kernels, step(): call(lambda *refs: combine_kernel(*refs, groups=groups, slots=slots, **se...  4.61 us
    ppermute x2, waiting for transfers between devices, send_block(): return lax.ppermute(value, ('group', 'tp'), pairs)  4.53 us
    ppermute x2, starting transfers between devices, send_block(): return lax.ppermute(value, ('group', 'tp'), pairs)  4 us
    unnamed x10, local copies, waits for them, and re-layouts  3.45 us
    pallas_call x1, Pallas kernels, step(): call(lambda *refs, taken=taken: local_kernel(*refs, kv_heads=kv_heads, pi...  2.85 us
    pallas_call x1, Pallas kernels, step(): call(lambda *refs, taken=taken: slot_kernel(*refs, groups=groups, kv_head...  2.8 us
  transfers between devices with their start and end apart: 20, of which 10 were waited for; matrix products, arithmetic and copies ran while one was open for 0% of the time, Pallas kernels for 14%

profile of v4, /device:TPU:0, one launch (start us, length us, event | category | flops | bytes accessed | tf_op | source)
XLA Modules:
  0.0 47.0 jit_solution(13236558019071196546)
XLA Ops:
  0.7 2.2 %copy-done.1 = bf16[16,512,256]{2,1,0:T(8,128)(2,1)S(1)} copy-done((bf16[16,512,256]{2,1,0:T(8,128)(2,1)S(1)}, bf16[16,512,256]{2,1,0:T(8,128)(2,1)}, u32[]{:S(2)}) %copy-start.1) | copy-done | bytes 4194328
  2.8 1.3 %copy-done = bf16[16,512,256]{2,1,0:T(8,128)(2,1)S(1)} copy-done((bf16[16,512,256]{2,1,0:T(8,128)(2,1)S(1)}, bf16[16,512,256]{2,1,0:T(8,128)(2,1)}, u32[]{:S(2)}) %copy-start) | copy-done | bytes 4194328
  4.1 2.8 %shard_map.114 = (f32[512,128]{1,0:T(8,128)S(1)}, bf16[16,2048]{1,0:T(8,128)(2,1)S(1)}, bf16[1024,2048]{1,0:T(8,128)(2,1)S(1)}) custom-call(s32[16]{0:T(128)} %refs_0_.3, bf16[16,2048]{1,0:T(8,128)(2,1)} %refs_1_.2, bf16[16,512,256]{2,1,0:T(8,128)(2,1)S(1)} %copy-done, bf16[16,512,256]{2,1,0:T(8,128)(2,1)S(1)} %copy-done.1, bf16[2048,8192]{1,0:T(8,128)(2,1)} %refs_3_.3, ...), custom_call_target="tpu_custom_call" | custom-call | bytes 8388608 | tf_op jit(solution)/shard_map/pallas_call | solution.py:362
  7.5 2.6 %collective-permute-start.2 = (bf16[16,2048]{1,0:T(8,128)(2,1)S(1)}, bf16[16,2048]{1,0:T(8,128)(2,1)S(1)}, u32[]{:S(2)}, u32[]{:S(2)}) collective-permute-start(bf16[16,2048]{1,0:T(8,128)(2,1)S(1)} %copy-done.4), channel_id=1, source_target_pairs={{0,8},{4,12},{8,0},{12,4},{16,24},{20,28},{24,16},{28,20},{1,9},{5... | collective-permute-start | bytes 196616 | tf_op jit(solution)/shard_map/ppermute | solution.py:304
  10.1 1.5 %collective-permute-start.6 = (bf16[16,2048]{1,0:T(8,128)(2,1)S(1)}, bf16[16,2048]{1,0:T(8,128)(2,1)S(1)}, u32[]{:S(2)}, u32[]{:S(2)}) collective-permute-start(bf16[16,2048]{1,0:T(8,128)(2,1)S(1)} %copy-done.4), channel_id=1, source_target_pairs={{0,24},{4,28},{8,16},{12,20},{16,8},{20,12},{24,0},{28,4},{1,25},{... | collective-permute-start | bytes 196616 | tf_op jit(solution)/shard_map/ppermute | solution.py:304
  11.6 1.1 %collective-permute-done.2.refs_5_ = bf16[16,2048]{1,0:T(8,128)(2,1)S(1)} collective-permute-done((bf16[16,2048]{1,0:T(8,128)(2,1)S(1)}, bf16[16,2048]{1,0:T(8,128)(2,1)S(1)}, u32[]{:S(2)}, u32[]{:S(2)}) %collective-permute-start.2) | collective-permute-done | bytes 65568 | tf_op jit(solution)/shard_map/ppermute | solution.py:304
  12.8 2.7 %collective-permute-done.6.refs_9_ = bf16[16,2048]{1,0:T(8,128)(2,1)S(1)} collective-permute-done((bf16[16,2048]{1,0:T(8,128)(2,1)S(1)}, bf16[16,2048]{1,0:T(8,128)(2,1)S(1)}, u32[]{:S(2)}, u32[]{:S(2)}) %collective-permute-start.6) | collective-permute-done | bytes 65568 | tf_op jit(solution)/shard_map/ppermute | solution.py:304
  15.5 1.2 %collective-permute-done.4.refs_7_ = bf16[16,2048]{1,0:T(8,128)(2,1)S(1)} collective-permute-done((bf16[16,2048]{1,0:T(8,128)(2,1)S(1)}, bf16[16,2048]{1,0:T(8,128)(2,1)S(1)}, u32[]{:S(2)}, u32[]{:S(2)}) %collective-permute-start.4) | collective-permute-done | bytes 65568 | tf_op jit(solution)/shard_map/ppermute | solution.py:304
  17.4 0.6 %collective-permute-done.5.refs_8_ = bf16[16,2048]{1,0:T(8,128)(2,1)S(1)} collective-permute-done((bf16[16,2048]{1,0:T(8,128)(2,1)S(1)}, bf16[16,2048]{1,0:T(8,128)(2,1)S(1)}, u32[]{:S(2)}, u32[]{:S(2)}) %collective-permute-start.5) | collective-permute-done | bytes 65568 | tf_op jit(solution)/shard_map/ppermute | solution.py:304
  17.9 2.8 %shard_map.115 = (f32[48,128]{1,0:T(8,128)S(1)}, bf16[1024,2048]{1,0:T(8,128)(2,1)S(1)}) custom-call(s32[2]{0:T(128)} %refs_0_.4, s32[2]{0:T(128)} %refs_1_.3, s32[1]{0:T(128)S(6)} %copy.12.refs_2_, bf16[16,2048]{1,0:T(8,128)(2,1)S(1)} %get-tuple-element.16.refs_3_, bf16[16,2048]{1,0:T(8,128)(2,1)S(1)} %collective-permute-done.1.refs_4_, ...), custom_call_target="tpu_custom_call" | custom-call | bytes 8388608 | tf_op jit(solution)/shard_map/pallas_call | solution.py:388
  20.8 1.5 %collective-permute-start.13 = (f32[48,128]{1,0:T(8,128)S(1)}, f32[48,128]{1,0:T(8,128)S(1)}, u32[]{:S(2)}, u32[]{:S(2)}) collective-permute-start(f32[48,128]{1,0:T(8,128)S(1)} %get-tuple-element.17.refs_2_.refs_1_), channel_id=1, source_target_pairs={{0,24},{4,28},{8,16},{12,20},{16,8},{20,12},{24,0},{28,4},{1,25},{... | collective-permute-start | bytes 73736 | tf_op jit(solution)/shard_map/ppermute | solution.py:304
  22.3 1.3 %collective-permute-start.11 = (f32[48,128]{1,0:T(8,128)S(1)}, f32[48,128]{1,0:T(8,128)S(1)}, u32[]{:S(2)}, u32[]{:S(2)}) collective-permute-start(f32[48,128]{1,0:T(8,128)S(1)} %get-tuple-element.17.refs_2_.refs_1_), channel_id=1, source_target_pairs={{0,16},{4,20},{8,24},{12,28},{16,0},{20,4},{24,8},{28,12},{1,17},{... | collective-permute-start | bytes 73736 | tf_op jit(solution)/shard_map/ppermute | solution.py:304
  23.6 0.7 %collective-permute-start.9 = (f32[48,128]{1,0:T(8,128)S(1)}, f32[48,128]{1,0:T(8,128)S(1)}, u32[]{:S(2)}, u32[]{:S(2)}) collective-permute-start(f32[48,128]{1,0:T(8,128)S(1)} %get-tuple-element.17.refs_2_.refs_1_), channel_id=1, source_target_pairs={{0,8},{4,12},{8,0},{12,4},{16,24},{20,28},{24,16},{28,20},{1,9},{5... | collective-permute-start | bytes 73736 | tf_op jit(solution)/shard_map/ppermute | solution.py:304
  24.3 1.2 %collective-permute-done.13.refs_8_ = f32[48,128]{1,0:T(8,128)S(1)} collective-permute-done((f32[48,128]{1,0:T(8,128)S(1)}, f32[48,128]{1,0:T(8,128)S(1)}, u32[]{:S(2)}, u32[]{:S(2)}) %collective-permute-start.13) | collective-permute-done | bytes 24608 | tf_op jit(solution)/shard_map/ppermute | solution.py:304
  26.1 1.3 %collective-permute-done.9.refs_4_ = f32[48,128]{1,0:T(8,128)S(1)} collective-permute-done((f32[48,128]{1,0:T(8,128)S(1)}, f32[48,128]{1,0:T(8,128)S(1)}, u32[]{:S(2)}, u32[]{:S(2)}) %collective-permute-start.9) | collective-permute-done | bytes 24608 | tf_op jit(solution)/shard_map/ppermute | solution.py:304
  27.5 2.2 %shard_map.117.refs_1_ = bf16[1024,2048]{1,0:T(8,128)(2,1)S(1)} custom-call(bf16[2048,8192]{1,0:T(8,128)(2,1)} %refs_3_.3, f32[48,128]{1,0:T(8,128)S(1)} %get-tuple-element.17.refs_2_.refs_1_), custom_call_target="tpu_custom_call" | custom-call | bytes 4194304 | tf_op jit(solution)/shard_map/pallas_call | solution.py:416
  29.7 4.6 %shard_map.116 = (bf16[32,2048]{1,0:T(8,128)(2,1)S(1)}, s32[1]{0:T(128)}, bf16[16,2048]{1,0:T(8,128)(2,1)S(1)}, bf16[16,2048]{1,0:T(8,128)(2,1)S(1)}, bf16[1024,2048]{1,0:T(8,128)(2,1)S(1)}) custom-call(f32[512,128]{1,0:T(8,128)S(1)} %get-tuple-element.15.refs_0_, f32[512,128]{1,0:T(8,128)S(1)} %collective-permute-done.refs_1_, ...), custom_call_target="tpu_custom_call" | custom-call | bytes 8388608 | tf_op jit(solution)/shard_map/pallas_call | solution.py:437
  34.9 1.6 %shard_map.118 = (bf16[16,2048]{1,0:T(8,128)(2,1)S(1)}, bf16[16,2048]{1,0:T(8,128)(2,1)S(1)}, f32[16,2048]{1,0:T(8,128)S(1)}) custom-call(bf16[32,2048]{1,0:T(8,128)(2,1)S(1)} %get-tuple-element.20.refs_0_, bf16[1024,2048]{1,0:T(8,128)(2,1)S(1)} %shard_map.117.refs_1_, bf16[1024,2048]{1,0:T(8,128)(2,1)S(1)} %get-tuple-element.21.refs_2_, ...), custom_call_target="tpu_custom_call" | custom-call | bytes 8388608 | tf_op jit(solution)/shard_map/pallas_call | solution.py:453
  36.5 2.7 %collective-permute-start.16 = (bf16[16,2048]{1,0:T(8,128)(2,1)S(1)}, bf16[16,2048]{1,0:T(8,128)(2,1)S(1)}, u32[]{:S(2)}, u32[]{:S(2)}) collective-permute-start(bf16[16,2048]{1,0:T(8,128)(2,1)S(1)} %get-tuple-element.24), channel_id=1, source_target_pairs={{0,2},{1,3},{2,0},{3,1},{4,7},{5,6},{6,5},{7,4},{8,10},{9,11},{10,... | collective-permute-start | bytes 196616 | tf_op jit(solution)/shard_map/ppermute | solution.py:299
  39.2 1.3 %collective-permute-start.18 = (bf16[16,2048]{1,0:T(8,128)(2,1)S(1)}, bf16[16,2048]{1,0:T(8,128)(2,1)S(1)}, u32[]{:S(2)}, u32[]{:S(2)}) collective-permute-start(bf16[16,2048]{1,0:T(8,128)(2,1)S(1)} %collective-permute-done.17), channel_id=1, source_target_pairs={{0,3},{1,2},{2,1},{3,0},{4,6},{5,7},{6,4},{7,5},{8,11},{9,10},{10,... | collective-permute-start | bytes 196616 | tf_op jit(solution)/shard_map/ppermute | solution.py:299
  40.9 3.7 %collective-permute-done.16.refs_0_ = bf16[16,2048]{1,0:T(8,128)(2,1)S(1)} collective-permute-done((bf16[16,2048]{1,0:T(8,128)(2,1)S(1)}, bf16[16,2048]{1,0:T(8,128)(2,1)S(1)}, u32[]{:S(2)}, u32[]{:S(2)}) %collective-permute-start.16) | collective-permute-done | bytes 65568 | tf_op jit(solution)/shard_map/ppermute | solution.py:299
  44.5 0.9 %collective-permute-done.18.refs_1_ = bf16[16,2048]{1,0:T(8,128)(2,1)S(1)} collective-permute-done((bf16[16,2048]{1,0:T(8,128)(2,1)S(1)}, bf16[16,2048]{1,0:T(8,128)(2,1)S(1)}, u32[]{:S(2)}, u32[]{:S(2)}) %collective-permute-start.18) | collective-permute-done | bytes 65568 | tf_op jit(solution)/shard_map/ppermute | solution.py:299
  45.4 0.9 %collective-permute-done.19.refs_2_ = bf16[16,2048]{1,0:T(8,128)(2,1)S(1)} collective-permute-done((bf16[16,2048]{1,0:T(8,128)(2,1)S(1)}, bf16[16,2048]{1,0:T(8,128)(2,1)S(1)}, u32[]{:S(2)}, u32[]{:S(2)}) %collective-permute-start.19) | collective-permute-done | bytes 65568 | tf_op jit(solution)/shard_map/ppermute | solution.py:304
  46.3 0.7 %shard_map.120 = bf16[16,2048]{1,0:T(8,128)(2,1)} custom-call(f32[16,2048]{1,0:T(8,128)S(1)} %get-tuple-element.22.own, bf16[16,2048]{1,0:T(8,128)(2,1)S(1)} %collective-permute-done.15.even.crossed, bf16[16,2048]{1,0:T(8,128)(2,1)S(1)} %collective-permute-done.16.refs_0_, bf16[16,2048]{1,0:T(8,128)(2,1)S(1)} %collective-permute-done.18.refs_1_, ...), custom_call_target="tpu_custom_call" | custom-call | tf_op jit(solution)/shard_map/pallas_call | solution.py:471
  (34 shorter events, 2.2 us)
Async XLA Ops:
  0.6 3.5 %copy-start = (bf16[16,512,256]{2,1,0:T(8,128)(2,1)S(1)}, bf16[16,512,256]{2,1,0:T(8,128)(2,1)}, u32[]{:S(2)}) copy-start(bf16[16,512,256]{2,1,0:T(8,128)(2,1)} %refs_2_.2) | copy-start | bytes 12582916
  4.1 3.4 %copy-start.4 = (bf16[16,2048]{1,0:T(8,128)(2,1)S(1)}, bf16[16,2048]{1,0:T(8,128)(2,1)}, u32[]{:S(2)}) copy-start(bf16[16,2048]{1,0:T(8,128)(2,1)} %refs_1_.2) | copy-start | bytes 196612
  4.1 13.8 %copy-start.2 = (bf16[2,4096,256]{2,1,0:T(8,128)(2,1)S(1)}, bf16[2,4096,256]{2,1,0:T(8,128)(2,1)}, u32[]{:S(2)}) copy-start(bf16[2,4096,256]{2,1,0:T(8,128)(2,1)} %refs_11_.1) | copy-start | bytes 12582916
  4.1 13.8 %copy-start.3 = (bf16[2,4096,256]{2,1,0:T(8,128)(2,1)S(1)}, bf16[2,4096,256]{2,1,0:T(8,128)(2,1)}, u32[]{:S(2)}) copy-start(bf16[2,4096,256]{2,1,0:T(8,128)(2,1)} %refs_12_.2) | copy-start | bytes 12582916
  7.0 22.7 %collective-permute-start = (f32[512,128]{1,0:T(8,128)S(1)}, f32[512,128]{1,0:T(8,128)S(1)}, u32[]{:S(2)}, u32[]{:S(2)}) collective-permute-start(f32[512,128]{1,0:T(8,128)S(1)} %get-tuple-element.15.refs_0_), channel_id=1, source_target_pairs={{0,4},{4,0},{8,12},{12,8},{16,20},{20,16},{24,28},{28,24},{1,5},{5... | collective-permute-start | bytes 786440 | tf_op jit(solution)/shard_map/ppermute | solution.py:304
  7.5 5.2 %collective-permute-start.2 = (bf16[16,2048]{1,0:T(8,128)(2,1)S(1)}, bf16[16,2048]{1,0:T(8,128)(2,1)S(1)}, u32[]{:S(2)}, u32[]{:S(2)}) collective-permute-start(bf16[16,2048]{1,0:T(8,128)(2,1)S(1)} %copy-done.4), channel_id=1, source_target_pairs={{0,8},{4,12},{8,0},{12,4},{16,24},{20,28},{24,16},{28,20},{1,9},{5... | collective-permute-start | bytes 196616 | tf_op jit(solution)/shard_map/ppermute | solution.py:304
  10.1 5.4 %collective-permute-start.6 = (bf16[16,2048]{1,0:T(8,128)(2,1)S(1)}, bf16[16,2048]{1,0:T(8,128)(2,1)S(1)}, u32[]{:S(2)}, u32[]{:S(2)}) collective-permute-start(bf16[16,2048]{1,0:T(8,128)(2,1)S(1)} %copy-done.4), channel_id=1, source_target_pairs={{0,24},{4,28},{8,16},{12,20},{16,8},{20,12},{24,0},{28,4},{1,25},{... | collective-permute-start | bytes 196616 | tf_op jit(solution)/shard_map/ppermute | solution.py:304
  11.6 5.1 %collective-permute-start.4 = (bf16[16,2048]{1,0:T(8,128)(2,1)S(1)}, bf16[16,2048]{1,0:T(8,128)(2,1)S(1)}, u32[]{:S(2)}, u32[]{:S(2)}) collective-permute-start(bf16[16,2048]{1,0:T(8,128)(2,1)S(1)} %copy-done.4), channel_id=1, source_target_pairs={{0,16},{4,20},{8,24},{12,28},{16,0},{20,4},{24,8},{28,12},{1,17},{... | collective-permute-start | bytes 196616 | tf_op jit(solution)/shard_map/ppermute | solution.py:304
  11.6 5.7 %collective-permute-start.1 = (bf16[16,2048]{1,0:T(8,128)(2,1)S(1)}, bf16[16,2048]{1,0:T(8,128)(2,1)S(1)}, u32[]{:S(2)}, u32[]{:S(2)}) collective-permute-start(bf16[16,2048]{1,0:T(8,128)(2,1)S(1)} %copy-done.4), channel_id=1, source_target_pairs={{0,4},{4,0},{8,12},{12,8},{16,20},{20,16},{24,28},{28,24},{1,5},{5... | collective-permute-start | bytes 196616 | tf_op jit(solution)/shard_map/ppermute | solution.py:304
  12.8 4.6 %collective-permute-start.3 = (bf16[16,2048]{1,0:T(8,128)(2,1)S(1)}, bf16[16,2048]{1,0:T(8,128)(2,1)S(1)}, u32[]{:S(2)}, u32[]{:S(2)}) collective-permute-start(bf16[16,2048]{1,0:T(8,128)(2,1)S(1)} %collective-permute-done.2.refs_5_), channel_id=1, source_target_pairs={{0,4},{4,0},{8,12},{12,8},{16,20},{20,16},{24,28},{28,24},{1,5},{5... | collective-permute-start | bytes 196616 | tf_op jit(solution)/shard_map/ppermute | solution.py:304
  15.5 1.9 %collective-permute-start.7 = (bf16[16,2048]{1,0:T(8,128)(2,1)S(1)}, bf16[16,2048]{1,0:T(8,128)(2,1)S(1)}, u32[]{:S(2)}, u32[]{:S(2)}) collective-permute-start(bf16[16,2048]{1,0:T(8,128)(2,1)S(1)} %collective-permute-done.6.refs_9_), channel_id=1, source_target_pairs={{0,4},{4,0},{8,12},{12,8},{16,20},{20,16},{24,28},{28,24},{1,5},{5... | collective-permute-start | bytes 196616 | tf_op jit(solution)/shard_map/ppermute | solution.py:304
  16.7 1.3 %collective-permute-start.5 = (bf16[16,2048]{1,0:T(8,128)(2,1)S(1)}, bf16[16,2048]{1,0:T(8,128)(2,1)S(1)}, u32[]{:S(2)}, u32[]{:S(2)}) collective-permute-start(bf16[16,2048]{1,0:T(8,128)(2,1)S(1)} %collective-permute-done.4.refs_7_), channel_id=1, source_target_pairs={{0,4},{4,0},{8,12},{12,8},{16,20},{20,16},{24,28},{28,24},{1,5},{5... | collective-permute-start | bytes 196616 | tf_op jit(solution)/shard_map/ppermute | solution.py:304
  20.8 4.8 %collective-permute-start.13 = (f32[48,128]{1,0:T(8,128)S(1)}, f32[48,128]{1,0:T(8,128)S(1)}, u32[]{:S(2)}, u32[]{:S(2)}) collective-permute-start(f32[48,128]{1,0:T(8,128)S(1)} %get-tuple-element.17.refs_2_.refs_1_), channel_id=1, source_target_pairs={{0,24},{4,28},{8,16},{12,20},{16,8},{20,12},{24,0},{28,4},{1,25},{... | collective-permute-start | bytes 73736 | tf_op jit(solution)/shard_map/ppermute | solution.py:304
  22.3 3.8 %collective-permute-start.11 = (f32[48,128]{1,0:T(8,128)S(1)}, f32[48,128]{1,0:T(8,128)S(1)}, u32[]{:S(2)}, u32[]{:S(2)}) collective-permute-start(f32[48,128]{1,0:T(8,128)S(1)} %get-tuple-element.17.refs_2_.refs_1_), channel_id=1, source_target_pairs={{0,16},{4,20},{8,24},{12,28},{16,0},{20,4},{24,8},{28,12},{1,17},{... | collective-permute-start | bytes 73736 | tf_op jit(solution)/shard_map/ppermute | solution.py:304
  23.6 3.8 %collective-permute-start.9 = (f32[48,128]{1,0:T(8,128)S(1)}, f32[48,128]{1,0:T(8,128)S(1)}, u32[]{:S(2)}, u32[]{:S(2)}) collective-permute-start(f32[48,128]{1,0:T(8,128)S(1)} %get-tuple-element.17.refs_2_.refs_1_), channel_id=1, source_target_pairs={{0,8},{4,12},{8,0},{12,4},{16,24},{20,28},{24,16},{28,20},{1,9},{5... | collective-permute-start | bytes 73736 | tf_op jit(solution)/shard_map/ppermute | solution.py:304
  24.3 5.3 %collective-permute-start.8 = (f32[48,128]{1,0:T(8,128)S(1)}, f32[48,128]{1,0:T(8,128)S(1)}, u32[]{:S(2)}, u32[]{:S(2)}) collective-permute-start(f32[48,128]{1,0:T(8,128)S(1)} %get-tuple-element.17.refs_2_.refs_1_), channel_id=1, source_target_pairs={{0,4},{4,0},{8,12},{12,8},{16,20},{20,16},{24,28},{28,24},{1,5},{5... | collective-permute-start | bytes 73736 | tf_op jit(solution)/shard_map/ppermute | solution.py:304
  25.5 4.1 %collective-permute-start.14 = (f32[48,128]{1,0:T(8,128)S(1)}, f32[48,128]{1,0:T(8,128)S(1)}, u32[]{:S(2)}, u32[]{:S(2)}) collective-permute-start(f32[48,128]{1,0:T(8,128)S(1)} %collective-permute-done.13.refs_8_), channel_id=1, source_target_pairs={{0,4},{4,0},{8,12},{12,8},{16,20},{20,16},{24,28},{28,24},{1,5},{5... | collective-permute-start | bytes 73736 | tf_op jit(solution)/shard_map/ppermute | solution.py:304
  26.1 3.6 %collective-permute-start.12 = (f32[48,128]{1,0:T(8,128)S(1)}, f32[48,128]{1,0:T(8,128)S(1)}, u32[]{:S(2)}, u32[]{:S(2)}) collective-permute-start(f32[48,128]{1,0:T(8,128)S(1)} %collective-permute-done.11.refs_6_), channel_id=1, source_target_pairs={{0,4},{4,0},{8,12},{12,8},{16,20},{20,16},{24,28},{28,24},{1,5},{5... | collective-permute-start | bytes 73736 | tf_op jit(solution)/shard_map/ppermute | solution.py:304
  27.5 2.2 %collective-permute-start.10 = (f32[48,128]{1,0:T(8,128)S(1)}, f32[48,128]{1,0:T(8,128)S(1)}, u32[]{:S(2)}, u32[]{:S(2)}) collective-permute-start(f32[48,128]{1,0:T(8,128)S(1)} %collective-permute-done.9.refs_4_), channel_id=1, source_target_pairs={{0,4},{4,0},{8,12},{12,8},{16,20},{20,16},{24,28},{28,24},{1,5},{5... | collective-permute-start | bytes 73736 | tf_op jit(solution)/shard_map/ppermute | solution.py:304
  34.3 4.9 %collective-permute-start.17 = (bf16[16,2048]{1,0:T(8,128)(2,1)S(1)}, bf16[16,2048]{1,0:T(8,128)(2,1)S(1)}, u32[]{:S(2)}, u32[]{:S(2)}) collective-permute-start(bf16[16,2048]{1,0:T(8,128)(2,1)S(1)} %get-tuple-element.25), channel_id=1, source_target_pairs={{0,4},{4,0},{8,12},{12,8},{16,20},{20,16},{24,28},{28,24},{1,5},{5... | collective-permute-start | bytes 196616 | tf_op jit(solution)/shard_map/ppermute | solution.py:304
  36.5 4.1 %collective-permute-start.15 = (bf16[16,2048]{1,0:T(8,128)(2,1)S(1)}, bf16[16,2048]{1,0:T(8,128)(2,1)S(1)}, u32[]{:S(2)}, u32[]{:S(2)}) collective-permute-start(bf16[16,2048]{1,0:T(8,128)(2,1)S(1)} %get-tuple-element.23), channel_id=1, source_target_pairs={{0,4},{4,0},{8,12},{12,8},{16,20},{20,16},{24,28},{28,24},{1,5},{5... | collective-permute-start | bytes 196616 | tf_op jit(solution)/shard_map/ppermute | solution.py:304
  36.5 8.0 %collective-permute-start.16 = (bf16[16,2048]{1,0:T(8,128)(2,1)S(1)}, bf16[16,2048]{1,0:T(8,128)(2,1)S(1)}, u32[]{:S(2)}, u32[]{:S(2)}) collective-permute-start(bf16[16,2048]{1,0:T(8,128)(2,1)S(1)} %get-tuple-element.24), channel_id=1, source_target_pairs={{0,2},{1,3},{2,0},{3,1},{4,7},{5,6},{6,5},{7,4},{8,10},{9,11},{10,... | collective-permute-start | bytes 196616 | tf_op jit(solution)/shard_map/ppermute | solution.py:299
  39.2 6.2 %collective-permute-start.18 = (bf16[16,2048]{1,0:T(8,128)(2,1)S(1)}, bf16[16,2048]{1,0:T(8,128)(2,1)S(1)}, u32[]{:S(2)}, u32[]{:S(2)}) collective-permute-start(bf16[16,2048]{1,0:T(8,128)(2,1)S(1)} %collective-permute-done.17), channel_id=1, source_target_pairs={{0,3},{1,2},{2,1},{3,0},{4,6},{5,7},{6,4},{7,5},{8,11},{9,10},{10,... | collective-permute-start | bytes 196616 | tf_op jit(solution)/shard_map/ppermute | solution.py:299
  40.6 5.7 %collective-permute-start.19 = (bf16[16,2048]{1,0:T(8,128)(2,1)S(1)}, bf16[16,2048]{1,0:T(8,128)(2,1)S(1)}, u32[]{:S(2)}, u32[]{:S(2)}) collective-permute-start(bf16[16,2048]{1,0:T(8,128)(2,1)S(1)} %shard_map.119), channel_id=1, source_target_pairs={{0,1},{1,0},{2,3},{3,2},{4,5},{5,4},{6,7},{7,6},{8,9},{9,8},{10,11... | collective-permute-start | bytes 196616 | tf_op jit(solution)/shard_map/ppermute | solution.py:304
  (1 other events, 2.2 us)

commit v5 on v4

--- a/solution.py
+++ b/solution.py
@@ -59,30 +59,24 @@
     ) * (1.0 / math.sqrt(HEAD_DIM))
 
 
-def copy_in(source, target, sem):
-    copy = pltpu.make_async_copy(source, target, sem)
-    copy.start()
-    return copy
-
-
 def open_kernel(_, token):
     token[...] = jnp.zeros_like(token)
 
 
 def local_kernel(
-    lengths_in, q_in, keys, values, weight_in, _, packed, q_ref, *rest,
+    lengths, q_ref, keys, values, weight_in, _, packed, *rest,
     rows, heads, kv_heads, pieces, columns,
 ):
-    lengths, q_heads, scores, weights, sems, fetch_sems = rest[len(pieces) :]
+    q_heads, scores, weights, fetch_sems = rest[len(pieces) :]
     positions = keys.shape[1]
-    lengths_copy = copy_in(lengths_in, lengths, sems.at[0])
-    q_copy = copy_in(q_in, q_ref, sems.at[1])
     weight_copies = fetch(weight_in, pieces, rest, fetch_sems, columns)
-    q_copy.wait()
-    wide = q_ref[...].astype(f32)
-    for h in range(heads):
-        q_heads[pl.ds(h, rows, stride=heads), :] = wide[:, h * HEAD_DIM : (h + 1) * HEAD_DIM]
-    lengths_copy.wait()
+
+    @region
+    def _():
+        wide = q_ref[...].astype(f32)
+        for h in range(heads):
+            q_heads[pl.ds(h, rows, stride=heads), :] = wide[:, h * HEAD_DIM : (h + 1) * HEAD_DIM]
+
     place = lax.broadcasted_iota(jnp.int32, (heads, positions), 1)
     lane = lax.broadcasted_iota(jnp.int32, (heads, LANES), 1)
     for r in range(rows):
@@ -97,9 +91,13 @@
         total = jnp.sum(weight_of, axis=-1, keepdims=True)
         weights[r] = weight_of.astype(bf16)
         packed[pl.ds((rows + r) * heads, heads), :] = jnp.where(lane == 0, high, total)
-    for r in range(rows):
-        mixed = jnp.dot(weights[r], values[r], preferred_element_type=f32)
-        packed[pl.ds(r * heads, heads), :] = own_columns(mixed, kv_heads)
+
+    @region
+    def _():
+        for r in range(rows):
+            mixed = jnp.dot(weights[r], values[r], preferred_element_type=f32)
+            packed[pl.ds(r * heads, heads), :] = own_columns(mixed, kv_heads)
+
     for copy in weight_copies:
         copy.wait()
 
@@ -123,12 +121,13 @@
         for i, (piece, target) in enumerate(zip(pieces, targets))
     ]
 
-    @pl.when(lax.axis_index("group") >= 0)
-    def _():
-        for copy in copies:
-            copy.start()
-
+    for copy in copies:
+        copy.start()
     return copies
+
+
+def region(body):
+    pl.when(lax.axis_index("group") >= 0)(body)
 
 
 def fetch_kernel(weight, _, *rest, pieces, columns):
@@ -137,18 +136,12 @@
 
 
 def slot_kernel(*refs, groups, rows, heads, kv_heads, slots, chunk, pieces, columns):
-    owners_in, fills_in, free = refs[:3]
+    owners, fills, free = refs[:3]
     shards = refs[3 : 3 + groups]
     keys, values, weight_in = refs[3 + groups : 6 + groups]
     packed, *rest = refs[6 + groups :]
-    owners, fills, q_heads, scores, sems, fetch_sems = rest[len(pieces) :]
+    q_heads, scores, fetch_sems = rest[len(pieces) :]
     weight_copies = fetch(weight_in, pieces, rest, fetch_sems, columns)
-    copies = [
-        copy_in(owners_in, owners, sems.at[0]),
-        copy_in(fills_in, fills, sems.at[1]),
-    ]
-    for copy in copies:
-        copy.wait()
     positions = keys.shape[1]
     me = lax.axis_index("group")
     row_at = lax.broadcasted_iota(jnp.int32, (rows, heads * HEAD_DIM), 0)
@@ -211,51 +204,58 @@
     own = rest.pop(0) if last else None
     mixed, high, total, sems = rest[len(pieces) :]
     copies = fetch(weight_in, pieces, rest, sems, columns)
-    flat, each = rows * heads, (slots + 1) * heads
-    me = lax.axis_index("group")
-    first, second = me * rows, jnp.bitwise_xor(me, 1) * rows
-    free = jnp.zeros((heads, LANES), f32)
-    found = []
-    for part in gathered:
-        for k in range(0, part.shape[0], each):
-            stats = part[k + slots * heads : k + each, :]
-            free = free + stats
-            for s in range(slots):
-                owner = stats[0, 2 * slots + s].astype(jnp.int32)
-                found.append((part, k, s, stats, owner))
-    free_total[0] = free[0, 3 * slots].astype(jnp.int32)
-    for i in range(2):
-        stats = local[i][flat:, :]
-        high[i * flat : (i + 1) * flat, :] = jnp.broadcast_to(stats[:, 0:1], (flat, LANES))
-    slot_stats = []
-    for part, k, s, stats, owner in found:
-        in_first = (owner >= first) & (owner < first + rows)
-        in_second = (owner >= second) & (owner < second + rows)
-        row = jnp.where(
-            in_first, owner - first, jnp.where(in_second, owner - second + rows, 0)
-        )
-        mine = in_first | in_second
-        at = pl.ds(pl.multiple_of(row * heads, heads), heads)
-        slot_high = jnp.broadcast_to(stats[:, s : s + 1], (heads, LANES))
-        slot_total = jnp.broadcast_to(stats[:, slots + s : slots + s + 1], (heads, LANES))
-        slot_stats.append((part, k + s * heads, mine, at, slot_high, slot_total))
-        high[at, :] = jnp.maximum(high[at, :], jnp.where(mine, slot_high, far_below))
-    for i in range(2):
-        at = slice(i * flat, (i + 1) * flat)
-        stats = local[i][flat:, :]
-        keep = jnp.exp(jnp.broadcast_to(stats[:, 0:1], (flat, LANES)) - high[at, :])
-        mixed[at, :] = keep * local[i][:flat, :]
-        total[at, :] = keep * jnp.broadcast_to(stats[:, 1:2], (flat, LANES))
-    for part, k, mine, at, slot_high, slot_total in slot_stats:
-        add = jnp.where(mine, jnp.exp(jnp.minimum(slot_high - high[at, :], 0.0)), 0.0)
-        mixed[at, :] = mixed[at, :] + add * part[k : k + heads, :]
-        total[at, :] = total[at, :] + add * slot_total
-    mixed[...] = mixed[...] / total[...]
-    for h in range(heads):
-        x_ref[:, h * HEAD_DIM : (h + 1) * HEAD_DIM] = mixed[
-            pl.ds(h, 2 * rows, stride=heads), :
-        ].astype(bf16)
-    project(x_ref[...], halves, same, other, chunk, own)
+
+    @region
+    def _():
+        flat, each = rows * heads, (slots + 1) * heads
+        me = lax.axis_index("group")
+        first, second = me * rows, jnp.bitwise_xor(me, 1) * rows
+        free = jnp.zeros((heads, LANES), f32)
+        found = []
+        for part in gathered:
+            for k in range(0, part.shape[0], each):
+                stats = part[k + slots * heads : k + each, :]
+                free = free + stats
+                for s in range(slots):
+                    owner = stats[0, 2 * slots + s].astype(jnp.int32)
+                    found.append((part, k, s, stats, owner))
+        free_total[0] = free[0, 3 * slots].astype(jnp.int32)
+        for i in range(2):
+            stats = local[i][flat:, :]
+            high[i * flat : (i + 1) * flat, :] = jnp.broadcast_to(stats[:, 0:1], (flat, LANES))
+        slot_stats = []
+        for part, k, s, stats, owner in found:
+            in_first = (owner >= first) & (owner < first + rows)
+            in_second = (owner >= second) & (owner < second + rows)
+            row = jnp.where(
+                in_first, owner - first, jnp.where(in_second, owner - second + rows, 0)
+            )
+            mine = in_first | in_second
+            at = pl.ds(pl.multiple_of(row * heads, heads), heads)
+            slot_high = jnp.broadcast_to(stats[:, s : s + 1], (heads, LANES))
+            slot_total = jnp.broadcast_to(stats[:, slots + s : slots + s + 1], (heads, LANES))
+            slot_stats.append((part, k + s * heads, mine, at, slot_high, slot_total))
+            high[at, :] = jnp.maximum(high[at, :], jnp.where(mine, slot_high, far_below))
+        for i in range(2):
+            at = slice(i * flat, (i + 1) * flat)
+            stats = local[i][flat:, :]
+            keep = jnp.exp(jnp.broadcast_to(stats[:, 0:1], (flat, LANES)) - high[at, :])
+            mixed[at, :] = keep * local[i][:flat, :]
+            total[at, :] = keep * jnp.broadcast_to(stats[:, 1:2], (flat, LANES))
+        for part, k, mine, at, slot_high, slot_total in slot_stats:
+            add = jnp.where(mine, jnp.exp(jnp.minimum(slot_high - high[at, :], 0.0)), 0.0)
+            mixed[at, :] = mixed[at, :] + add * part[k : k + heads, :]
+            total[at, :] = total[at, :] + add * slot_total
+        mixed[...] = mixed[...] / total[...]
+        for h in range(heads):
+            x_ref[:, h * HEAD_DIM : (h + 1) * HEAD_DIM] = mixed[
+                pl.ds(h, 2 * rows, stride=heads), :
+            ].astype(bf16)
+
+    @region
+    def _():
+        project(x_ref[...], halves, same, other, chunk, own)
+
     for copy in copies:
         copy.wait()
 
@@ -265,7 +265,7 @@
     weight_in, same, other, *rest = refs[2:]
     own = rest.pop(0) if last else None
     copies = fetch(weight_in, pieces, rest, rest[-1], columns)
-    project(x_ref[...], halves, same, other, chunk, own)
+    region(lambda: project(x_ref[...], halves, same, other, chunk, own))
     for copy in copies:
         copy.wait()
 
@@ -338,10 +338,7 @@
     sizes = dict(rows=rows, heads=heads)
 
     shards = gather_group(queries)
-    queries, row_lengths, slot_owner, slot_fill, out_weight = (
-        pltpu.with_memory_space_constraint(argument, pltpu.MemorySpace.HBM)
-        for argument in (queries, row_lengths, slot_owner, slot_fill, out_weight)
-    )
+    out_weight = pltpu.with_memory_space_constraint(out_weight, pltpu.MemorySpace.HBM)
     copies = pltpu.SemaphoreType.DMA
 
     order = list(range(tp // 2 - 1, -1, -1))
@@ -359,29 +356,25 @@
         out_weight
     )
     taken = take(1)
-    local, own_queries, *more = call(
+    local, *more = call(
         lambda *refs, taken=taken: local_kernel(
             *refs, kv_heads=kv_heads, pieces=taken, columns=columns, **sizes
         ),
         [
             jax.ShapeDtypeStruct((2 * rows * heads, LANES), f32),
-            jax.ShapeDtypeStruct(queries.shape, queries.dtype),
         ]
         + [held] * len(taken),
-        [HBM, HBM, VMEM, VMEM, HBM, VMEM],
+        [SMEM, VMEM, VMEM, VMEM, HBM, VMEM],
         scratch=[
-            pltpu.SMEM(row_lengths.shape, jnp.int32),
             pltpu.VMEM((rows * heads, HEAD_DIM), f32),
             pltpu.VMEM((rows * heads, cache_keys.shape[1]), f32),
             pltpu.VMEM((rows, heads, cache_keys.shape[1]), bf16),
-            copies((2,)),
             copies((1,)),
         ],
         moved=2 * (cache_keys.size + cache_values.size),
         vmem=4 << 20,
     )(row_lengths, queries, cache_keys, cache_values, out_weight, token)
     weights.update(zip(taken, more))
-    shards[0] = own_queries
     pair_local = swap(local, "group", 1)
 
     taken = take(1)
@@ -397,13 +390,10 @@
             **sizes,
         ),
         [jax.ShapeDtypeStruct(((slots + 1) * heads, LANES), f32)] + [held] * len(taken),
-        [HBM] * 2 + [SMEM] + [VMEM] * (groups + 2) + [HBM],
+        [SMEM] * 3 + [VMEM] * (groups + 2) + [HBM],
         scratch=[
-            pltpu.SMEM(slot_owner.shape, jnp.int32),
-            pltpu.SMEM(slot_fill.shape, jnp.int32),
             pltpu.VMEM((slots * heads, HEAD_DIM), f32),
             pltpu.VMEM((slots * heads, positions), f32),
-            copies((2,)),
             copies((1,)),
         ],
         moved=2 * (pool_keys.size + pool_values.size),

time: 47.2 us -> 45.3 us (0.960)
  Pallas kernels: 14.7 us -> 13 us
  waiting for transfers between devices: 14.2 us -> 13.4 us
  starting transfers between devices: 13.2 us -> 13.8 us
    pallas_call x1, Pallas kernels: 4.61 us -> 2.74 us  [step(): call(lambda *refs: combine_kernel(*refs, groups=groups, slots=slots, **se...]
    ppermute x18, starting transfers between devices: 9.2 us -> 10.7 us  [swap(): return lax.ppermute(value, axis, [(i, i ^ mask) for i in range(size)])]
    ppermute x2, starting transfers between devices: 4 us -> 3.07 us  [send_block(): return lax.ppermute(value, ('group', 'tp'), pairs)]
    ppermute x2, waiting for transfers between devices: 4.53 us -> 3.71 us  [send_block(): return lax.ppermute(value, ('group', 'tp'), pairs)]
    unnamed x10 -> x16, local copies, waits for them, and re-layouts: 3.45 us -> 3.48 us
  transfers between devices with their start and end apart: 20 -> 20, of which waited for: 10 -> 10; matrix products, arithmetic and copies ran while one was open for 0% -> 0% of each run, Pallas kernels for 14% -> 11%
where the time goes in v5:
time: 45.3 us; the launch traced here: 45.1 us
  starting transfers between devices  13.8 us (30%)
  waiting for transfers between devices  13.4 us (30%)
  Pallas kernels  13 us (29%)
  local copies, waits for them, and re-layouts  3.48 us (8%)
  between operations  1.48 us (3%)
    ppermute x18, starting transfers between devices, swap(): return lax.ppermute(value, axis, [(i, i ^ mask) for i in range(size)])  10.7 us
    ppermute x18, waiting for transfers between devices, swap(): return lax.ppermute(value, axis, [(i, i ^ mask) for i in range(size)])  9.69 us
    ppermute x2, waiting for transfers between devices, send_block(): return lax.ppermute(value, ('group', 'tp'), pairs)  3.71 us
    unnamed x16, local copies, waits for them, and re-layouts  3.48 us
    ppermute x2, starting transfers between devices, send_block(): return lax.ppermute(value, ('group', 'tp'), pairs)  3.07 us
    pallas_call x1, Pallas kernels, step(): call(lambda *refs, taken=taken: local_kernel(*refs, kv_heads=kv_heads, pi...  3.04 us
    pallas_call x1, Pallas kernels, step(): call(lambda *refs, taken=taken: slot_kernel(*refs, groups=groups, kv_head...  2.76 us
    pallas_call x1, Pallas kernels, step(): call(lambda *refs: combine_kernel(*refs, groups=groups, slots=slots, **se...  2.74 us
  transfers between devices with their start and end apart: 20, of which 10 were waited for; matrix products, arithmetic and copies ran while one was open for 0% of the time, Pallas kernels for 11%

profile of v5, /device:TPU:0, one launch (start us, length us, event | category | flops | bytes accessed | tf_op | source)
XLA Modules:
  0.0 45.1 jit_solution(15196429042231688517)
XLA Ops:
  0.7 0.8 %copy-done.4 = bf16[16,2048]{1,0:T(8,128)(2,1)S(1)} copy-done((bf16[16,2048]{1,0:T(8,128)(2,1)S(1)}, bf16[16,2048]{1,0:T(8,128)(2,1)}, u32[]{:S(2)}) %copy-start.4) | copy-done | bytes 65560
  1.5 1.4 %copy-done = bf16[16,512,256]{2,1,0:T(8,128)(2,1)S(1)} copy-done((bf16[16,512,256]{2,1,0:T(8,128)(2,1)S(1)}, bf16[16,512,256]{2,1,0:T(8,128)(2,1)}, u32[]{:S(2)}) %copy-start) | copy-done | bytes 4194328
  2.9 1.3 %copy-done.1 = bf16[16,512,256]{2,1,0:T(8,128)(2,1)S(1)} copy-done((bf16[16,512,256]{2,1,0:T(8,128)(2,1)S(1)}, bf16[16,512,256]{2,1,0:T(8,128)(2,1)}, u32[]{:S(2)}) %copy-start.1) | copy-done | bytes 4194328
  4.2 3.0 %shard_map.114 = (f32[512,128]{1,0:T(8,128)S(1)}, bf16[1024,2048]{1,0:T(8,128)(2,1)S(1)}) custom-call(s32[16]{0:T(128)S(1)} %copy-done.5, bf16[16,2048]{1,0:T(8,128)(2,1)S(1)} %copy-done.4, bf16[16,512,256]{2,1,0:T(8,128)(2,1)S(1)} %copy-done, bf16[16,512,256]{2,1,0:T(8,128)(2,1)S(1)} %copy-done.1, bf16[2048,8192]{1,0:T(8,128)(2,1)} %refs_3_.5, ...), custom_call_target="tpu_custom_call" | custom-call | bytes 8388608 | tf_op jit(solution)/shard_map/pallas_call | solution.py:359
  7.8 2.6 %collective-permute-start.2 = (bf16[16,2048]{1,0:T(8,128)(2,1)S(1)}, bf16[16,2048]{1,0:T(8,128)(2,1)S(1)}, u32[]{:S(2)}, u32[]{:S(2)}) collective-permute-start(bf16[16,2048]{1,0:T(8,128)(2,1)S(1)} %copy-done.4), channel_id=1, source_target_pairs={{0,8},{4,12},{8,0},{12,4},{16,24},{20,28},{24,16},{28,20},{1,9},{5... | collective-permute-start | bytes 196616 | tf_op jit(solution)/shard_map/ppermute | solution.py:304
  10.3 1.5 %collective-permute-start.4 = (bf16[16,2048]{1,0:T(8,128)(2,1)S(1)}, bf16[16,2048]{1,0:T(8,128)(2,1)S(1)}, u32[]{:S(2)}, u32[]{:S(2)}) collective-permute-start(bf16[16,2048]{1,0:T(8,128)(2,1)S(1)} %copy-done.4), channel_id=1, source_target_pairs={{0,16},{4,20},{8,24},{12,28},{16,0},{20,4},{24,8},{28,12},{1,17},{... | collective-permute-start | bytes 196616 | tf_op jit(solution)/shard_map/ppermute | solution.py:304
  11.9 1.1 %collective-permute-done.2.refs_5_ = bf16[16,2048]{1,0:T(8,128)(2,1)S(1)} collective-permute-done((bf16[16,2048]{1,0:T(8,128)(2,1)S(1)}, bf16[16,2048]{1,0:T(8,128)(2,1)S(1)}, u32[]{:S(2)}, u32[]{:S(2)}) %collective-permute-start.2) | collective-permute-done | bytes 65568 | tf_op jit(solution)/shard_map/ppermute | solution.py:304
  13.0 1.6 %collective-permute-done.4.refs_7_ = bf16[16,2048]{1,0:T(8,128)(2,1)S(1)} collective-permute-done((bf16[16,2048]{1,0:T(8,128)(2,1)S(1)}, bf16[16,2048]{1,0:T(8,128)(2,1)S(1)}, u32[]{:S(2)}, u32[]{:S(2)}) %collective-permute-start.4) | collective-permute-done | bytes 65568 | tf_op jit(solution)/shard_map/ppermute | solution.py:304
  14.6 2.4 %collective-permute-done.6.refs_9_ = bf16[16,2048]{1,0:T(8,128)(2,1)S(1)} collective-permute-done((bf16[16,2048]{1,0:T(8,128)(2,1)S(1)}, bf16[16,2048]{1,0:T(8,128)(2,1)S(1)}, u32[]{:S(2)}, u32[]{:S(2)}) %collective-permute-start.6) | collective-permute-done | bytes 65568 | tf_op jit(solution)/shard_map/ppermute | solution.py:304
  18.3 2.8 %shard_map.115 = (f32[48,128]{1,0:T(8,128)S(1)}, bf16[1024,2048]{1,0:T(8,128)(2,1)S(1)}) custom-call(s32[2]{0:T(128)S(1)} %copy-done.6, s32[2]{0:T(128)S(1)} %copy-done.7, s32[1]{0:T(128)S(6)} %copy.12.refs_2_, bf16[16,2048]{1,0:T(8,128)(2,1)S(1)} %copy-done.4, bf16[16,2048]{1,0:T(8,128)(2,1)S(1)} %collective-permute-done.1.refs_4_, ...), custom_call_target="tpu_custom_call" | custom-call | bytes 8388608 | tf_op jit(solution)/shard_map/pallas_call | solution.py:381
  21.0 0.6 %collective-permute-start.9 = (f32[48,128]{1,0:T(8,128)S(1)}, f32[48,128]{1,0:T(8,128)S(1)}, u32[]{:S(2)}, u32[]{:S(2)}) collective-permute-start(f32[48,128]{1,0:T(8,128)S(1)} %get-tuple-element.15.refs_2_.refs_1_), channel_id=1, source_target_pairs={{0,8},{4,12},{8,0},{12,4},{16,24},{20,28},{24,16},{28,20},{1,9},{5... | collective-permute-start | bytes 73736 | tf_op jit(solution)/shard_map/ppermute | solution.py:304
  21.6 0.7 %collective-permute-start.11 = (f32[48,128]{1,0:T(8,128)S(1)}, f32[48,128]{1,0:T(8,128)S(1)}, u32[]{:S(2)}, u32[]{:S(2)}) collective-permute-start(f32[48,128]{1,0:T(8,128)S(1)} %get-tuple-element.15.refs_2_.refs_1_), channel_id=1, source_target_pairs={{0,16},{4,20},{8,24},{12,28},{16,0},{20,4},{24,8},{28,12},{1,17},{... | collective-permute-start | bytes 73736 | tf_op jit(solution)/shard_map/ppermute | solution.py:304
  22.3 2.3 %collective-permute-start.13 = (f32[48,128]{1,0:T(8,128)S(1)}, f32[48,128]{1,0:T(8,128)S(1)}, u32[]{:S(2)}, u32[]{:S(2)}) collective-permute-start(f32[48,128]{1,0:T(8,128)S(1)} %get-tuple-element.15.refs_2_.refs_1_), channel_id=1, source_target_pairs={{0,24},{4,28},{8,16},{12,20},{16,8},{20,12},{24,0},{28,4},{1,25},{... | collective-permute-start | bytes 73736 | tf_op jit(solution)/shard_map/ppermute | solution.py:304
  25.5 1.6 %collective-permute-done.13.refs_8_ = f32[48,128]{1,0:T(8,128)S(1)} collective-permute-done((f32[48,128]{1,0:T(8,128)S(1)}, f32[48,128]{1,0:T(8,128)S(1)}, u32[]{:S(2)}, u32[]{:S(2)}) %collective-permute-start.13) | collective-permute-done | bytes 24608 | tf_op jit(solution)/shard_map/ppermute | solution.py:304
  27.0 2.2 %shard_map.117.refs_1_ = bf16[1024,2048]{1,0:T(8,128)(2,1)S(1)} custom-call(bf16[2048,8192]{1,0:T(8,128)(2,1)} %refs_3_.5, f32[48,128]{1,0:T(8,128)S(1)} %get-tuple-element.15.refs_2_.refs_1_), custom_call_target="tpu_custom_call" | custom-call | bytes 4194304 | tf_op jit(solution)/shard_map/pallas_call | solution.py:406
  29.3 2.7 %shard_map.116 = (bf16[32,2048]{1,0:T(8,128)(2,1)S(1)}, s32[1]{0:T(128)}, bf16[16,2048]{1,0:T(8,128)(2,1)S(1)}, bf16[16,2048]{1,0:T(8,128)(2,1)S(1)}, bf16[1024,2048]{1,0:T(8,128)(2,1)S(1)}) custom-call(f32[512,128]{1,0:T(8,128)S(1)} %get-tuple-element.14.refs_0_, f32[512,128]{1,0:T(8,128)S(1)} %collective-permute-done.refs_1_, ...), custom_call_target="tpu_custom_call" | custom-call | bytes 8388608 | tf_op jit(solution)/shard_map/pallas_call | solution.py:427
  32.0 1.6 %shard_map.118 = (bf16[16,2048]{1,0:T(8,128)(2,1)S(1)}, bf16[16,2048]{1,0:T(8,128)(2,1)S(1)}, f32[16,2048]{1,0:T(8,128)S(1)}) custom-call(bf16[32,2048]{1,0:T(8,128)(2,1)S(1)} %get-tuple-element.18.refs_0_, bf16[1024,2048]{1,0:T(8,128)(2,1)S(1)} %shard_map.117.refs_1_, bf16[1024,2048]{1,0:T(8,128)(2,1)S(1)} %get-tuple-element.19.refs_2_, ...), custom_call_target="tpu_custom_call" | custom-call | bytes 8388608 | tf_op jit(solution)/shard_map/pallas_call | solution.py:443
  34.3 2.4 %collective-permute-start.16 = (bf16[16,2048]{1,0:T(8,128)(2,1)S(1)}, bf16[16,2048]{1,0:T(8,128)(2,1)S(1)}, u32[]{:S(2)}, u32[]{:S(2)}) collective-permute-start(bf16[16,2048]{1,0:T(8,128)(2,1)S(1)} %get-tuple-element.22), channel_id=1, source_target_pairs={{0,2},{1,3},{2,0},{3,1},{4,7},{5,6},{6,5},{7,4},{8,10},{9,11},{10,... | collective-permute-start | bytes 196616 | tf_op jit(solution)/shard_map/ppermute | solution.py:299
  36.7 1.6 %collective-permute-start.19 = (bf16[16,2048]{1,0:T(8,128)(2,1)S(1)}, bf16[16,2048]{1,0:T(8,128)(2,1)S(1)}, u32[]{:S(2)}, u32[]{:S(2)}) collective-permute-start(bf16[16,2048]{1,0:T(8,128)(2,1)S(1)} %shard_map.119), channel_id=1, source_target_pairs={{0,1},{1,0},{2,3},{3,2},{4,5},{5,4},{6,7},{7,6},{8,9},{9,8},{10,11... | collective-permute-start | bytes 196616 | tf_op jit(solution)/shard_map/ppermute | solution.py:304
  38.4 0.6 %collective-permute-start.18 = (bf16[16,2048]{1,0:T(8,128)(2,1)S(1)}, bf16[16,2048]{1,0:T(8,128)(2,1)S(1)}, u32[]{:S(2)}, u32[]{:S(2)}) collective-permute-start(bf16[16,2048]{1,0:T(8,128)(2,1)S(1)} %collective-permute-done.17), channel_id=1, source_target_pairs={{0,3},{1,2},{2,1},{3,0},{4,6},{5,7},{6,4},{7,5},{8,11},{9,10},{10,... | collective-permute-start | bytes 196616 | tf_op jit(solution)/shard_map/ppermute | solution.py:299
  39.0 1.9 %collective-permute-done.16.refs_0_ = bf16[16,2048]{1,0:T(8,128)(2,1)S(1)} collective-permute-done((bf16[16,2048]{1,0:T(8,128)(2,1)S(1)}, bf16[16,2048]{1,0:T(8,128)(2,1)S(1)}, u32[]{:S(2)}, u32[]{:S(2)}) %collective-permute-start.16) | collective-permute-done | bytes 65568 | tf_op jit(solution)/shard_map/ppermute | solution.py:299
  40.9 1.7 %collective-permute-done.19.refs_2_ = bf16[16,2048]{1,0:T(8,128)(2,1)S(1)} collective-permute-done((bf16[16,2048]{1,0:T(8,128)(2,1)S(1)}, bf16[16,2048]{1,0:T(8,128)(2,1)S(1)}, u32[]{:S(2)}, u32[]{:S(2)}) %collective-permute-start.19) | collective-permute-done | bytes 65568 | tf_op jit(solution)/shard_map/ppermute | solution.py:304
  42.6 1.8 %collective-permute-done.18.refs_1_ = bf16[16,2048]{1,0:T(8,128)(2,1)S(1)} collective-permute-done((bf16[16,2048]{1,0:T(8,128)(2,1)S(1)}, bf16[16,2048]{1,0:T(8,128)(2,1)S(1)}, u32[]{:S(2)}, u32[]{:S(2)}) %collective-permute-start.18) | collective-permute-done | bytes 65568 | tf_op jit(solution)/shard_map/ppermute | solution.py:299
  44.4 0.7 %shard_map.120 = bf16[16,2048]{1,0:T(8,128)(2,1)} custom-call(f32[16,2048]{1,0:T(8,128)S(1)} %get-tuple-element.20.own, bf16[16,2048]{1,0:T(8,128)(2,1)S(1)} %collective-permute-done.15.even.crossed, bf16[16,2048]{1,0:T(8,128)(2,1)S(1)} %collective-permute-done.16.refs_0_, bf16[16,2048]{1,0:T(8,128)(2,1)S(1)} %collective-permute-done.18.refs_1_, ...), custom_call_target="tpu_custom_call" | custom-call | tf_op jit(solution)/shard_map/pallas_call | solution.py:461
  (40 shorter events, 2.7 us)
Async XLA Ops:
  4.1 14.1 %copy-start.2 = (bf16[2,4096,256]{2,1,0:T(8,128)(2,1)S(1)}, bf16[2,4096,256]{2,1,0:T(8,128)(2,1)}, u32[]{:S(2)}) copy-start(bf16[2,4096,256]{2,1,0:T(8,128)(2,1)} %refs_11_.1) | copy-start | bytes 12582916
  4.1 14.1 %copy-start.3 = (bf16[2,4096,256]{2,1,0:T(8,128)(2,1)S(1)}, bf16[2,4096,256]{2,1,0:T(8,128)(2,1)}, u32[]{:S(2)}) copy-start(bf16[2,4096,256]{2,1,0:T(8,128)(2,1)} %refs_12_.2) | copy-start | bytes 12582916
  4.1 14.1 %copy-start.6 = (s32[2]{0:T(128)S(1)}, s32[2]{0:T(128)}, u32[]{:S(2)}) copy-start(s32[2]{0:T(128)} %refs_0_.4) | copy-start | bytes 28
  4.1 14.1 %copy-start.7 = (s32[2]{0:T(128)S(1)}, s32[2]{0:T(128)}, u32[]{:S(2)}) copy-start(s32[2]{0:T(128)} %refs_1_.3) | copy-start | bytes 28
  7.2 22.1 %collective-permute-start = (f32[512,128]{1,0:T(8,128)S(1)}, f32[512,128]{1,0:T(8,128)S(1)}, u32[]{:S(2)}, u32[]{:S(2)}) collective-permute-start(f32[512,128]{1,0:T(8,128)S(1)} %get-tuple-element.14.refs_0_), channel_id=1, source_target_pairs={{0,4},{4,0},{8,12},{12,8},{16,20},{20,16},{24,28},{28,24},{1,5},{5... | collective-permute-start | bytes 786440 | tf_op jit(solution)/shard_map/ppermute | solution.py:304
  7.8 5.2 %collective-permute-start.2 = (bf16[16,2048]{1,0:T(8,128)(2,1)S(1)}, bf16[16,2048]{1,0:T(8,128)(2,1)S(1)}, u32[]{:S(2)}, u32[]{:S(2)}) collective-permute-start(bf16[16,2048]{1,0:T(8,128)(2,1)S(1)} %copy-done.4), channel_id=1, source_target_pairs={{0,8},{4,12},{8,0},{12,4},{16,24},{20,28},{24,16},{28,20},{1,9},{5... | collective-permute-start | bytes 196616 | tf_op jit(solution)/shard_map/ppermute | solution.py:304
  10.3 4.3 %collective-permute-start.4 = (bf16[16,2048]{1,0:T(8,128)(2,1)S(1)}, bf16[16,2048]{1,0:T(8,128)(2,1)S(1)}, u32[]{:S(2)}, u32[]{:S(2)}) collective-permute-start(bf16[16,2048]{1,0:T(8,128)(2,1)S(1)} %copy-done.4), channel_id=1, source_target_pairs={{0,16},{4,20},{8,24},{12,28},{16,0},{20,4},{24,8},{28,12},{1,17},{... | collective-permute-start | bytes 196616 | tf_op jit(solution)/shard_map/ppermute | solution.py:304
  11.8 5.2 %collective-permute-start.6 = (bf16[16,2048]{1,0:T(8,128)(2,1)S(1)}, bf16[16,2048]{1,0:T(8,128)(2,1)S(1)}, u32[]{:S(2)}, u32[]{:S(2)}) collective-permute-start(bf16[16,2048]{1,0:T(8,128)(2,1)S(1)} %copy-done.4), channel_id=1, source_target_pairs={{0,24},{4,28},{8,16},{12,20},{16,8},{20,12},{24,0},{28,4},{1,25},{... | collective-permute-start | bytes 196616 | tf_op jit(solution)/shard_map/ppermute | solution.py:304
  11.9 5.8 %collective-permute-start.1 = (bf16[16,2048]{1,0:T(8,128)(2,1)S(1)}, bf16[16,2048]{1,0:T(8,128)(2,1)S(1)}, u32[]{:S(2)}, u32[]{:S(2)}) collective-permute-start(bf16[16,2048]{1,0:T(8,128)(2,1)S(1)} %copy-done.4), channel_id=1, source_target_pairs={{0,4},{4,0},{8,12},{12,8},{16,20},{20,16},{24,28},{28,24},{1,5},{5... | collective-permute-start | bytes 196616 | tf_op jit(solution)/shard_map/ppermute | solution.py:304
  13.0 4.7 %collective-permute-start.3 = (bf16[16,2048]{1,0:T(8,128)(2,1)S(1)}, bf16[16,2048]{1,0:T(8,128)(2,1)S(1)}, u32[]{:S(2)}, u32[]{:S(2)}) collective-permute-start(bf16[16,2048]{1,0:T(8,128)(2,1)S(1)} %collective-permute-done.2.refs_5_), channel_id=1, source_target_pairs={{0,4},{4,0},{8,12},{12,8},{16,20},{20,16},{24,28},{28,24},{1,5},{5... | collective-permute-start | bytes 196616 | tf_op jit(solution)/shard_map/ppermute | solution.py:304
  14.6 3.1 %collective-permute-start.5 = (bf16[16,2048]{1,0:T(8,128)(2,1)S(1)}, bf16[16,2048]{1,0:T(8,128)(2,1)S(1)}, u32[]{:S(2)}, u32[]{:S(2)}) collective-permute-start(bf16[16,2048]{1,0:T(8,128)(2,1)S(1)} %collective-permute-done.4.refs_7_), channel_id=1, source_target_pairs={{0,4},{4,0},{8,12},{12,8},{16,20},{20,16},{24,28},{28,24},{1,5},{5... | collective-permute-start | bytes 196616 | tf_op jit(solution)/shard_map/ppermute | solution.py:304
  17.0 1.3 %collective-permute-start.7 = (bf16[16,2048]{1,0:T(8,128)(2,1)S(1)}, bf16[16,2048]{1,0:T(8,128)(2,1)S(1)}, u32[]{:S(2)}, u32[]{:S(2)}) collective-permute-start(bf16[16,2048]{1,0:T(8,128)(2,1)S(1)} %collective-permute-done.6.refs_9_), channel_id=1, source_target_pairs={{0,4},{4,0},{8,12},{12,8},{16,20},{20,16},{24,28},{28,24},{1,5},{5... | collective-permute-start | bytes 196616 | tf_op jit(solution)/shard_map/ppermute | solution.py:304
  21.0 3.9 %collective-permute-start.9 = (f32[48,128]{1,0:T(8,128)S(1)}, f32[48,128]{1,0:T(8,128)S(1)}, u32[]{:S(2)}, u32[]{:S(2)}) collective-permute-start(f32[48,128]{1,0:T(8,128)S(1)} %get-tuple-element.15.refs_2_.refs_1_), channel_id=1, source_target_pairs={{0,8},{4,12},{8,0},{12,4},{16,24},{20,28},{24,16},{28,20},{1,9},{5... | collective-permute-start | bytes 73736 | tf_op jit(solution)/shard_map/ppermute | solution.py:304
  21.6 3.8 %collective-permute-start.11 = (f32[48,128]{1,0:T(8,128)S(1)}, f32[48,128]{1,0:T(8,128)S(1)}, u32[]{:S(2)}, u32[]{:S(2)}) collective-permute-start(f32[48,128]{1,0:T(8,128)S(1)} %get-tuple-element.15.refs_2_.refs_1_), channel_id=1, source_target_pairs={{0,16},{4,20},{8,24},{12,28},{16,0},{20,4},{24,8},{28,12},{1,17},{... | collective-permute-start | bytes 73736 | tf_op jit(solution)/shard_map/ppermute | solution.py:304
  22.3 4.7 %collective-permute-start.13 = (f32[48,128]{1,0:T(8,128)S(1)}, f32[48,128]{1,0:T(8,128)S(1)}, u32[]{:S(2)}, u32[]{:S(2)}) collective-permute-start(f32[48,128]{1,0:T(8,128)S(1)} %get-tuple-element.15.refs_2_.refs_1_), channel_id=1, source_target_pairs={{0,24},{4,28},{8,16},{12,20},{16,8},{20,12},{24,0},{28,4},{1,25},{... | collective-permute-start | bytes 73736 | tf_op jit(solution)/shard_map/ppermute | solution.py:304
  24.6 4.6 %collective-permute-start.8 = (f32[48,128]{1,0:T(8,128)S(1)}, f32[48,128]{1,0:T(8,128)S(1)}, u32[]{:S(2)}, u32[]{:S(2)}) collective-permute-start(f32[48,128]{1,0:T(8,128)S(1)} %get-tuple-element.15.refs_2_.refs_1_), channel_id=1, source_target_pairs={{0,4},{4,0},{8,12},{12,8},{16,20},{20,16},{24,28},{28,24},{1,5},{5... | collective-permute-start | bytes 73736 | tf_op jit(solution)/shard_map/ppermute | solution.py:304
  24.9 4.3 %collective-permute-start.10 = (f32[48,128]{1,0:T(8,128)S(1)}, f32[48,128]{1,0:T(8,128)S(1)}, u32[]{:S(2)}, u32[]{:S(2)}) collective-permute-start(f32[48,128]{1,0:T(8,128)S(1)} %collective-permute-done.9.refs_4_), channel_id=1, source_target_pairs={{0,4},{4,0},{8,12},{12,8},{16,20},{20,16},{24,28},{28,24},{1,5},{5... | collective-permute-start | bytes 73736 | tf_op jit(solution)/shard_map/ppermute | solution.py:304
  25.5 3.8 %collective-permute-start.12 = (f32[48,128]{1,0:T(8,128)S(1)}, f32[48,128]{1,0:T(8,128)S(1)}, u32[]{:S(2)}, u32[]{:S(2)}) collective-permute-start(f32[48,128]{1,0:T(8,128)S(1)} %collective-permute-done.11.refs_6_), channel_id=1, source_target_pairs={{0,4},{4,0},{8,12},{12,8},{16,20},{20,16},{24,28},{28,24},{1,5},{5... | collective-permute-start | bytes 73736 | tf_op jit(solution)/shard_map/ppermute | solution.py:304
  27.0 2.2 %collective-permute-start.14 = (f32[48,128]{1,0:T(8,128)S(1)}, f32[48,128]{1,0:T(8,128)S(1)}, u32[]{:S(2)}, u32[]{:S(2)}) collective-permute-start(f32[48,128]{1,0:T(8,128)S(1)} %collective-permute-done.13.refs_8_), channel_id=1, source_target_pairs={{0,4},{4,0},{8,12},{12,8},{16,20},{20,16},{24,28},{28,24},{1,5},{5... | collective-permute-start | bytes 73736 | tf_op jit(solution)/shard_map/ppermute | solution.py:304
  33.6 3.1 %collective-permute-start.15 = (bf16[16,2048]{1,0:T(8,128)(2,1)S(1)}, bf16[16,2048]{1,0:T(8,128)(2,1)S(1)}, u32[]{:S(2)}, u32[]{:S(2)}) collective-permute-start(bf16[16,2048]{1,0:T(8,128)(2,1)S(1)} %get-tuple-element.21), channel_id=1, source_target_pairs={{0,4},{4,0},{8,12},{12,8},{16,20},{20,16},{24,28},{28,24},{1,5},{5... | collective-permute-start | bytes 196616 | tf_op jit(solution)/shard_map/ppermute | solution.py:304
  34.2 4.2 %collective-permute-start.17 = (bf16[16,2048]{1,0:T(8,128)(2,1)S(1)}, bf16[16,2048]{1,0:T(8,128)(2,1)S(1)}, u32[]{:S(2)}, u32[]{:S(2)}) collective-permute-start(bf16[16,2048]{1,0:T(8,128)(2,1)S(1)} %get-tuple-element.23), channel_id=1, source_target_pairs={{0,4},{4,0},{8,12},{12,8},{16,20},{20,16},{24,28},{28,24},{1,5},{5... | collective-permute-start | bytes 196616 | tf_op jit(solution)/shard_map/ppermute | solution.py:304
  34.3 6.7 %collective-permute-start.16 = (bf16[16,2048]{1,0:T(8,128)(2,1)S(1)}, bf16[16,2048]{1,0:T(8,128)(2,1)S(1)}, u32[]{:S(2)}, u32[]{:S(2)}) collective-permute-start(bf16[16,2048]{1,0:T(8,128)(2,1)S(1)} %get-tuple-element.22), channel_id=1, source_target_pairs={{0,2},{1,3},{2,0},{3,1},{4,7},{5,6},{6,5},{7,4},{8,10},{9,11},{10,... | collective-permute-start | bytes 196616 | tf_op jit(solution)/shard_map/ppermute | solution.py:299
  36.7 5.9 %collective-permute-start.19 = (bf16[16,2048]{1,0:T(8,128)(2,1)S(1)}, bf16[16,2048]{1,0:T(8,128)(2,1)S(1)}, u32[]{:S(2)}, u32[]{:S(2)}) collective-permute-start(bf16[16,2048]{1,0:T(8,128)(2,1)S(1)} %shard_map.119), channel_id=1, source_target_pairs={{0,1},{1,0},{2,3},{3,2},{4,5},{5,4},{6,7},{7,6},{8,9},{9,8},{10,11... | collective-permute-start | bytes 196616 | tf_op jit(solution)/shard_map/ppermute | solution.py:304
  38.4 6.1 %collective-permute-start.18 = (bf16[16,2048]{1,0:T(8,128)(2,1)S(1)}, bf16[16,2048]{1,0:T(8,128)(2,1)S(1)}, u32[]{:S(2)}, u32[]{:S(2)}) collective-permute-start(bf16[16,2048]{1,0:T(8,128)(2,1)S(1)} %collective-permute-done.17), channel_id=1, source_target_pairs={{0,3},{1,2},{2,1},{3,0},{4,6},{5,7},{6,4},{7,5},{8,11},{9,10},{10,... | collective-permute-start | bytes 196616 | tf_op jit(solution)/shard_map/ppermute | solution.py:299
  (4 other events, 10.0 us)
